TPU v7x, 32 devices: a whole 2x2x4 slice. The times are simulated.
32 devices in a mesh: ctx: 8 (over z, x), fsdp: 4 (over y, core).
Axes of the slice: x: 2, y: 2, z: 4, core: 2. Of those that a mesh axis runs over, the one named last changes fastest.
Arguments:
- query_in: bfloat16 [4096, 4096], P('ctx', 'fsdp'), may hold values from -6 to 6
- key_in: bfloat16 [4096, 4096], P('ctx', 'fsdp'), may hold values from -6 to 6
- value_in: bfloat16 [4096, 4096], P('ctx', 'fsdp'), may hold values from -6 to 6
- residues: float32 [16, 256], P(None, 'fsdp'), may hold values from -1.5 to 1.5
- decay_rate: float32 [16, 256], P(None, 'fsdp'), may hold values from 6.1035156e-05 to 0.1
- short_filter: float32 [3, 3, 4096], P(None, None, 'fsdp'), may hold values from -3 to 3
- skip_gain: float32 [1, 4096], P(None, 'fsdp'), may hold values from -3 to 3
Outputs:
- mixed_out: bfloat16 [4096, 4096], P('ctx', 'fsdp')
All inputs are finite; a program needn't handle non-finite values.
Results may differ from a plain program's by a relative error of at most 0.001.
Values may be sent and summed in bfloat16 or wider, within the bound.
No kernel may reach another device: no remote copies, remote signals or barrier semaphores. Data moves between devices by JAX's collectives and lax.ppermute only.
A program may use at most 320 MiB of HBM per device.

v0:
```python
import jax
import jax.numpy as jnp
from jax import lax
from jax.sharding import PartitionSpec as P

SPAN = 512


def shifted(block, axis, distance):
    devices = range(lax.axis_size(axis))
    route = [(i - distance, i) for i in devices if i - distance in devices]
    return lax.ppermute(block, axis, route)


def filter_taps(residues, decay_rate, count):
    norm = jnp.sqrt(-jnp.expm1(-2.0 * decay_rate))
    weight = residues * norm
    steps = jnp.arange(count).astype(jnp.float32)
    return jnp.sum(weight[:, :, None] * jnp.exp(-decay_rate[:, :, None] * steps), axis=0)


def toeplitz(taps):
    count = taps.shape[1]
    lag = jnp.arange(count)[:, None] - jnp.arange(count)[None, :]
    picked = jnp.take(taps, jnp.clip(lag, 0, count - 1), axis=1)
    return jnp.where(lag >= 0, picked, jnp.zeros_like(picked))


def short_conv(padded, weights, count):
    width = weights.shape[0]
    total = jnp.zeros((count, weights.shape[1]), jnp.float32)
    for shift_at in range(width):
        begin = width - 1 - shift_at
        total = total + weights[shift_at][None, :] * padded[begin : begin + count]
    return total


def body(query_in, key_in, value_in, residues, decay_rate, short_filter, skip_gain):
    local_len, width = query_in.shape
    modes, groups = residues.shape
    group_size = width // groups
    taps_len = short_filter.shape[1]
    block = SPAN
    count = local_len // block
    high = lax.Precision.HIGHEST
    edge = local_len - (taps_len - 1)
    rim = (query_in[edge:], key_in[edge:], value_in[edge:])
    prev_q, prev_k, prev_v = shifted((rim[0], rim[1], rim[2]), "ctx", 1)
    q_short = short_conv(
        jnp.concatenate([prev_q, query_in], 0).astype(jnp.float32), short_filter[0], local_len
    )
    k_short = short_conv(
        jnp.concatenate([prev_k, key_in], 0).astype(jnp.float32), short_filter[1], local_len
    )
    v_short = short_conv(
        jnp.concatenate([prev_v, value_in], 0).astype(jnp.float32), short_filter[2], local_len
    )
    gated = k_short * v_short
    blocks = gated.reshape(count, block, groups, group_size)
    toe = toeplitz(filter_taps(residues, decay_rate, block))
    local = jnp.einsum("gts,ksgj->ktgj", toe, blocks, precision=high)
    norm = jnp.sqrt(-jnp.expm1(-2.0 * decay_rate))
    weight = residues * norm
    steps = jnp.arange(block).astype(jnp.float32)
    lead = weight[:, :, None] * jnp.exp(-decay_rate[:, :, None] * (steps + 1.0))
    tail = jnp.exp(-decay_rate[:, :, None] * (block - 1.0 - steps))
    block_fresh = jnp.einsum("ngs,ksgj->kngj", tail, blocks, precision=high)
    block_power = jnp.exp(-decay_rate * block)

    def carry_step(state, item):
        return (state * block_power[:, :, None] + item, state)

    own_final, own_prefix = lax.scan(
        carry_step, jnp.zeros((modes, groups, group_size), jnp.float32), block_fresh
    )
    fresh = own_final.reshape(modes, width)
    me_index = lax.axis_index("ctx")
    piece = lax.all_gather(fresh, "ctx", axis=0, tiled=True)
    owners_count = piece.shape[0] // modes
    pieces = piece.reshape(owners_count, modes, width)
    owner = jnp.arange(owners_count)
    gap = me_index - 1 - owner
    gap_f = jnp.maximum(gap, 0).astype(jnp.float32)
    factor = jnp.exp(-decay_rate[None] * (local_len * gap_f[:, None, None]))
    factor = jnp.where(gap[:, None, None] >= 0, factor, jnp.zeros_like(factor))
    spread = jnp.repeat(factor, group_size, axis=2)
    state_in = jnp.sum(spread * pieces, axis=0)
    block_steps = jnp.arange(count).astype(jnp.float32)
    reach = jnp.exp(-decay_rate[None] * (block * block_steps[:, None, None]))
    entering = own_prefix + state_in.reshape(modes, groups, group_size)[None] * reach[..., None]
    term = jnp.einsum("ngt,kngj->ktgj", lead, entering, precision=high)
    long_conv = (local + term).reshape(local_len, width)
    return (q_short * (long_conv + skip_gain[0][None, :] * gated)).astype(jnp.bfloat16)


def solution(mesh):
    placed = (
        P("ctx", "fsdp"),
        P("ctx", "fsdp"),
        P("ctx", "fsdp"),
        P(None, "fsdp"),
        P(None, "fsdp"),
        P(None, None, "fsdp"),
        P(None, "fsdp"),
    )
    return jax.shard_map(
        body, mesh=mesh, in_specs=placed, out_specs=P("ctx", "fsdp"), check_vma=False
    )
```

profile of v0, /device:TPU:0, one launch (start us, length us, event | category | flops | bytes accessed | tf_op | source)
XLA Modules:
  0.0 1112.9 jit_solution(13351788246723797117)
XLA Ops:
  1.6 5.6 collective-permute-start.1
  8.8 3.5 collective-permute-start.2
  13.0 0.9 copy.41
  13.9 3.4 collective-permute-start
  18.1 1.0 fusion.33
  21.7 1.3 multiply_reduce_fusion.1
  23.6 1.3 copy.44
  24.9 1.3 copy.46
  26.3 1.3 copy.42
  27.8 0.9 mul.268
  28.8 860.0 %gather_fusion = f32[262144,64]{1,0:T(8,128)} fusion(f32[64,512]{0,1:T(8,128)S(1)} %copy.49, s32[262144]{0:T(1024)S(1)} %broadcast_clamp_fusion), kind=kCustom, calls=%fused_computation | custom fusion | bytes 135266304 | tf_op jit(solution)/shard_map/jit(_take)/gather | solution.py:25
  888.8 101.6 %copy.50 = f32[512,512,64]{1,0,2:T(8,128)} copy(f32[512,512,64]{2,1,0:T(8,128)} %bitcast.10) | data formatting | bytes 134217728 | tf_op jit(solution)/shard_map/jit(_take)/gather | solution.py:25
  990.4 1.6 maximum_convert_fusion.1
  992.1 1.5 maximum_convert_fusion.2
  993.7 3.7 fusion.9
  997.4 2.6 fusion.21
  1000.2 31.4 %all_gather.3 = f32[128,1024]{1,0:T(8,128)S(1)} all-gather(f32[16,1024]{1,0:T(8,128)S(1)} %add.80), channel_id=1, replica_groups=mesh['ctx'=8,'fsdp'=4] {'ctx'}, dimensions={0}, use_global_device_ids=true | all-gather | bytes 589824 | tf_op jit(solution)/shard_map/all_gather | solution.py:78
  1031.6 2.8 reshape.128
  1034.4 3.0 multiply_reduce_fusion
  1037.6 65.9 %fusion = f32[64,16,512]{2,1,0:T(8,128)} fusion(f32[512,64,16]{0,2,1:T(8,128)S(1)} %bitcast.35, f32[512,512,64]{1,0,2:T(8,128)} %copy.50, pred[512,512]{1,0:T(8,128)(4,1)S(1)} %copy-done.3, pred[512,512]{1,0:T(8,128)(4,1)S(1)} %copy-done.4), kind=kOutput, calls=%fused_computation.1 | convolution fusion | flops 3254779904 | bytes 71827456 | tf_op jit(solution)/shard_map/gts,ksgj->ktgj/dot_general | solution.py:61
  1103.6 4.2 fusion.24
  1107.8 1.5 maximum_convert_fusion
  1109.4 2.2 fusion.15
  1111.6 1.3 copy.53
  (88 shorter events, 8.6 us)
Async XLA Ops:
  0.0 19.1 %copy-start.16 = (f32[3,3,1024]{2,1,0:T(4,128)S(1)}, f32[3,3,1024]{2,1,0:T(4,128)}, u32[]{:S(2)}) copy-start(f32[3,3,1024]{2,1,0:T(4,128)} %param.12) | copy-start | bytes 110596
  0.0 19.8 %copy-start.29 = (f32[16,64]{1,0:T(8,128)S(1)}, f32[16,64]{1,0:T(8,128)}, u32[]{:S(2)}) copy-start(f32[16,64]{1,0:T(8,128)} %param.10) | copy-start | bytes 12292
  0.0 19.8 %copy-start.28 = (f32[16,64]{1,0:T(8,128)S(1)}, f32[16,64]{1,0:T(8,128)}, u32[]{:S(2)}) copy-start(f32[16,64]{1,0:T(8,128)} %param.11) | copy-start | bytes 12292
  1.6 988.8 %collective-permute-start.1 = (bf16[2,1024]{0,1:T(8,128)(2,1)}, bf16[2,1024]{0,1:T(8,128)(2,1)}, u32[]{:S(2)}, u32[]{:S(2)}) collective-permute-start(bf16[2,1024]{0,1:T(8,128)(2,1)} %copy.43), channel_id=1, source_target_pairs={{0,4},{4,8},{8,12},{12,16},{16,20},{20,24},{24,28},{1,5},{5,9},{9,... | collective-permute-start | bytes 12296 | tf_op jit(solution)/shard_map/ppermute | solution.py:12
  8.8 983.3 %collective-permute-start.2 = (bf16[2,1024]{0,1:T(8,128)(2,1)}, bf16[2,1024]{0,1:T(8,128)(2,1)}, u32[]{:S(2)}, u32[]{:S(2)}) collective-permute-start(bf16[2,1024]{0,1:T(8,128)(2,1)} %copy.45), channel_id=1, source_target_pairs={{0,4},{4,8},{8,12},{12,16},{16,20},{20,24},{24,28},{1,5},{5,9},{9,... | collective-permute-start | bytes 12296 | tf_op jit(solution)/shard_map/ppermute | solution.py:12
  13.9 1093.9 %collective-permute-start = (bf16[2,1024]{0,1:T(8,128)(2,1)}, bf16[2,1024]{0,1:T(8,128)(2,1)}, u32[]{:S(2)}, u32[]{:S(2)}) collective-permute-start(bf16[2,1024]{0,1:T(8,128)(2,1)} %copy.41), channel_id=1, source_target_pairs={{0,4},{4,8},{8,12},{12,16},{16,20},{20,24},{24,28},{1,5},{5,9},{9,... | collective-permute-start | bytes 12296 | tf_op jit(solution)/shard_map/ppermute | solution.py:12
  20.8 2.8 copy-start.5
  21.0 3.9 copy-start.6
  26.3 2.4 copy-start.14
  888.8 101.6 %copy-start.2 = (bf16[512,1024]{0,1:T(8,128)(2,1)S(1)}, bf16[512,1024]{0,1:T(8,128)(2,1)}, u32[]{:S(2)}) copy-start(bf16[512,1024]{0,1:T(8,128)(2,1)} %copy.44) | copy-start | bytes 3145732
  990.4 1.7 copy-start.1
  992.0 1.6 copy-start.20
  992.0 1.6 copy-start.21
  992.0 1.6 copy-start.22
  993.7 3.7 copy-start.9
  993.7 3.7 copy-start.26
  997.4 2.8 copy-start.11
  1031.6 2.8 copy-start.10
  1034.4 3.0 copy-start.15
  1034.4 3.2 copy-start.3
  1034.4 3.2 copy-start.4
  1037.6 66.0 %copy-start.13 = (f32[16,64]{0,1:T(8,128)S(1)}, f32[16,64]{0,1:T(8,128)}, u32[]{:S(2)}) copy-start(f32[16,64]{0,1:T(8,128)} %copy-done.12) | copy-start | bytes 12292
  1037.6 65.9 %copy-start.27 = (f32[512]{0:T(512)S(1)}, f32[512]{0:T(512)}, u32[]{:S(2)}) copy-start(f32[512]{0:T(512)} %fusion.38) | copy-start | bytes 6148
  1103.6 4.2 copy-start
  (10 other events, 15.0 us)
where the time goes:
time: 1110 us
  local copies, waits for them, and re-layouts  977 us (88%)
  matrix products  72.7 us (7%)
  blocking collectives  31.4 us (3%)
  other arithmetic  18.9 us (2%)
  starting transfers between devices  12.5 us (1%)
    gather x2, local copies, waits for them, and re-layouts, toeplitz(): picked = jnp.take(taps, jnp.clip(lag, 0, count - 1), axis=1)  962 us
    dot_general x1, matrix products, body(): local = jnp.einsum('gts,ksgj->ktgj', toe, blocks, precision=high)  65.9 us
    all_gather x1, blocking collectives, body(): piece = lax.all_gather(fresh, 'ctx', axis=0, tiled=True)  31.4 us
  transfers between devices with their start and end apart: 3, of which 0 were waited for; matrix products, arithmetic and copies ran while one was open for 95% of the time, Pallas kernels for 0%

commit v1 on v0

v1 whole, which is shorter than its diff:
```python
import functools

import jax
import jax.numpy as jnp
from jax import lax
from jax.experimental import pallas as pl
from jax.experimental.pallas import tpu as pltpu
from jax.sharding import PartitionSpec as P

LANES = 128
SUB = 8
F32 = jnp.float32
BF16 = jnp.bfloat16


def split2(x):
    hi = x.astype(BF16)
    return hi, (x - hi.astype(F32)).astype(BF16)


def expand(table, tile, lanes, size):
    groups = table.shape[1]
    row = lax.broadcasted_iota(jnp.int32, (groups, lanes), 0)
    col = lax.broadcasted_iota(jnp.int32, (groups, lanes), 1)
    pick = (row == tile * (lanes // size) + col // size).astype(BF16)
    one, rest = split2(table)
    two, three = split2(table - one.astype(F32))
    out = jnp.dot(one, pick, preferred_element_type=F32)
    out = out + jnp.dot(two, pick, preferred_element_type=F32)
    return out + jnp.dot(three, pick, preferred_element_type=F32)


def norm_of(decay):
    x = 2.0 * decay
    series = x * (1.0 - x * (0.5 - x * (1.0 / 6 - x * (1.0 / 24 - x * (1.0 / 120 - x * (1.0 / 720))))))
    return jnp.sqrt(series)


def short3(x, before, taps):
    full = jnp.concatenate([before, x], 0)
    one = pltpu.roll(full, 1, 0)[SUB:]
    two = pltpu.roll(full, 2, 0)[SUB:]
    return taps[0] * x + taps[1] * one + taps[2] * two


def state_kernel(size, halo_ref, k_ref, v_ref, sf_ref, decay_ref, gated_ref, fresh_ref, spread_ref):
    length, lanes = k_ref.shape
    modes = decay_ref.shape[0]
    first = lax.axis_index("ctx") > 0
    keep = jnp.where(first, 1.0, 0.0).astype(F32)
    rates = expand(decay_ref[...], pl.program_id(0), lanes, size)
    spread_ref[...] = rates
    for part in range(lanes // LANES):
        at = slice(part * LANES, (part + 1) * LANES)
        rate = rates[:, at]
        step8 = jnp.exp(-float(SUB) * rate)
        step8 = [jnp.broadcast_to(step8[n : n + 1], (SUB, LANES)) for n in range(modes)]
        kt = [sf_ref[1, i : i + 1, at] for i in range(3)]
        vt = [sf_ref[2, i : i + 1, at] for i in range(3)]
        k_before = halo_ref[2 * SUB : 4 * SUB, at].astype(F32)[SUB:] * keep
        v_before = halo_ref[4 * SUB : 6 * SUB, at].astype(F32)[SUB:] * keep

        def step(i, carry):
            k_before, v_before, acc = carry
            rows = pl.ds(pl.multiple_of(i * 2 * SUB, 2 * SUB), 2 * SUB)
            k = k_ref[rows, at].astype(F32)
            v = v_ref[rows, at].astype(F32)
            gated = short3(k, k_before, kt) * short3(v, v_before, vt)
            gated_ref[rows, at] = gated
            for half in range(2):
                x = gated[half * SUB : (half + 1) * SUB]
                acc = [a * s + x for a, s in zip(acc, step8)]
            return k[SUB:], v[SUB:], acc

        zero = jnp.zeros((SUB, LANES), F32)
        _, _, acc = lax.fori_loop(
            0, length // (2 * SUB), step, (k_before, v_before, [zero] * modes), unroll=4
        )
        back = (SUB - 1 - lax.broadcasted_iota(jnp.int32, (SUB, LANES), 0)).astype(F32)
        for n in range(modes):
            weighted = acc[n] * jnp.exp(-rate[n : n + 1] * back)
            fresh_ref[n : n + 1, at] = jnp.sum(weighted, axis=0, keepdims=True)


def fold8(parts):
    sub = lax.broadcasted_iota(jnp.int32, parts[0].shape, 0)

    def join(a, b, gap):
        low = (sub // gap) % 2 == 0
        return jnp.where(low, a + pltpu.roll(a, SUB - gap, 0), b + pltpu.roll(b, gap, 0))

    parts = [join(parts[t], parts[t + 4], 4) for t in range(4)]
    parts = [join(parts[t], parts[t + 2], 2) for t in range(2)]
    return join(parts[0], parts[1], 1)


def local_kernel(size, first_tile, gated_ref, spread_ref, res_ref, skip_ref, out_ref):
    length, lanes = gated_ref.shape
    modes = res_ref.shape[0]
    rate = spread_ref[...]
    weight = expand(res_ref[...], first_tile + pl.program_id(0), lanes, size) * norm_of(rate)
    ratio = jnp.exp(-rate)
    skip = skip_ref[...]

    def step(i, state):
        base = pl.multiple_of(i * SUB, SUB)
        parts = []
        for t in range(SUB):
            x = gated_ref[pl.ds(base + t, 1), :]
            state = state * ratio + x
            mixed = state * weight
            total = mixed[:SUB]
            for at in range(SUB, modes, SUB):
                total = total + mixed[at : at + SUB]
            parts.append(total)
        rows = pl.ds(base, SUB)
        out_ref[rows, :] = fold8(parts) + skip * gated_ref[rows, :]
        return state

    lax.fori_loop(0, length // SUB, step, jnp.zeros((modes, lanes), F32))


def lead_kernel(size, res_ref, decay_ref, hi_ref, lo_ref):
    length, lanes = hi_ref.shape
    modes = decay_ref.shape[0]
    lane = lax.broadcasted_iota(jnp.int32, (modes, lanes), 1)
    own = lane % size == lax.broadcasted_iota(jnp.int32, (modes, lanes), 0)

    def row(table):
        wide = expand(table, pl.program_id(0), lanes, size)
        return jnp.sum(jnp.where(own, wide, 0.0), axis=0, keepdims=True)

    rate = row(decay_ref[...])
    weight = row(res_ref[...]) * norm_of(rate)
    steps = lax.broadcasted_iota(jnp.int32, (length, lanes), 0).astype(F32) + 1.0
    hi, lo = split2(weight * jnp.exp(-rate * steps))
    hi_ref[...] = hi
    lo_ref[...] = lo


def mix_kernel(size, bit, halo_ref, q_ref, sf_ref, spread_ref, prefix_ref, got_ref, local_ref, hi_ref, lo_ref, out_ref):
    length, lanes = q_ref.shape
    modes = spread_ref.shape[0]
    me = lax.axis_index("ctx")
    keep = jnp.where(me > 0, 1.0, 0.0).astype(F32)
    upper = jnp.where((me // bit) % 2 == 1, 1.0, 0.0).astype(F32)
    gap = (me % bit * length).astype(F32)
    state = prefix_ref[...] + jnp.exp(-spread_ref[...] * gap) * (got_ref[...] * upper)
    groups = lanes // size
    rows = groups * modes
    row = lax.broadcasted_iota(jnp.int32, (rows, lanes), 0)
    col = lax.broadcasted_iota(jnp.int32, (rows, lanes), 1)
    wide = jnp.where(row // modes == col // size, jnp.concatenate([state] * groups, 0), 0.0)
    hi, lo = split2(wide)
    term = jnp.dot(hi_ref[...], hi, preferred_element_type=F32)
    term = term + jnp.dot(lo_ref[...], hi, preferred_element_type=F32)
    term = term + jnp.dot(hi_ref[...], lo, preferred_element_type=F32)
    before = halo_ref[...].astype(F32)[SUB:] * keep
    q_short = short3(q_ref[...].astype(F32), before, [sf_ref[0, i : i + 1, :] for i in range(3)])
    out_ref[...] = (q_short * (local_ref[...] + term)).astype(BF16)


def body(query_in, key_in, value_in, residues, decay_rate, short_filter, skip_gain):
    length, width = query_in.shape
    modes, groups = residues.shape
    size = width // groups
    ranks = lax.axis_size("ctx")
    me = lax.axis_index("ctx")
    rim = 2 * SUB
    edge = length - rim
    rims = jnp.concatenate([query_in[edge:], key_in[edge:], value_in[edge:]], 0)
    with jax.named_scope("halo"):
        halo = lax.ppermute(rims, "ctx", [(i, (i + 1) % ranks) for i in range(ranks)])

    tile = min(width, 2 * LANES)
    grid = width // tile
    whole = lambda a: pl.BlockSpec(a.shape, lambda j: (0,) * a.ndim)
    cols = lambda rows, lanes, first=0: pl.BlockSpec((rows, lanes), lambda j: (0, j + first))
    taps_spec = lambda lanes: pl.BlockSpec((3, 3, lanes), lambda j: (0, 0, j))

    lead_shape = jax.ShapeDtypeStruct((length, groups * modes), BF16)
    lead_hi, lead_lo = pl.pallas_call(
        functools.partial(lead_kernel, size),
        grid=(groups * modes // tile,),
        in_specs=[whole(residues), whole(decay_rate)],
        out_specs=[cols(length, tile)] * 2,
        out_shape=[lead_shape] * 2,
        name="lead",
    )(residues, decay_rate)

    gated, fresh, spread = pl.pallas_call(
        functools.partial(state_kernel, size),
        grid=(grid,),
        in_specs=[cols(3 * rim, tile), cols(length, tile), cols(length, tile), taps_spec(tile), whole(decay_rate)],
        out_specs=[cols(length, tile), cols(modes, tile), cols(modes, tile)],
        out_shape=[
            jax.ShapeDtypeStruct((length, width), F32),
            jax.ShapeDtypeStruct((modes, width), F32),
            jax.ShapeDtypeStruct((modes, width), F32),
        ],
        name="state",
    )(halo, key_in, value_in, short_filter, decay_rate)

    local = pl.pallas_call(
        functools.partial(local_kernel, size, 0),
        grid=(grid,),
        in_specs=[cols(length, tile), cols(modes, tile), whole(residues), cols(1, tile)],
        out_specs=cols(length, tile),
        out_shape=jax.ShapeDtypeStruct((length, width), F32),
        name="local",
    )(gated, spread, residues, skip_gain)

    total, prefix, bit = fresh, jnp.zeros_like(fresh), 1
    while bit < ranks:
        with jax.named_scope("scan%d" % bit):
            got = lax.ppermute(total, "ctx", [(i, i ^ bit) for i in range(ranks)])
        if bit * 2 < ranks:
            upper = (me // bit) % 2 == 1
            span = jnp.exp(-spread * float(length * bit))
            reach = jnp.exp(-spread * (length * (me % bit)).astype(F32))
            prefix = prefix + jnp.where(upper, reach * got, 0.0)
            total = jnp.where(upper, total + span * got, got + span * total)
        bit *= 2

    return pl.pallas_call(
        functools.partial(mix_kernel, size, bit // 2),
        grid=(grid,),
        in_specs=[
            cols(rim, tile),
            cols(length, tile),
            taps_spec(tile),
            cols(modes, tile),
            cols(modes, tile),
            cols(modes, tile),
            cols(length, tile),
            cols(length, tile),
            cols(length, tile),
        ],
        out_specs=cols(length, tile),
        out_shape=jax.ShapeDtypeStruct((length, width), BF16),
        name="mix",
    )(halo, query_in, short_filter, spread, prefix, got, local, lead_hi, lead_lo)


def solution(mesh):
    placed = (
        P("ctx", "fsdp"),
        P("ctx", "fsdp"),
        P("ctx", "fsdp"),
        P(None, "fsdp"),
        P(None, "fsdp"),
        P(None, None, "fsdp"),
        P(None, "fsdp"),
    )
    return jax.shard_map(
        body, mesh=mesh, in_specs=placed, out_specs=P("ctx", "fsdp"), check_vma=False
    )
```

time: 1110 us -> 53 us (0.05)
  local copies, waits for them, and re-layouts: 977 us -> 3.55 us
  matrix products: 72.7 us -> 0 us
  blocking collectives: 31.4 us -> 0 us
  Pallas kernels: 0 us -> 28 us
  other arithmetic: 18.9 us -> 2.42 us
  waiting for transfers between devices: 0.01 us -> 14.5 us
    gather x2 -> x0, local copies, waits for them, and re-layouts: 962 us -> none  [toeplitz(): picked = jnp.take(taps, jnp.clip(lag, 0, count - 1), axis=1)]
    dot_general x3 -> x0, matrix products: 72.7 us -> none  [the longest x1 65.9 us: body(): local = jnp.einsum('gts,ksgj->ktgj', toe, blocks, precision=high)]
    all_gather x1 -> x0, blocking collectives: 31.4 us -> none  [body(): piece = lax.all_gather(fresh, 'ctx', axis=0, tiled=True)]
    pallas_call x0 -> x4, Pallas kernels: none -> 28 us  [the longest x1 12.4 us: body(): pl.pallas_call(functools.partial(local_kernel, size, 0), grid=(grid,), in...]
    ppermute x3 -> x4, waiting for transfers between devices: 0.01 us -> 14.5 us  [the longest x3 8.67 us: body(): got = lax.ppermute(total, 'ctx', [(i, i ^ bit) for i in range(ranks)])]
  transfers between devices with their start and end apart: 3 -> 4, of which waited for: 0 -> 3; matrix products, arithmetic and copies ran while one was open for 95% -> 0% of each run, Pallas kernels for 0% -> 30%
where the time goes in v1:
time: 53 us; the launch traced here: 52.4 us
  Pallas kernels  28 us (53%)
  waiting for transfers between devices  14.5 us (27%)
  starting transfers between devices  3.87 us (7%)
  local copies, waits for them, and re-layouts  3.55 us (7%)
  other arithmetic  2.42 us (5%)
    pallas_call x1, Pallas kernels, body(): pl.pallas_call(functools.partial(local_kernel, size, 0), grid=(grid,), in...  12.4 us
    ppermute x3, waiting for transfers between devices, body(): got = lax.ppermute(total, 'ctx', [(i, i ^ bit) for i in range(ranks)])  8.67 us
    pallas_call x1, Pallas kernels, body(): pl.pallas_call(functools.partial(state_kernel, size), grid=(grid,), in_sp...  7.05 us
    ppermute x1, waiting for transfers between devices, body(): lax.ppermute(rims, 'ctx', [(i, (i + 1) % ranks) for i in range(ranks)])  5.83 us
    pallas_call x1, Pallas kernels, body(): pl.pallas_call(functools.partial(mix_kernel, size, bit // 2), grid=(grid,...  5.09 us
    pallas_call x1, Pallas kernels, body(): pl.pallas_call(functools.partial(lead_kernel, size), grid=(groups * modes...  3.46 us
    ppermute x1, starting transfers between devices, body(): lax.ppermute(rims, 'ctx', [(i, (i + 1) % ranks) for i in range(ranks)])  3.02 us
    select_n x2, other arithmetic, body(): total = jnp.where(upper, total + span * got, got + span * total)  2.41 us
  transfers between devices with their start and end apart: 4, of which 3 were waited for; matrix products, arithmetic and copies ran while one was open for 0% of the time, Pallas kernels for 30%

profile of v1, /device:TPU:0, one launch (start us, length us, event | category | flops | bytes accessed | tf_op | source)
XLA Modules:
  0.0 52.4 jit_solution(299012012844746001)
XLA Ops:
  0.0 0.8 %slice.10 = bf16[16,1024]{1,0:T(8,128)(2,1)S(1)} slice(bf16[512,1024]{1,0:T(8,128)(2,1)} %k_ref.1), slice={[496:512], [0:1024]} | slice | bytes 65536 | tf_op jit(solution)/shard_map/slice | solution.py:171
  0.8 0.8 %slice.11 = bf16[16,1024]{1,0:T(8,128)(2,1)S(1)} slice(bf16[512,1024]{1,0:T(8,128)(2,1)} %v_ref.1), slice={[496:512], [0:1024]} | slice | bytes 65536 | tf_op jit(solution)/shard_map/slice | solution.py:171
  1.5 0.8 %slice.9 = bf16[16,1024]{1,0:T(8,128)(2,1)S(1)} slice(bf16[512,1024]{1,0:T(8,128)(2,1)} %q_ref.1), slice={[496:512], [0:1024]} | slice | bytes 65536 | tf_op jit(solution)/shard_map/slice | solution.py:171
  2.3 3.0 %collective-permute-start = (bf16[48,1024]{1,0:T(8,128)(2,1)S(1)}, bf16[48,1024]{1,0:T(8,128)(2,1)S(1)}, u32[]{:S(2)}, u32[]{:S(2)}) collective-permute-start(bf16[48,1024]{1,0:T(8,128)(2,1)S(1)} %pad_maximum_fusion), channel_id=1, source_target_pairs={{0,4},{4,8},{8,12},{12,16},{16,20},{20,24},{24,28},{28,0},{1,5},{5... | collective-permute-start | bytes 294920 | tf_op jit(solution)/shard_map/halo/ppermute | solution.py:173
  5.3 5.8 %collective-permute-done.halo_ref = bf16[48,1024]{1,0:T(8,128)(2,1)S(1)} collective-permute-done((bf16[48,1024]{1,0:T(8,128)(2,1)S(1)}, bf16[48,1024]{1,0:T(8,128)(2,1)S(1)}, u32[]{:S(2)}, u32[]{:S(2)}) %collective-permute-start) | collective-permute-done | bytes 98336 | tf_op jit(solution)/shard_map/halo/ppermute | solution.py:173
  11.1 0.0 copy-start
  11.1 0.6 %copy-done = bf16[48,1024]{1,0:T(8,128)(2,1)} copy-done((bf16[48,1024]{1,0:T(8,128)(2,1)}, bf16[48,1024]{1,0:T(8,128)(2,1)S(1)}, u32[]{:S(2)}) %copy-start) | copy-done | bytes 98328
  11.8 7.0 %state.1 = (f32[512,1024]{1,0:T(8,128)}, f32[16,1024]{1,0:T(8,128)}, f32[16,1024]{1,0:T(8,128)}) custom-call(bf16[48,1024]{1,0:T(8,128)(2,1)} %copy-done, bf16[512,1024]{1,0:T(8,128)(2,1)} %k_ref.1, bf16[512,1024]{1,0:T(8,128)(2,1)} %v_ref.1, f32[3,3,1024]{2,1,0:T(4,128)} %sf_ref.3, f32[16,64]{1,0:T(8,128)} %decay_ref.3), custom_call_target="tpu_custom_call" | custom-call | tf_op jit(solution)/shard_map/state/pallas_call | solution.py:191
  18.8 0.0 collective-permute-start.1
  18.9 4.5 %collective-permute-done.1 = f32[16,1024]{1,0:T(8,128)S(1)} collective-permute-done((f32[16,1024]{1,0:T(8,128)}, f32[16,1024]{1,0:T(8,128)S(1)}, u32[]{:S(2)}, u32[]{:S(2)}) %collective-permute-start.1) | collective-permute-done | bytes 65568 | tf_op jit(solution)/shard_map/scan1/ppermute | solution.py:216
  23.3 0.9 %add_select_fusion.1 = f32[16,1024]{1,0:T(8,128)S(1)} fusion(f32[16,1024]{1,0:T(8,128)S(1)} %collective-permute-done.1, f32[16,1024]{1,0:T(8,128)} %get-tuple-element.11, f32[16,1024]{1,0:T(8,128)} %get-tuple-element.10.spread_ref, pred[]{:T(512)S(6)} %eq.11), kind=kLoop, calls=%fused_computation.3 | loop fusion | flops 114688 | bytes 262145 | tf_op jit(solution)/shard_map/jit(_where)/select_n | solution.py:222
  24.2 0.1 collective-permute-start.2
  24.3 4.2 %collective-permute-done.2 = f32[16,1024]{1,0:T(8,128)S(1)} collective-permute-done((f32[16,1024]{1,0:T(8,128)S(1)}, f32[16,1024]{1,0:T(8,128)S(1)}, u32[]{:S(2)}, u32[]{:S(2)}) %collective-permute-start.2) | collective-permute-done | bytes 65568 | tf_op jit(solution)/shard_map/scan2/ppermute | solution.py:216
  28.6 1.5 %add_select_fusion = (f32[16,1024]{1,0:T(8,128)S(1)}, f32[16,1024]{1,0:T(8,128)}) fusion(f32[16,1024]{1,0:T(8,128)S(1)} %collective-permute-done.2, f32[16,1024]{1,0:T(8,128)S(1)} %add_select_fusion.1, f32[16,1024]{1,0:T(8,128)} %get-tuple-element.10.spread_ref, pred[]{:T(512)S(6)} %eq.12, f32[]{:T(128)S(6)} %convert_element_type.4, ...), kind=kLoop, calls=%fused_computation.1 | loop fusion | flops 229376 | bytes 393222 | tf_op jit(solution)/shard_map/jit(_where)/select_n | solution.py:222
  30.1 0.8 %collective-permute-start.3 = (f32[16,1024]{1,0:T(8,128)S(1)}, f32[16,1024]{1,0:T(8,128)S(1)}, u32[]{:S(2)}, u32[]{:S(2)}) collective-permute-start(f32[16,1024]{1,0:T(8,128)S(1)} %get-tuple-element.15), channel_id=1, source_target_pairs={{0,16},{4,20},{8,24},{12,28},{16,0},{20,4},{24,8},{28,12},{1,17},{... | collective-permute-start | bytes 196616 | tf_op jit(solution)/shard_map/scan4/ppermute | solution.py:216
  30.8 3.5 %lead.1 = (bf16[512,1024]{1,0:T(8,128)(2,1)}, bf16[512,1024]{1,0:T(8,128)(2,1)}) custom-call(f32[16,64]{1,0:T(8,128)} %res_ref.3, f32[16,64]{1,0:T(8,128)} %decay_ref.3), custom_call_target="tpu_custom_call" | custom-call | tf_op jit(solution)/shard_map/lead/pallas_call | solution.py:182
  34.3 12.4 %local.1.local_ref = f32[512,1024]{1,0:T(8,128)} custom-call(f32[512,1024]{1,0:T(8,128)} %get-tuple-element.12.gated_ref, f32[16,1024]{1,0:T(8,128)} %get-tuple-element.10.spread_ref, f32[16,64]{1,0:T(8,128)} %res_ref.3, f32[1,1024]{1,0:T(1,128)} %skip_ref.1), custom_call_target="tpu_custom_call" | custom-call | tf_op jit(solution)/shard_map/local/pallas_call | solution.py:204
  46.7 0.0 collective-permute-done.3.got_ref
  46.7 0.0 copy-start.1
  46.7 0.6 %copy-done.1 = f32[16,1024]{1,0:T(8,128)} copy-done((f32[16,1024]{1,0:T(8,128)}, f32[16,1024]{1,0:T(8,128)S(1)}, u32[]{:S(2)}) %copy-start.1) | copy-done | bytes 65560
  47.3 5.1 %mix.1 = bf16[512,1024]{1,0:T(8,128)(2,1)} custom-call(bf16[48,1024]{1,0:T(8,128)(2,1)} %copy-done, bf16[512,1024]{1,0:T(8,128)(2,1)} %q_ref.1, f32[3,3,1024]{2,1,0:T(4,128)} %sf_ref.3, f32[16,1024]{1,0:T(8,128)} %get-tuple-element.10.spread_ref, f32[16,1024]{1,0:T(8,128)} %get-tuple-element.16.prefix_ref, f32[16,1024]{1,0:T(8,128)} %copy-done.1, ...), custom_call_target="tpu_custom_call" | custom-call | tf_op jit(solution)/shard_map/mix/pallas_call | solution.py:225
  (1 shorter events, 0.0 us)
Async XLA Ops:
  2.3 8.9 %collective-permute-start = (bf16[48,1024]{1,0:T(8,128)(2,1)S(1)}, bf16[48,1024]{1,0:T(8,128)(2,1)S(1)}, u32[]{:S(2)}, u32[]{:S(2)}) collective-permute-start(bf16[48,1024]{1,0:T(8,128)(2,1)S(1)} %pad_maximum_fusion), channel_id=1, source_target_pairs={{0,4},{4,8},{8,12},{12,16},{16,20},{20,24},{24,28},{28,0},{1,5},{5... | collective-permute-start | bytes 294920 | tf_op jit(solution)/shard_map/halo/ppermute | solution.py:173
  11.1 0.6 %copy-start = (bf16[48,1024]{1,0:T(8,128)(2,1)}, bf16[48,1024]{1,0:T(8,128)(2,1)S(1)}, u32[]{:S(2)}) copy-start(bf16[48,1024]{1,0:T(8,128)(2,1)S(1)} %collective-permute-done.halo_ref) | copy-start | bytes 294916
  18.8 4.5 %collective-permute-start.1 = (f32[16,1024]{1,0:T(8,128)}, f32[16,1024]{1,0:T(8,128)S(1)}, u32[]{:S(2)}, u32[]{:S(2)}) collective-permute-start(f32[16,1024]{1,0:T(8,128)} %get-tuple-element.11), channel_id=1, source_target_pairs={{0,4},{4,0},{8,12},{12,8},{16,20},{20,16},{24,28},{28,24},{1,5},{5... | collective-permute-start | bytes 196616 | tf_op jit(solution)/shard_map/scan1/ppermute | solution.py:216
  24.2 4.3 %collective-permute-start.2 = (f32[16,1024]{1,0:T(8,128)S(1)}, f32[16,1024]{1,0:T(8,128)S(1)}, u32[]{:S(2)}, u32[]{:S(2)}) collective-permute-start(f32[16,1024]{1,0:T(8,128)S(1)} %add_select_fusion.1), channel_id=1, source_target_pairs={{0,8},{4,12},{8,0},{12,4},{16,24},{20,28},{24,16},{28,20},{1,9},{5... | collective-permute-start | bytes 196616 | tf_op jit(solution)/shard_map/scan2/ppermute | solution.py:216
  30.1 16.6 %collective-permute-start.3 = (f32[16,1024]{1,0:T(8,128)S(1)}, f32[16,1024]{1,0:T(8,128)S(1)}, u32[]{:S(2)}, u32[]{:S(2)}) collective-permute-start(f32[16,1024]{1,0:T(8,128)S(1)} %get-tuple-element.15), channel_id=1, source_target_pairs={{0,16},{4,20},{8,24},{12,28},{16,0},{20,4},{24,8},{28,12},{1,17},{... | collective-permute-start | bytes 196616 | tf_op jit(solution)/shard_map/scan4/ppermute | solution.py:216
  46.7 0.6 %copy-start.1 = (f32[16,1024]{1,0:T(8,128)}, f32[16,1024]{1,0:T(8,128)S(1)}, u32[]{:S(2)}) copy-start(f32[16,1024]{1,0:T(8,128)S(1)} %collective-permute-done.3.got_ref) | copy-start | bytes 196612

commit v2 on v0

v2 whole, which is shorter than its diff:
```python
import functools

import jax
import jax.numpy as jnp
from jax import lax
from jax.experimental import pallas as pl
from jax.experimental.pallas import tpu as pltpu
from jax.sharding import PartitionSpec as P


LANES = 128
WIDE = 256
SUB = 8
RIM = 16
F32 = jnp.float32
BF16 = jnp.bfloat16
VMEM = pl.BlockSpec(memory_space=pltpu.VMEM)
PARAMS = pltpu.CompilerParams(vmem_limit_bytes=8 << 20)


def split2(x):
    hi = x.astype(BF16)
    return hi, (x - hi.astype(F32)).astype(BF16)


def expand(table, first, lanes, size):
    groups = table.shape[1]
    row = lax.broadcasted_iota(jnp.int32, (groups, lanes), 0)
    col = lax.broadcasted_iota(jnp.int32, (groups, lanes), 1)
    pick = (row == first + col // size).astype(BF16)
    one, _ = split2(table)
    two, three = split2(table - one.astype(F32))
    out = jnp.dot(one, pick, preferred_element_type=F32)
    out = out + jnp.dot(two, pick, preferred_element_type=F32)
    return out + jnp.dot(three, pick, preferred_element_type=F32)


def norm_of(decay):
    x = 2.0 * decay
    total = jnp.full_like(x, 1.0)
    for k in range(9, 1, -1):
        total = 1.0 - x * total * (1.0 / k)
    return jnp.sqrt(x * total)


def short3(ref, start, count, taps):
    at = SUB + start
    out = taps[0] * ref[at : at + count]
    out = out + taps[1] * ref[at - 1 : at - 1 + count]
    return out + taps[2] * ref[at - 2 : at - 2 + count]


def rim_kernel(q_ref, k_ref, v_ref, out_ref, sem):
    copies = []
    for i, ref in enumerate((q_ref, k_ref, v_ref)):
        rim = ref.at[ref.shape[0] - RIM :]
        copies.append(pltpu.make_async_copy(rim, out_ref.at[i * RIM : (i + 1) * RIM], sem.at[i]))
        copies[i].start()
    for copy in copies:
        copy.wait()


def table_kernel(res_ref, decay_ref, lead_hi, lead_lo, tail_hi, tail_lo, spread_ref, span_ref, reach_ref):
    length, width = lead_hi.shape
    modes = decay_ref.shape[0]
    phases = span_ref.shape[0]
    me = lax.axis_index("ctx")
    lane = lax.broadcasted_iota(jnp.int32, (modes, LANES), 1)
    own = lane % modes == lax.broadcasted_iota(jnp.int32, (modes, LANES), 0)
    down = lax.broadcasted_iota(jnp.int32, (LANES, LANES), 0).astype(F32)
    along = lax.broadcasted_iota(jnp.int32, (LANES, LANES), 1).astype(F32)
    for tile in range(width // LANES):
        at = slice(tile * LANES, (tile + 1) * LANES)
        rates = expand(decay_ref[...], tile * (LANES // modes), LANES, modes)
        gains = expand(res_ref[...], tile * (LANES // modes), LANES, modes) * norm_of(rates)
        rate = jnp.sum(jnp.where(own, rates, 0.0), axis=0, keepdims=True)
        gain = jnp.sum(jnp.where(own, gains, 0.0), axis=0, keepdims=True)
        spread_ref[:, at] = rates
        for b in range(phases):
            upper = jnp.where((me >> b) % 2 == 1, 1.0, 0.0).astype(F32)
            gap = (me % (1 << b) * length).astype(F32)
            span_ref[b, :, at] = jnp.exp(-rates * float(length << b))
            reach_ref[b, :, at] = jnp.exp(-rates * gap) * upper
        lead = gain * jnp.exp(-rate * (down + 1.0))
        hop = jnp.exp(-rate * float(LANES))
        rate_rows = jnp.transpose(jnp.broadcast_to(rate, (LANES, LANES)))
        tail = jnp.exp(-rate_rows * (LANES - 1.0 - along))
        hop_rows = jnp.exp(-rate_rows * float(LANES))
        for c in range(length // LANES):
            rows = slice(c * LANES, (c + 1) * LANES)
            back = slice(length - (c + 1) * LANES, length - c * LANES)
            hi, lo = split2(lead)
            lead_hi[rows, at], lead_lo[rows, at] = hi, lo
            hi, lo = split2(tail)
            tail_hi[at, back], tail_lo[at, back] = hi, lo
            lead = lead * hop
            tail = tail * hop_rows


def state_kernel(size, halo_ref, k_ref, v_ref, sf_ref, tail_hi, tail_lo, gated_ref, fresh_ref, kf, vf, xh, xl):
    length, lanes = k_ref.shape
    modes = fresh_ref.shape[0]
    tile = pl.program_id(0)
    keep = jnp.where(lax.axis_index("ctx") > 0, 1.0, 0.0).astype(F32)
    row = lax.broadcasted_iota(jnp.int32, (modes, LANES), 1) // size
    for part in range(lanes // LANES):
        at = slice(part * LANES, (part + 1) * LANES)
        base = pl.multiple_of(tile * lanes + part * LANES, LANES)
        kf[0:SUB] = halo_ref[RIM : 2 * RIM, at].astype(F32)[SUB:] * keep
        vf[0:SUB] = halo_ref[2 * RIM : 3 * RIM, at].astype(F32)[SUB:] * keep
        kt = [sf_ref[1, i : i + 1, at] for i in range(3)]
        vt = [sf_ref[2, i : i + 1, at] for i in range(3)]
        piece = 64
        for start in range(0, length, piece):
            rows = slice(start, start + piece)
            kf[SUB + start : SUB + start + piece] = k_ref[rows, at].astype(F32)
            vf[SUB + start : SUB + start + piece] = v_ref[rows, at].astype(F32)
            gated = short3(kf, start, piece, kt) * short3(vf, start, piece, vt)
            gated_ref[rows, pl.ds(base, LANES)] = gated
            xh[rows], xl[rows] = split2(gated)
        table = pl.ds(base, LANES)
        out = jnp.dot(tail_hi[table, :], xh[...], preferred_element_type=F32)
        out = out + jnp.dot(tail_lo[table, :], xh[...], preferred_element_type=F32)
        out = out + jnp.dot(tail_hi[table, :], xl[...], preferred_element_type=F32)
        total = jnp.zeros((modes, LANES), F32)
        for g in range(LANES // size):
            total = jnp.where(row == g, out[g * modes : (g + 1) * modes], total)
        fresh_ref[:, pl.ds(base, LANES)] = total


def fold8(parts):
    sub = lax.broadcasted_iota(jnp.int32, parts[0].shape, 0)

    def join(a, b, gap):
        low = (sub // gap) % 2 == 0
        return jnp.where(low, a + pltpu.roll(a, SUB - gap, 0), b + pltpu.roll(b, gap, 0))

    parts = [join(parts[t], parts[t + 4], 4) for t in range(4)]
    parts = [join(parts[t], parts[t + 2], 2) for t in range(2)]
    return join(parts[0], parts[1], 1)


def local_kernel(size, first, gated_ref, spread_ref, res_ref, skip_ref, out_ref):
    length, lanes = out_ref.shape
    modes = res_ref.shape[0]
    at = slice(first, first + lanes)
    rate = spread_ref[:, at]
    weight = expand(res_ref[...], first // size, lanes, size) * norm_of(rate)
    ratio = jnp.exp(-rate)
    skip = skip_ref[:, at]

    def step(i, state):
        base = pl.multiple_of(i * SUB, SUB)
        parts = []
        for t in range(SUB):
            x = gated_ref[pl.ds(base + t, 1), at]
            state = state * ratio + x
            mixed = state * weight
            total = mixed[:SUB]
            for m in range(SUB, modes, SUB):
                total = total + mixed[m : m + SUB]
            parts.append(total)
        rows = pl.ds(base, SUB)
        out_ref[rows, :] = fold8(parts) + skip * gated_ref[rows, at]
        return state

    lax.fori_loop(0, length // SUB, step, jnp.zeros((modes, lanes), F32))


def mix_kernel(size, phases, parts, *refs):
    halo_ref, q_ref, sf_ref, reach_ref, lead_hi, lead_lo = refs[:6]
    gots = refs[6 : 6 + phases]
    locals_ = refs[6 + phases : 6 + phases + parts]
    out_ref, qf, stage, sem = refs[6 + phases + parts :]
    length, width = q_ref.shape
    modes = reach_ref.shape[1]
    keep = jnp.where(lax.axis_index("ctx") > 0, 1.0, 0.0).astype(F32)
    where = []
    for ref in locals_:
        where += [(ref, c) for c in range(0, ref.shape[1], LANES)]
    span = min(WIDE, width)
    groups = span // size
    row = lax.broadcasted_iota(jnp.int32, (groups * modes, span), 0)
    col = lax.broadcasted_iota(jnp.int32, (groups * modes, span), 1)
    block = row // modes == col // size
    copies = []
    for tile in range(width // span):
        at = slice(tile * span, (tile + 1) * span)
        state = reach_ref[0, :, at] * gots[0][:, at]
        for b in range(1, phases):
            state = state + reach_ref[b, :, at] * gots[b][:, at]
        wide = jnp.where(block, jnp.concatenate([state] * groups, 0), 0.0)
        hi, lo = split2(wide)
        term = jnp.dot(lead_hi[:, at], hi, preferred_element_type=F32)
        term = term + jnp.dot(lead_lo[:, at], hi, preferred_element_type=F32)
        term = term + jnp.dot(lead_hi[:, at], lo, preferred_element_type=F32)
        for half in range(span // LANES):
            lane = tile * span + half * LANES
            cut = slice(lane, lane + LANES)
            qf[0:SUB] = halo_ref[0:RIM, cut].astype(F32)[SUB:] * keep
            qf[SUB:] = q_ref[:, cut].astype(F32)
            taps = [sf_ref[0, i : i + 1, cut] for i in range(3)]
            near, c = where[lane // LANES]
            own = near[:, c : c + LANES] + term[:, half * LANES : (half + 1) * LANES]
            stage[:, cut] = (short3(qf, 0, length, taps) * own).astype(BF16)
        copy = pltpu.make_async_copy(stage.at[:, at], out_ref.at[:, at], sem.at[tile])
        copy.start()
        copies.append(copy)
    for copy in copies:
        copy.wait()


def body(query_in, key_in, value_in, residues, decay_rate, short_filter, skip_gain):
    length, width = query_in.shape
    modes, groups = residues.shape
    size = width // groups
    ranks = lax.axis_size("ctx")
    phases = ranks.bit_length() - 1
    rims = pl.pallas_call(
        rim_kernel,
        in_specs=[pl.BlockSpec(memory_space=pltpu.HBM)] * 3,
        out_specs=VMEM,
        out_shape=jax.ShapeDtypeStruct((3 * RIM, width), BF16),
        scratch_shapes=[pltpu.SemaphoreType.DMA((3,))],
        compiler_params=pltpu.CompilerParams(vmem_limit_bytes=60 << 20),
        name="rim",
    )(query_in, key_in, value_in)
    halo = lax.ppermute(rims, "ctx", [(i, (i + 1) % ranks) for i in range(ranks)])

    lead_shape = jax.ShapeDtypeStruct((length, width), BF16)
    tail_shape = jax.ShapeDtypeStruct((width, length), BF16)
    scan_shape = jax.ShapeDtypeStruct((phases, modes, width), F32)
    row_shape = jax.ShapeDtypeStruct((modes, width), F32)
    lead_hi, lead_lo, tail_hi, tail_lo, spread, span, reach = pl.pallas_call(
        table_kernel,
        in_specs=[VMEM] * 2,
        out_specs=[VMEM] * 7,
        out_shape=[lead_shape, lead_shape, tail_shape, tail_shape, row_shape, scan_shape, scan_shape],
        compiler_params=PARAMS,
        cost_estimate=pl.CostEstimate(flops=10**7, bytes_accessed=5 << 20, transcendentals=0),
        name="tables",
    )(residues, decay_rate)

    tile = min(width, WIDE)
    cols = lambda rows: pl.BlockSpec((rows, tile), lambda j: (0, j))
    gated, fresh = pl.pallas_call(
        functools.partial(state_kernel, size),
        grid=(width // tile,),
        in_specs=[
            cols(3 * RIM),
            cols(length),
            cols(length),
            pl.BlockSpec((3, 3, tile), lambda j: (0, 0, j)),
            VMEM,
            VMEM,
        ],
        out_specs=[VMEM] * 2,
        out_shape=[jax.ShapeDtypeStruct((length, width), F32), row_shape],
        scratch_shapes=[
            pltpu.VMEM((SUB + length, LANES), F32),
            pltpu.VMEM((SUB + length, LANES), F32),
            pltpu.VMEM((length, LANES), BF16),
            pltpu.VMEM((length, LANES), BF16),
        ],
        compiler_params=PARAMS,
        name="state",
    )(halo, key_in, value_in, short_filter, tail_hi, tail_lo)

    unit = LANES if width // LANES >= 2 * phases else min(width, WIDE)
    cuts = [width // unit * b // phases * unit for b in range(phases + 1)]
    nears, gots, total = [], [], fresh
    for b in range(phases):
        got = lax.ppermute(total, "ctx", [(i, i ^ (1 << b)) for i in range(ranks)])
        gots.append(got)
        lanes = cuts[b + 1] - cuts[b]
        if lanes:
            nears.append(
                pl.pallas_call(
                    functools.partial(local_kernel, size, cuts[b]),
                    in_specs=[VMEM] * 4,
                    out_specs=VMEM,
                    out_shape=jax.ShapeDtypeStruct((length, lanes), F32),
                    compiler_params=PARAMS,
                    cost_estimate=pl.CostEstimate(flops=10**7, bytes_accessed=4 << 20, transcendentals=0),
                    name="near",
                )(gated, spread, residues, skip_gain)
            )
        if b + 1 < phases:
            upper = (lax.axis_index("ctx") >> b) % 2 == 1
            total = jnp.where(upper, total + span[b] * got, got + span[b] * total)

    return pl.pallas_call(
        functools.partial(mix_kernel, size, phases, len(nears)),
        in_specs=[VMEM] * (6 + phases + len(nears)),
        out_specs=pl.BlockSpec(memory_space=pl.ANY),
        out_shape=jax.ShapeDtypeStruct((length, width), BF16),
        scratch_shapes=[
            pltpu.VMEM((SUB + length, LANES), F32),
            pltpu.VMEM((length, width), BF16),
            pltpu.SemaphoreType.DMA((max(1, width // WIDE),)),
        ],
        compiler_params=PARAMS,
        name="mix",
    )(halo, query_in, short_filter, reach, lead_hi, lead_lo, *gots, *nears)


def solution(mesh):
    placed = (
        P("ctx", "fsdp"),
        P("ctx", "fsdp"),
        P("ctx", "fsdp"),
        P(None, "fsdp"),
        P(None, "fsdp"),
        P(None, None, "fsdp"),
        P(None, "fsdp"),
    )
    return jax.shard_map(
        body, mesh=mesh, in_specs=placed, out_specs=P("ctx", "fsdp"), check_vma=False
    )
```

time: 1110 us -> 41 us (0.04)
  local copies, waits for them, and re-layouts: 977 us -> 4.59 us
  matrix products: 72.7 us -> 0 us
  blocking collectives: 31.4 us -> 0 us
  Pallas kernels: 0 us -> 18.9 us
  other arithmetic: 18.9 us -> 1.74 us
  waiting for transfers between devices: 0.01 us -> 11.3 us
    gather x2 -> x0, local copies, waits for them, and re-layouts: 962 us -> none  [toeplitz(): picked = jnp.take(taps, jnp.clip(lag, 0, count - 1), axis=1)]
    dot_general x3 -> x0, matrix products: 72.7 us -> none  [the longest x1 65.9 us: body(): local = jnp.einsum('gts,ksgj->ktgj', toe, blocks, precision=high)]
    all_gather x1 -> x0, blocking collectives: 31.4 us -> none  [body(): piece = lax.all_gather(fresh, 'ctx', axis=0, tiled=True)]
    pallas_call x0 -> x7, Pallas kernels: none -> 18.9 us  [the longest x3 9.43 us: body(): pl.pallas_call(functools.partial(local_kernel, size, cuts[b]), in_specs=[...]
    ppermute x3 -> x4, waiting for transfers between devices: 0.01 us -> 11.3 us  [the longest x3 8.72 us: body(): got = lax.ppermute(total, 'ctx', [(i, i ^ 1 << b) for i in range(ranks)])]
  transfers between devices with their start and end apart: 3 -> 4, of which waited for: 0 -> 3; matrix products, arithmetic and copies ran while one was open for 95% -> 0% of each run, Pallas kernels for 0% -> 27%
where the time goes in v2:
time: 41 us; the launch traced here: 40.6 us
  Pallas kernels  18.9 us (46%)
  waiting for transfers between devices  11.3 us (28%)
  local copies, waits for them, and re-layouts  4.59 us (11%)
  starting transfers between devices  3.95 us (10%)
  other arithmetic  1.74 us (4%)
    pallas_call x3, Pallas kernels, body(): pl.pallas_call(functools.partial(local_kernel, size, cuts[b]), in_specs=[...  9.43 us
    ppermute x3, waiting for transfers between devices, body(): got = lax.ppermute(total, 'ctx', [(i, i ^ 1 << b) for i in range(ranks)])  8.72 us
    unnamed x26, local copies, waits for them, and re-layouts  4.59 us
    pallas_call x1, Pallas kernels, body(): pl.pallas_call(functools.partial(state_kernel, size), grid=(width // tile...  3.99 us
    ppermute x1, starting transfers between devices, body(): lax.ppermute(rims, 'ctx', [(i, (i + 1) % ranks) for i in range(ranks)])  3.03 us
    ppermute x1, waiting for transfers between devices, body(): lax.ppermute(rims, 'ctx', [(i, (i + 1) % ranks) for i in range(ranks)])  2.56 us
    pallas_call x1, Pallas kernels, body(): pl.pallas_call(functools.partial(mix_kernel, size, phases, len(nears)), i...  2.47 us
    select_n x2, other arithmetic, body(): total = jnp.where(upper, total + span[b] * got, got + span[b] * total)  1.74 us
  transfers between devices with their start and end apart: 4, of which 3 were waited for; matrix products, arithmetic and copies ran while one was open for 0% of the time, Pallas kernels for 27%

profile of v2, /device:TPU:0, one launch (start us, length us, event | category | flops | bytes accessed | tf_op | source)
XLA Modules:
  0.0 40.6 jit_solution(18004419200775672886)
XLA Ops:
  0.0 1.5 %rim.1 = bf16[48,1024]{1,0:T(8,128)(2,1)} custom-call(bf16[512,1024]{1,0:T(8,128)(2,1)} %refs_1_.1, bf16[512,1024]{1,0:T(8,128)(2,1)} %k_ref.3, bf16[512,1024]{1,0:T(8,128)(2,1)} %v_ref.3), custom_call_target="tpu_custom_call" | custom-call | tf_op jit(solution)/shard_map/rim/pallas_call | solution.py:219
  1.6 3.0 %collective-permute-start = (bf16[48,1024]{1,0:T(8,128)(2,1)}, bf16[48,1024]{1,0:T(8,128)(2,1)S(1)}, u32[]{:S(2)}, u32[]{:S(2)}) collective-permute-start(bf16[48,1024]{1,0:T(8,128)(2,1)} %rim.1), channel_id=1, source_target_pairs={{0,4},{4,8},{8,12},{12,16},{16,20},{20,24},{24,28},{28,0},{1,5},{5... | collective-permute-start | bytes 294920 | tf_op jit(solution)/shard_map/ppermute | solution.py:228
  4.6 1.5 %tables.1 = (bf16[512,1024]{1,0:T(8,128)(2,1)S(1)}, bf16[512,1024]{1,0:T(8,128)(2,1)S(1)}, bf16[1024,512]{1,0:T(8,128)(2,1)S(1)}, bf16[1024,512]{1,0:T(8,128)(2,...) custom-call(f32[16,64]{1,0:T(8,128)S(1)} %copy-done.9, f32[16,64]{1,0:T(8,128)S(1)} %copy-done.12), custom_call_target="tpu_custom_call" | custom-call | flops 10000000 | bytes 5242880 | tf_op jit(solution)/shard_map/tables/pallas_call | solution.py:234
  6.1 0.0 copy-start.3
  6.1 1.0 %copy-done.3 = bf16[512,1024]{1,0:T(8,128)(2,1)} copy-done((bf16[512,1024]{1,0:T(8,128)(2,1)}, bf16[512,1024]{1,0:T(8,128)(2,1)S(1)}, u32[]{:S(2)}) %copy-start.3) | copy-done | bytes 1048600
  7.1 1.0 %copy-done.5 = bf16[512,1024]{1,0:T(8,128)(2,1)} copy-done((bf16[512,1024]{1,0:T(8,128)(2,1)}, bf16[512,1024]{1,0:T(8,128)(2,1)S(1)}, u32[]{:S(2)}) %copy-start.5) | copy-done | bytes 1048600
  8.1 2.6 %collective-permute-done.halo_ref.refs_0_ = bf16[48,1024]{1,0:T(8,128)(2,1)S(1)} collective-permute-done((bf16[48,1024]{1,0:T(8,128)(2,1)}, bf16[48,1024]{1,0:T(8,128)(2,1)S(1)}, u32[]{:S(2)}, u32[]{:S(2)}) %collective-permute-start) | collective-permute-done | bytes 98336 | tf_op jit(solution)/shard_map/ppermute | solution.py:228
  10.6 1.2 %copy-done.1 = bf16[512,1024]{1,0:T(8,128)(2,1)S(1)} copy-done((bf16[512,1024]{1,0:T(8,128)(2,1)S(1)}, bf16[512,1024]{1,0:T(8,128)(2,1)}, u32[]{:S(2)}) %copy-start.1) | copy-done | bytes 1048600
  11.9 4.0 %state.1 = (f32[512,1024]{1,0:T(8,128)S(1)}, f32[16,1024]{1,0:T(8,128)}) custom-call(bf16[48,1024]{1,0:T(8,128)(2,1)S(1)} %collective-permute-done.halo_ref.refs_0_, bf16[512,1024]{1,0:T(8,128)(2,1)S(1)} %copy-done, bf16[512,1024]{1,0:T(8,128)(2,1)S(1)} %copy-done.1, f32[3,3,1024]{2,1,0:T(4,128)S(1)} %copy-done.7, ...), custom_call_target="tpu_custom_call" | custom-call | tf_op jit(solution)/shard_map/state/pallas_call | solution.py:246
  15.9 0.0 collective-permute-start.1
  15.9 4.5 %collective-permute-done.1.refs_6_ = f32[16,1024]{1,0:T(8,128)S(1)} collective-permute-done((f32[16,1024]{1,0:T(8,128)}, f32[16,1024]{1,0:T(8,128)S(1)}, u32[]{:S(2)}, u32[]{:S(2)}) %collective-permute-start.1) | collective-permute-done | bytes 65568 | tf_op jit(solution)/shard_map/ppermute | solution.py:273
  20.3 0.9 %fusion.4 = f32[16,1024]{1,0:T(8,128)S(1)} fusion(f32[16,1024]{1,0:T(8,128)} %get-tuple-element.19, f32[16,1024]{1,0:T(8,128)S(1)} %collective-permute-done.1.refs_6_, f32[3,16,1024]{2,1,0:T(8,128)} %copy-done.8, pred[]{:T(512)S(6)} %eq.9), kind=kLoop, calls=%fused_computation.8 | loop fusion | flops 81920 | bytes 262145 | tf_op jit(solution)/shard_map/jit(_where)/select_n | solution.py:290
  21.2 0.1 collective-permute-start.2
  21.3 4.2 %collective-permute-done.2.refs_7_ = f32[16,1024]{1,0:T(8,128)S(1)} collective-permute-done((f32[16,1024]{1,0:T(8,128)S(1)}, f32[16,1024]{1,0:T(8,128)S(1)}, u32[]{:S(2)}, u32[]{:S(2)}) %collective-permute-start.2) | collective-permute-done | bytes 65568 | tf_op jit(solution)/shard_map/ppermute | solution.py:273
  25.6 0.9 %fusion.1 = f32[16,1024]{1,0:T(8,128)S(1)} fusion(f32[16,1024]{1,0:T(8,128)S(1)} %fusion.4, f32[16,1024]{1,0:T(8,128)S(1)} %collective-permute-done.2.refs_7_, f32[3,16,1024]{2,1,0:T(8,128)} %copy-done.8, pred[]{:T(512)S(6)} %eq.10), kind=kLoop, calls=%fused_computation.3 | loop fusion | flops 81920 | bytes 262145 | tf_op jit(solution)/shard_map/jit(_where)/select_n | solution.py:290
  26.4 0.8 %collective-permute-start.3 = (f32[16,1024]{1,0:T(8,128)S(1)}, f32[16,1024]{1,0:T(8,128)S(1)}, u32[]{:S(2)}, u32[]{:S(2)}) collective-permute-start(f32[16,1024]{1,0:T(8,128)S(1)} %fusion.1), channel_id=1, source_target_pairs={{0,16},{4,20},{8,24},{12,28},{16,0},{20,4},{24,8},{28,12},{1,17},{... | collective-permute-start | bytes 196616 | tf_op jit(solution)/shard_map/ppermute | solution.py:273
  27.3 0.7 %copy-done.10 = f32[16,64]{1,0:T(8,128)S(1)} copy-done((f32[16,64]{1,0:T(8,128)S(1)}, f32[16,64]{1,0:T(8,128)}, u32[]{:S(2)}) %copy-start.10) | copy-done | bytes 4120
  28.0 0.7 %copy-done.11 = f32[1,1024]{1,0:T(1,128)S(1)} copy-done((f32[1,1024]{1,0:T(1,128)S(1)}, f32[1,1024]{1,0:T(1,128)}, u32[]{:S(2)}) %copy-start.11) | copy-done | bytes 4120
  28.6 2.6 %near.3.refs_9_ = f32[512,256]{1,0:T(8,128)S(1)} custom-call(f32[512,1024]{1,0:T(8,128)S(1)} %get-tuple-element.21.gated_ref, f32[16,1024]{1,0:T(8,128)S(1)} %get-tuple-element.22.spread_ref, f32[16,64]{1,0:T(8,128)S(1)} %copy-done.10, f32[1,1024]{1,0:T(1,128)S(1)} %copy-done.11), custom_call_target="tpu_custom_call" | custom-call | flops 10000000 | bytes 4194304 | tf_op jit(solution)/shard_map/near/pallas_call | solution.py:278
  31.3 3.4 %near.4.refs_10_ = f32[512,384]{1,0:T(8,128)S(1)} custom-call(f32[512,1024]{1,0:T(8,128)S(1)} %get-tuple-element.21.gated_ref, f32[16,1024]{1,0:T(8,128)S(1)} %get-tuple-element.22.spread_ref, f32[16,64]{1,0:T(8,128)S(1)} %copy-done.10, f32[1,1024]{1,0:T(1,128)S(1)} %copy-done.11), custom_call_target="tpu_custom_call" | custom-call | flops 10000000 | bytes 4194304 | tf_op jit(solution)/shard_map/near/pallas_call | solution.py:278
  34.7 0.0 copy-start.2
  34.7 0.0 copy-start.4
  34.7 3.4 %near.5.refs_11_ = f32[512,384]{1,0:T(8,128)S(1)} custom-call(f32[512,1024]{1,0:T(8,128)S(1)} %get-tuple-element.21.gated_ref, f32[16,1024]{1,0:T(8,128)S(1)} %get-tuple-element.22.spread_ref, f32[16,64]{1,0:T(8,128)S(1)} %copy-done.10, f32[1,1024]{1,0:T(1,128)S(1)} %copy-done.11), custom_call_target="tpu_custom_call" | custom-call | flops 10000000 | bytes 4194304 | tf_op jit(solution)/shard_map/near/pallas_call | solution.py:278
  38.2 2.5 %mix.1 = bf16[512,1024]{1,0:T(8,128)(2,1)} custom-call(bf16[48,1024]{1,0:T(8,128)(2,1)S(1)} %collective-permute-done.halo_ref.refs_0_, bf16[512,1024]{1,0:T(8,128)(2,1)S(1)} %copy-done.2, f32[3,3,1024]{2,1,0:T(4,128)S(1)} %copy-done.7, f32[3,16,1024]{2,1,0:T(8,128)S(1)} %get-tuple-element.14.refs_3_, bf16[512,1024]{1,0:T(8,128)(2,1)S(1)} %copy-done.4, ...), custom_call_target="tpu_custom_call" | custom-call | tf_op jit(solution)/shard_map/mix/pallas_call | solution.py:292
  (19 shorter events, 0.0 us)
Async XLA Ops:
  0.0 10.6 %copy-start = (bf16[512,1024]{1,0:T(8,128)(2,1)S(1)}, bf16[512,1024]{1,0:T(8,128)(2,1)}, u32[]{:S(2)}) copy-start(bf16[512,1024]{1,0:T(8,128)(2,1)} %k_ref.3) | copy-start | bytes 3145732
  0.0 4.6 %copy-start.9 = (f32[16,64]{1,0:T(8,128)S(1)}, f32[16,64]{1,0:T(8,128)}, u32[]{:S(2)}) copy-start(f32[16,64]{1,0:T(8,128)} %res_ref.7) | copy-start | bytes 12292
  0.0 4.6 %copy-start.12 = (f32[16,64]{1,0:T(8,128)S(1)}, f32[16,64]{1,0:T(8,128)}, u32[]{:S(2)}) copy-start(f32[16,64]{1,0:T(8,128)} %decay_ref.1) | copy-start | bytes 12292
  0.0 10.6 %copy-start.7 = (f32[3,3,1024]{2,1,0:T(4,128)S(1)}, f32[3,3,1024]{2,1,0:T(4,128)}, u32[]{:S(2)}) copy-start(f32[3,3,1024]{2,1,0:T(4,128)} %refs_2_.1) | copy-start | bytes 110596
  1.6 9.1 %collective-permute-start = (bf16[48,1024]{1,0:T(8,128)(2,1)}, bf16[48,1024]{1,0:T(8,128)(2,1)S(1)}, u32[]{:S(2)}, u32[]{:S(2)}) collective-permute-start(bf16[48,1024]{1,0:T(8,128)(2,1)} %rim.1), channel_id=1, source_target_pairs={{0,4},{4,8},{8,12},{12,16},{16,20},{20,24},{24,28},{28,0},{1,5},{5... | collective-permute-start | bytes 294920 | tf_op jit(solution)/shard_map/ppermute | solution.py:228
  6.1 1.0 %copy-start.3 = (bf16[512,1024]{1,0:T(8,128)(2,1)}, bf16[512,1024]{1,0:T(8,128)(2,1)S(1)}, u32[]{:S(2)}) copy-start(bf16[512,1024]{1,0:T(8,128)(2,1)S(1)} %get-tuple-element.15.refs_4_) | copy-start | bytes 3145732
  7.1 1.0 %copy-start.5 = (bf16[512,1024]{1,0:T(8,128)(2,1)}, bf16[512,1024]{1,0:T(8,128)(2,1)S(1)}, u32[]{:S(2)}) copy-start(bf16[512,1024]{1,0:T(8,128)(2,1)S(1)} %get-tuple-element.16.refs_5_) | copy-start | bytes 3145732
  8.1 7.8 %copy-start.8 = (f32[3,16,1024]{2,1,0:T(8,128)}, f32[3,16,1024]{2,1,0:T(8,128)S(1)}, u32[]{:S(2)}) copy-start(f32[3,16,1024]{2,1,0:T(8,128)S(1)} %get-tuple-element.20) | copy-start | bytes 589828
  10.6 1.2 %copy-start.1 = (bf16[512,1024]{1,0:T(8,128)(2,1)S(1)}, bf16[512,1024]{1,0:T(8,128)(2,1)}, u32[]{:S(2)}) copy-start(bf16[512,1024]{1,0:T(8,128)(2,1)} %v_ref.3) | copy-start | bytes 3145732
  15.9 4.5 %collective-permute-start.1 = (f32[16,1024]{1,0:T(8,128)}, f32[16,1024]{1,0:T(8,128)S(1)}, u32[]{:S(2)}, u32[]{:S(2)}) collective-permute-start(f32[16,1024]{1,0:T(8,128)} %get-tuple-element.19), channel_id=1, source_target_pairs={{0,4},{4,0},{8,12},{12,8},{16,20},{20,16},{24,28},{28,24},{1,5},{5... | collective-permute-start | bytes 196616 | tf_op jit(solution)/shard_map/ppermute | solution.py:273
  21.2 4.3 %collective-permute-start.2 = (f32[16,1024]{1,0:T(8,128)S(1)}, f32[16,1024]{1,0:T(8,128)S(1)}, u32[]{:S(2)}, u32[]{:S(2)}) collective-permute-start(f32[16,1024]{1,0:T(8,128)S(1)} %fusion.4), channel_id=1, source_target_pairs={{0,8},{4,12},{8,0},{12,4},{16,24},{20,28},{24,16},{28,20},{1,9},{5... | collective-permute-start | bytes 196616 | tf_op jit(solution)/shard_map/ppermute | solution.py:273
  26.4 11.7 %collective-permute-start.3 = (f32[16,1024]{1,0:T(8,128)S(1)}, f32[16,1024]{1,0:T(8,128)S(1)}, u32[]{:S(2)}, u32[]{:S(2)}) collective-permute-start(f32[16,1024]{1,0:T(8,128)S(1)} %fusion.1), channel_id=1, source_target_pairs={{0,16},{4,20},{8,24},{12,28},{16,0},{20,4},{24,8},{28,12},{1,17},{... | collective-permute-start | bytes 196616 | tf_op jit(solution)/shard_map/ppermute | solution.py:273
  27.3 0.7 %copy-start.10 = (f32[16,64]{1,0:T(8,128)S(1)}, f32[16,64]{1,0:T(8,128)}, u32[]{:S(2)}) copy-start(f32[16,64]{1,0:T(8,128)} %res_ref.7) | copy-start | bytes 12292
  28.0 0.7 %copy-start.11 = (f32[1,1024]{1,0:T(1,128)S(1)}, f32[1,1024]{1,0:T(1,128)}, u32[]{:S(2)}) copy-start(f32[1,1024]{1,0:T(1,128)} %skip_ref.5) | copy-start | bytes 12292
  31.2 6.9 %copy-start.6 = (bf16[512,1024]{1,0:T(8,128)(2,1)S(1)}, bf16[512,1024]{1,0:T(8,128)(2,1)}, u32[]{:S(2)}) copy-start(bf16[512,1024]{1,0:T(8,128)(2,1)} %copy-done.5) | copy-start | bytes 3145732
  34.7 3.5 %copy-start.2 = (bf16[512,1024]{1,0:T(8,128)(2,1)S(1)}, bf16[512,1024]{1,0:T(8,128)(2,1)}, u32[]{:S(2)}) copy-start(bf16[512,1024]{1,0:T(8,128)(2,1)} %refs_1_.1) | copy-start | bytes 3145732
  34.7 3.5 %copy-start.4 = (bf16[512,1024]{1,0:T(8,128)(2,1)S(1)}, bf16[512,1024]{1,0:T(8,128)(2,1)}, u32[]{:S(2)}) copy-start(bf16[512,1024]{1,0:T(8,128)(2,1)} %copy-done.3) | copy-start | bytes 3145732

commit v3 on v2

--- a/solution.py
+++ b/solution.py
@@ -60,10 +60,11 @@
         copy.wait()
 
 
-def table_kernel(res_ref, decay_ref, lead_hi, lead_lo, tail_hi, tail_lo, spread_ref, span_ref, reach_ref):
+def table_kernel(res_ref, decay_ref, skip_ref, lead_hi, lead_lo, tail_hi, tail_lo, ratio_ref, gain_ref, plain_ref, seam_ref, span_ref, reach_ref):
     length, width = lead_hi.shape
     modes = decay_ref.shape[0]
-    phases = span_ref.shape[0]
+    phases = reach_ref.shape[0]
+    plain_ref[...] = skip_ref[...]
     me = lax.axis_index("ctx")
     lane = lax.broadcasted_iota(jnp.int32, (modes, LANES), 1)
     own = lane % modes == lax.broadcasted_iota(jnp.int32, (modes, LANES), 0)
@@ -75,11 +76,15 @@
         gains = expand(res_ref[...], tile * (LANES // modes), LANES, modes) * norm_of(rates)
         rate = jnp.sum(jnp.where(own, rates, 0.0), axis=0, keepdims=True)
         gain = jnp.sum(jnp.where(own, gains, 0.0), axis=0, keepdims=True)
-        spread_ref[:, at] = rates
+        ratio_ref[:, at] = jnp.exp(-rates)
+        gain_ref[:, at] = gains
+        for i in range(2):
+            seam_ref[i, :, at] = jnp.exp(-rates * (length - 1.0 - i))
         for b in range(phases):
             upper = jnp.where((me >> b) % 2 == 1, 1.0, 0.0).astype(F32)
             gap = (me % (1 << b) * length).astype(F32)
-            span_ref[b, :, at] = jnp.exp(-rates * float(length << b))
+            if b + 1 < phases:
+                span_ref[b, :, at] = jnp.exp(-rates * float(length << b))
             reach_ref[b, :, at] = jnp.exp(-rates * gap) * upper
         lead = gain * jnp.exp(-rate * (down + 1.0))
         hop = jnp.exp(-rate * float(LANES))
@@ -97,25 +102,27 @@
             tail = tail * hop_rows
 
 
-def state_kernel(size, halo_ref, k_ref, v_ref, sf_ref, tail_hi, tail_lo, gated_ref, fresh_ref, kf, vf, xh, xl):
+def state_kernel(size, k_ref, v_ref, sf_ref, tail_hi, tail_lo, gated_ref, fresh_ref, kf, vf, xh, xl):
     length, lanes = k_ref.shape
     modes = fresh_ref.shape[0]
     tile = pl.program_id(0)
-    keep = jnp.where(lax.axis_index("ctx") > 0, 1.0, 0.0).astype(F32)
     row = lax.broadcasted_iota(jnp.int32, (modes, LANES), 1) // size
+    piece = 64
+    inner = lax.broadcasted_iota(jnp.int32, (piece, LANES), 0) >= 2
+    kf[0:SUB] = jnp.zeros((SUB, LANES), F32)
+    vf[0:SUB] = jnp.zeros((SUB, LANES), F32)
     for part in range(lanes // LANES):
         at = slice(part * LANES, (part + 1) * LANES)
         base = pl.multiple_of(tile * lanes + part * LANES, LANES)
-        kf[0:SUB] = halo_ref[RIM : 2 * RIM, at].astype(F32)[SUB:] * keep
-        vf[0:SUB] = halo_ref[2 * RIM : 3 * RIM, at].astype(F32)[SUB:] * keep
         kt = [sf_ref[1, i : i + 1, at] for i in range(3)]
         vt = [sf_ref[2, i : i + 1, at] for i in range(3)]
-        piece = 64
         for start in range(0, length, piece):
             rows = slice(start, start + piece)
             kf[SUB + start : SUB + start + piece] = k_ref[rows, at].astype(F32)
             vf[SUB + start : SUB + start + piece] = v_ref[rows, at].astype(F32)
             gated = short3(kf, start, piece, kt) * short3(vf, start, piece, vt)
+            if start == 0:
+                gated = jnp.where(inner, gated, 0.0)
             gated_ref[rows, pl.ds(base, LANES)] = gated
             xh[rows], xl[rows] = split2(gated)
         table = pl.ds(base, LANES)
@@ -128,6 +135,27 @@
         fresh_ref[:, pl.ds(base, LANES)] = total
 
 
+def seam_kernel(halo_ref, k_ref, v_ref, sf_ref, seam_ref, fresh_ref, gated_ref, out_ref, whole_ref, kf, vf):
+    keep = jnp.where(lax.axis_index("ctx") > 0, 1.0, 0.0).astype(F32)
+    kf[0:SUB] = halo_ref[RIM : 2 * RIM].astype(F32)[SUB:] * keep
+    vf[0:SUB] = halo_ref[2 * RIM : 3 * RIM].astype(F32)[SUB:] * keep
+    kf[SUB:] = k_ref[0:RIM].astype(F32)[:SUB]
+    vf[SUB:] = v_ref[0:RIM].astype(F32)[:SUB]
+    kt = [sf_ref[1, i : i + 1, :] for i in range(3)]
+    vt = [sf_ref[2, i : i + 1, :] for i in range(3)]
+    head = short3(kf, 0, SUB, kt) * short3(vf, 0, SUB, vt)
+    whole_ref[0:SUB] = head
+    out_ref[...] = fresh_ref[...] + seam_ref[0] * head[0:1] + seam_ref[1] * head[1:2]
+
+
+def merge_kernel(b, total_ref, got_ref, span_ref, out_ref):
+    upper = (lax.axis_index("ctx") >> b) % 2 == 1
+    total, got = total_ref[...], got_ref[...]
+    late = jnp.where(upper, total, got)
+    early = jnp.where(upper, got, total)
+    out_ref[...] = late + span_ref[b] * early
+
+
 def fold8(parts):
     sub = lax.broadcasted_iota(jnp.int32, parts[0].shape, 0)
 
@@ -140,14 +168,13 @@
     return join(parts[0], parts[1], 1)
 
 
-def local_kernel(size, first, gated_ref, spread_ref, res_ref, skip_ref, out_ref):
+def local_kernel(first, gated_ref, ratio_ref, gain_ref, plain_ref, out_ref):
     length, lanes = out_ref.shape
-    modes = res_ref.shape[0]
+    modes = ratio_ref.shape[0]
     at = slice(first, first + lanes)
-    rate = spread_ref[:, at]
-    weight = expand(res_ref[...], first // size, lanes, size) * norm_of(rate)
-    ratio = jnp.exp(-rate)
-    skip = skip_ref[:, at]
+    ratio = ratio_ref[:, at]
+    weight = gain_ref[:, at]
+    skip = plain_ref[:, at]
 
     def step(i, state):
         base = pl.multiple_of(i * SUB, SUB)
@@ -222,24 +249,27 @@
         out_specs=VMEM,
         out_shape=jax.ShapeDtypeStruct((3 * RIM, width), BF16),
         scratch_shapes=[pltpu.SemaphoreType.DMA((3,))],
-        compiler_params=pltpu.CompilerParams(vmem_limit_bytes=60 << 20),
+        compiler_params=pltpu.CompilerParams(vmem_limit_bytes=4 << 20),
         name="rim",
-    )(query_in, key_in, value_in)
+    )(*[pltpu.with_memory_space_constraint(a, pltpu.HBM) for a in (query_in, key_in, value_in)])
     halo = lax.ppermute(rims, "ctx", [(i, (i + 1) % ranks) for i in range(ranks)])
 
     lead_shape = jax.ShapeDtypeStruct((length, width), BF16)
     tail_shape = jax.ShapeDtypeStruct((width, length), BF16)
-    scan_shape = jax.ShapeDtypeStruct((phases, modes, width), F32)
+    scan_shape = lambda count: jax.ShapeDtypeStruct((count, modes, width), F32)
     row_shape = jax.ShapeDtypeStruct((modes, width), F32)
-    lead_hi, lead_lo, tail_hi, tail_lo, spread, span, reach = pl.pallas_call(
+    lead_hi, lead_lo, tail_hi, tail_lo, ratio, gain, plain, seam, span, reach = pl.pallas_call(
         table_kernel,
-        in_specs=[VMEM] * 2,
-        out_specs=[VMEM] * 7,
-        out_shape=[lead_shape, lead_shape, tail_shape, tail_shape, row_shape, scan_shape, scan_shape],
+        in_specs=[VMEM] * 3,
+        out_specs=[VMEM] * 10,
+        out_shape=[lead_shape] * 2
+        + [tail_shape] * 2
+        + [row_shape] * 2
+        + [jax.ShapeDtypeStruct((1, width), F32), scan_shape(2), scan_shape(max(1, phases - 1)), scan_shape(phases)],
         compiler_params=PARAMS,
         cost_estimate=pl.CostEstimate(flops=10**7, bytes_accessed=5 << 20, transcendentals=0),
         name="tables",
-    )(residues, decay_rate)
+    )(residues, decay_rate, skip_gain)
 
     tile = min(width, WIDE)
     cols = lambda rows: pl.BlockSpec((rows, tile), lambda j: (0, j))
@@ -247,7 +277,6 @@
         functools.partial(state_kernel, size),
         grid=(width // tile,),
         in_specs=[
-            cols(3 * RIM),
             cols(length),
             cols(length),
             pl.BlockSpec((3, 3, tile), lambda j: (0, 0, j)),
@@ -263,8 +292,19 @@
             pltpu.VMEM((length, LANES), BF16),
         ],
         compiler_params=PARAMS,
+        cost_estimate=pl.CostEstimate(flops=10**7, bytes_accessed=5 << 20, transcendentals=0),
         name="state",
-    )(halo, key_in, value_in, short_filter, tail_hi, tail_lo)
+    )(key_in, value_in, short_filter, tail_hi, tail_lo)
+    fresh, gated = pl.pallas_call(
+        seam_kernel,
+        in_specs=[VMEM] * 7,
+        out_specs=[VMEM] * 2,
+        out_shape=[row_shape, jax.ShapeDtypeStruct((length, width), F32)],
+        input_output_aliases={6: 1},
+        scratch_shapes=[pltpu.VMEM((2 * SUB, width), F32)] * 2,
+        compiler_params=PARAMS,
+        name="seam",
+    )(halo, key_in, value_in, short_filter, seam, fresh, gated)
 
     unit = LANES if width // LANES >= 2 * phases else min(width, WIDE)
     cuts = [width // unit * b // phases * unit for b in range(phases + 1)]
@@ -276,18 +316,24 @@
         if lanes:
             nears.append(
                 pl.pallas_call(
-                    functools.partial(local_kernel, size, cuts[b]),
+                    functools.partial(local_kernel, cuts[b]),
                     in_specs=[VMEM] * 4,
                     out_specs=VMEM,
                     out_shape=jax.ShapeDtypeStruct((length, lanes), F32),
                     compiler_params=PARAMS,
                     cost_estimate=pl.CostEstimate(flops=10**7, bytes_accessed=4 << 20, transcendentals=0),
                     name="near",
-                )(gated, spread, residues, skip_gain)
+                )(gated, ratio, gain, plain)
             )
         if b + 1 < phases:
-            upper = (lax.axis_index("ctx") >> b) % 2 == 1
-            total = jnp.where(upper, total + span[b] * got, got + span[b] * total)
+            total = pl.pallas_call(
+                functools.partial(merge_kernel, b),
+                in_specs=[VMEM] * 3,
+                out_specs=VMEM,
+                out_shape=row_shape,
+                compiler_params=PARAMS,
+                name="merge",
+            )(total, got, span)
 
     return pl.pallas_call(
         functools.partial(mix_kernel, size, phases, len(nears)),

time: 41 us -> 32.6 us (0.80)
  local copies, waits for them, and re-layouts: 4.59 us -> 0.03 us
  waiting for transfers between devices: 11.3 us -> 7.68 us
  starting transfers between devices: 3.95 us -> 6.86 us
  other arithmetic: 1.74 us -> 0 us
  Pallas kernels: 18.9 us -> 17.7 us
    unnamed x26 -> x14, local copies, waits for them, and re-layouts: 4.59 us -> 0.03 us
    ppermute x3, starting transfers between devices: 0.92 us -> 3.83 us  [body(): got = lax.ppermute(total, 'ctx', [(i, i ^ 1 << b) for i in range(ranks)])]
    ppermute x3, waiting for transfers between devices: 8.72 us -> 6.91 us  [body(): got = lax.ppermute(total, 'ctx', [(i, i ^ 1 << b) for i in range(ranks)])]
    ppermute x1, waiting for transfers between devices: 2.56 us -> 0.77 us  [body(): lax.ppermute(rims, 'ctx', [(i, (i + 1) % ranks) for i in range(ranks)])]
    select_n x2 -> x0, other arithmetic: 1.74 us -> none  [body(): total = jnp.where(upper, total + span[b] * got, got + span[b] * total)]
    pallas_call x1, Pallas kernels: 1.54 us -> 0.96 us  [body(): pl.pallas_call(rim_kernel, in_specs=[pl.BlockSpec(memory_space=pltpu.HBM)...]
    pallas_call x1, Pallas kernels: 3.99 us -> 3.49 us  [body(): pl.pallas_call(functools.partial(state_kernel, size), grid=(width // tile...]
    pallas_call x4 -> x7, Pallas kernels: 10.9 us -> 10.8 us  [the longest x3 9.17 us: body(): pl.pallas_call(functools.partial(local_kernel, cuts[b]), in_specs=[VMEM]...]
  transfers between devices with their start and end apart: 4 -> 4, of which waited for: 3 -> 3; matrix products, arithmetic and copies ran while one was open for 0% -> 0% of each run, Pallas kernels for 27% -> 44%
where the time goes in v3:
time: 32.6 us; the launch traced here: 32.4 us
  Pallas kernels  17.7 us (54%)
  waiting for transfers between devices  7.68 us (24%)
  starting transfers between devices  6.86 us (21%)
    pallas_call x3, Pallas kernels, body(): pl.pallas_call(functools.partial(local_kernel, cuts[b]), in_specs=[VMEM]...  9.17 us
    ppermute x3, waiting for transfers between devices, body(): got = lax.ppermute(total, 'ctx', [(i, i ^ 1 << b) for i in range(ranks)])  6.91 us
    ppermute x3, starting transfers between devices, body(): got = lax.ppermute(total, 'ctx', [(i, i ^ 1 << b) for i in range(ranks)])  3.83 us
    pallas_call x1, Pallas kernels, body(): pl.pallas_call(functools.partial(state_kernel, size), grid=(width // tile...  3.49 us
    ppermute x1, starting transfers between devices, body(): lax.ppermute(rims, 'ctx', [(i, (i + 1) % ranks) for i in range(ranks)])  3.03 us
    pallas_call x1, Pallas kernels, body(): pl.pallas_call(functools.partial(mix_kernel, size, phases, len(nears)), i...  2.49 us
    pallas_call x1, Pallas kernels, body(): pl.pallas_call(table_kernel, in_specs=[VMEM] * 3, out_specs=[VMEM] * 10,...  1.53 us
    pallas_call x1, Pallas kernels, body(): pl.pallas_call(rim_kernel, in_specs=[pl.BlockSpec(memory_space=pltpu.HBM)...  0.96 us
  transfers between devices with their start and end apart: 4, of which 3 were waited for; matrix products, arithmetic and copies ran while one was open for 0% of the time, Pallas kernels for 44%

profile of v3, /device:TPU:0, one launch (start us, length us, event | category | flops | bytes accessed | tf_op | source)
XLA Modules:
  0.0 32.4 jit_solution(16354560797513710798)
XLA Ops:
  0.0 0.0 copy-start.3
  0.0 1.0 %rim.1 = bf16[48,1024]{1,0:T(8,128)(2,1)S(1)} custom-call(bf16[512,1024]{1,0:T(8,128)(2,1)} %refs_1_.1, bf16[512,1024]{1,0:T(8,128)(2,1)} %k_ref.5, bf16[512,1024]{1,0:T(8,128)(2,1)} %v_ref.5), custom_call_target="tpu_custom_call" | custom-call | tf_op jit(solution)/shard_map/rim/pallas_call | solution.py:246
  1.0 3.0 %collective-permute-start = (bf16[48,1024]{1,0:T(8,128)(2,1)S(1)}, bf16[48,1024]{1,0:T(8,128)(2,1)S(1)}, u32[]{:S(2)}, u32[]{:S(2)}) collective-permute-start(bf16[48,1024]{1,0:T(8,128)(2,1)S(1)} %rim.1), channel_id=1, source_target_pairs={{0,4},{4,8},{8,12},{12,16},{16,20},{20,24},{24,28},{28,0},{1,5},{5... | collective-permute-start | bytes 294920 | tf_op jit(solution)/shard_map/ppermute | solution.py:255
  4.0 0.0 copy-done.6
  4.0 0.0 copy-done.5
  4.0 0.0 copy-done.4
  4.0 1.5 %tables.1 = (bf16[512,1024]{1,0:T(8,128)(2,1)S(1)}, bf16[512,1024]{1,0:T(8,128)(2,1)S(1)}, bf16[1024,512]{1,0:T(8,128)(2,1)S(1)}, bf16[1024,512]{1,0:T(8,128)(2,...) custom-call(f32[16,64]{1,0:T(8,128)S(1)} %copy-done.4, ...), custom_call_target="tpu_custom_call" | custom-call | flops 10000000 | bytes 5242880 | tf_op jit(solution)/shard_map/tables/pallas_call | solution.py:261
  5.6 0.0 copy-done.1
  5.6 0.0 copy-done
  5.6 0.0 copy-done.3
  5.6 3.5 %state.1 = (f32[512,1024]{1,0:T(8,128)S(1)}, f32[16,1024]{1,0:T(8,128)S(1)}) custom-call(bf16[512,1024]{1,0:T(8,128)(2,1)S(1)} %copy-done, bf16[512,1024]{1,0:T(8,128)(2,1)S(1)} %copy-done.1, f32[3,3,1024]{2,1,0:T(4,128)S(1)} %copy-done.3, bf16[1024,512]{1,0:T(8,128)(2,1)S(1)} %get-tuple-element.23.tail_hi, bf16[1024,512]{1,0:T(8,128)(2,1)S(1)} %get-tuple-element.24.tail_lo), custom_call_target="tpu_custom_call" | custom-call | flops 10000000 | bytes 5242880 | tf_op jit(solution)/shard_map/state/pallas_call | solution.py:276
  9.1 0.8 %collective-permute-done.halo_ref.refs_0_ = bf16[48,1024]{1,0:T(8,128)(2,1)S(1)} collective-permute-done((bf16[48,1024]{1,0:T(8,128)(2,1)S(1)}, bf16[48,1024]{1,0:T(8,128)(2,1)S(1)}, u32[]{:S(2)}, u32[]{:S(2)}) %collective-permute-start) | collective-permute-done | bytes 98336 | tf_op jit(solution)/shard_map/ppermute | solution.py:255
  9.9 0.1 seam.1
  9.9 0.9 %collective-permute-start.1 = (f32[16,1024]{1,0:T(8,128)S(1)}, f32[16,1024]{1,0:T(8,128)S(1)}, u32[]{:S(2)}, u32[]{:S(2)}) collective-permute-start(f32[16,1024]{1,0:T(8,128)S(1)} %get-tuple-element.27.total_ref), channel_id=1, source_target_pairs={{0,4},{4,0},{8,12},{12,8},{16,20},{20,16},{24,28},{28,24},{1,5},{5... | collective-permute-start | bytes 196616 | tf_op jit(solution)/shard_map/ppermute | solution.py:313
  10.8 3.5 %collective-permute-done.1.got_ref.refs_6_ = f32[16,1024]{1,0:T(8,128)S(1)} collective-permute-done((f32[16,1024]{1,0:T(8,128)S(1)}, f32[16,1024]{1,0:T(8,128)S(1)}, u32[]{:S(2)}, u32[]{:S(2)}) %collective-permute-start.1) | collective-permute-done | bytes 65568 | tf_op jit(solution)/shard_map/ppermute | solution.py:313
  14.3 0.9 %collective-permute-start.2 = (f32[16,1024]{1,0:T(8,128)S(1)}, f32[16,1024]{1,0:T(8,128)S(1)}, u32[]{:S(2)}, u32[]{:S(2)}) collective-permute-start(f32[16,1024]{1,0:T(8,128)S(1)} %merge.2.total_ref), channel_id=1, source_target_pairs={{0,8},{4,12},{8,0},{12,4},{16,24},{20,28},{24,16},{28,20},{1,9},{5... | collective-permute-start | bytes 196616 | tf_op jit(solution)/shard_map/ppermute | solution.py:313
  15.2 3.4 %collective-permute-done.2.got_ref.refs_7_ = f32[16,1024]{1,0:T(8,128)S(1)} collective-permute-done((f32[16,1024]{1,0:T(8,128)S(1)}, f32[16,1024]{1,0:T(8,128)S(1)}, u32[]{:S(2)}, u32[]{:S(2)}) %collective-permute-start.2) | collective-permute-done | bytes 65568 | tf_op jit(solution)/shard_map/ppermute | solution.py:313
  18.6 2.1 %collective-permute-start.3 = (f32[16,1024]{1,0:T(8,128)S(1)}, f32[16,1024]{1,0:T(8,128)S(1)}, u32[]{:S(2)}, u32[]{:S(2)}) collective-permute-start(f32[16,1024]{1,0:T(8,128)S(1)} %merge.3), channel_id=1, source_target_pairs={{0,16},{4,20},{8,24},{12,28},{16,0},{20,4},{24,8},{28,12},{1,17},{... | collective-permute-start | bytes 196616 | tf_op jit(solution)/shard_map/ppermute | solution.py:313
  20.7 2.5 %near.3.refs_9_ = f32[512,256]{1,0:T(8,128)S(1)} custom-call(f32[512,1024]{1,0:T(8,128)S(1)} %get-tuple-element.29.gated_ref, f32[16,1024]{1,0:T(8,128)S(1)} %get-tuple-element.30.ratio_ref, f32[16,1024]{1,0:T(8,128)S(1)} %get-tuple-element.31.gain_ref, f32[1,1024]{1,0:T(1,128)S(1)} %get-tuple-element.32.plain_ref), custom_call_target="tpu_custom_call" | custom-call | flops 10000000 | bytes 4194304 | tf_op jit(solution)/shard_map/near/pallas_call | solution.py:318
  23.2 3.3 %near.5.refs_11_ = f32[512,384]{1,0:T(8,128)S(1)} custom-call(f32[512,1024]{1,0:T(8,128)S(1)} %get-tuple-element.29.gated_ref, f32[16,1024]{1,0:T(8,128)S(1)} %get-tuple-element.30.ratio_ref, f32[16,1024]{1,0:T(8,128)S(1)} %get-tuple-element.31.gain_ref, f32[1,1024]{1,0:T(1,128)S(1)} %get-tuple-element.32.plain_ref), custom_call_target="tpu_custom_call" | custom-call | flops 10000000 | bytes 4194304 | tf_op jit(solution)/shard_map/near/pallas_call | solution.py:318
  26.6 0.0 copy-start.2
  26.6 3.3 %near.4.refs_10_ = f32[512,384]{1,0:T(8,128)S(1)} custom-call(f32[512,1024]{1,0:T(8,128)S(1)} %get-tuple-element.29.gated_ref, f32[16,1024]{1,0:T(8,128)S(1)} %get-tuple-element.30.ratio_ref, f32[16,1024]{1,0:T(8,128)S(1)} %get-tuple-element.31.gain_ref, f32[1,1024]{1,0:T(1,128)S(1)} %get-tuple-element.32.plain_ref), custom_call_target="tpu_custom_call" | custom-call | flops 10000000 | bytes 4194304 | tf_op jit(solution)/shard_map/near/pallas_call | solution.py:318
  29.9 0.0 collective-permute-done.3.refs_8_
  29.9 2.5 %mix.1 = bf16[512,1024]{1,0:T(8,128)(2,1)} custom-call(bf16[48,1024]{1,0:T(8,128)(2,1)S(1)} %collective-permute-done.halo_ref.refs_0_, bf16[512,1024]{1,0:T(8,128)(2,1)S(1)} %copy-done.2, f32[3,3,1024]{2,1,0:T(4,128)S(1)} %copy-done.3, f32[3,16,1024]{2,1,0:T(8,128)S(1)} %get-tuple-element.19.refs_3_, bf16[512,1024]{1,0:T(8,128)(2,1)S(1)} %get-tuple-element.20.refs_4_, ...), custom_call_target="tpu_custom_call" | custom-call | tf_op jit(solution)/shard_map/mix/pallas_call | solution.py:338
  (8 shorter events, 0.0 us)
Async XLA Ops:
  0.0 5.6 %copy-start.1 = (bf16[512,1024]{1,0:T(8,128)(2,1)S(1)}, bf16[512,1024]{1,0:T(8,128)(2,1)}, u32[]{:S(2)}) copy-start(bf16[512,1024]{1,0:T(8,128)(2,1)} %v_ref.5) | copy-start | bytes 3145732
  0.0 5.6 %copy-start = (bf16[512,1024]{1,0:T(8,128)(2,1)S(1)}, bf16[512,1024]{1,0:T(8,128)(2,1)}, u32[]{:S(2)}) copy-start(bf16[512,1024]{1,0:T(8,128)(2,1)} %k_ref.5) | copy-start | bytes 3145732
  0.0 4.0 %copy-start.6 = (f32[1,1024]{1,0:T(1,128)S(1)}, f32[1,1024]{1,0:T(1,128)}, u32[]{:S(2)}) copy-start(f32[1,1024]{1,0:T(1,128)} %skip_ref.1) | copy-start | bytes 12292
  0.0 4.0 %copy-start.5 = (f32[16,64]{1,0:T(8,128)S(1)}, f32[16,64]{1,0:T(8,128)}, u32[]{:S(2)}) copy-start(f32[16,64]{1,0:T(8,128)} %decay_ref.1) | copy-start | bytes 12292
  0.0 4.0 %copy-start.4 = (f32[16,64]{1,0:T(8,128)S(1)}, f32[16,64]{1,0:T(8,128)}, u32[]{:S(2)}) copy-start(f32[16,64]{1,0:T(8,128)} %res_ref.1) | copy-start | bytes 12292
  0.0 5.6 %copy-start.3 = (f32[3,3,1024]{2,1,0:T(4,128)S(1)}, f32[3,3,1024]{2,1,0:T(4,128)}, u32[]{:S(2)}) copy-start(f32[3,3,1024]{2,1,0:T(4,128)} %refs_2_.1) | copy-start | bytes 110596
  1.0 8.9 %collective-permute-start = (bf16[48,1024]{1,0:T(8,128)(2,1)S(1)}, bf16[48,1024]{1,0:T(8,128)(2,1)S(1)}, u32[]{:S(2)}, u32[]{:S(2)}) collective-permute-start(bf16[48,1024]{1,0:T(8,128)(2,1)S(1)} %rim.1), channel_id=1, source_target_pairs={{0,4},{4,8},{8,12},{12,16},{16,20},{20,24},{24,28},{28,0},{1,5},{5... | collective-permute-start | bytes 294920 | tf_op jit(solution)/shard_map/ppermute | solution.py:255
  9.9 4.3 %collective-permute-start.1 = (f32[16,1024]{1,0:T(8,128)S(1)}, f32[16,1024]{1,0:T(8,128)S(1)}, u32[]{:S(2)}, u32[]{:S(2)}) collective-permute-start(f32[16,1024]{1,0:T(8,128)S(1)} %get-tuple-element.27.total_ref), channel_id=1, source_target_pairs={{0,4},{4,0},{8,12},{12,8},{16,20},{20,16},{24,28},{28,24},{1,5},{5... | collective-permute-start | bytes 196616 | tf_op jit(solution)/shard_map/ppermute | solution.py:313
  14.3 4.3 %collective-permute-start.2 = (f32[16,1024]{1,0:T(8,128)S(1)}, f32[16,1024]{1,0:T(8,128)S(1)}, u32[]{:S(2)}, u32[]{:S(2)}) collective-permute-start(f32[16,1024]{1,0:T(8,128)S(1)} %merge.2.total_ref), channel_id=1, source_target_pairs={{0,8},{4,12},{8,0},{12,4},{16,24},{20,28},{24,16},{28,20},{1,9},{5... | collective-permute-start | bytes 196616 | tf_op jit(solution)/shard_map/ppermute | solution.py:313
  18.6 11.3 %collective-permute-start.3 = (f32[16,1024]{1,0:T(8,128)S(1)}, f32[16,1024]{1,0:T(8,128)S(1)}, u32[]{:S(2)}, u32[]{:S(2)}) collective-permute-start(f32[16,1024]{1,0:T(8,128)S(1)} %merge.3), channel_id=1, source_target_pairs={{0,16},{4,20},{8,24},{12,28},{16,0},{20,4},{24,8},{28,12},{1,17},{... | collective-permute-start | bytes 196616 | tf_op jit(solution)/shard_map/ppermute | solution.py:313
  26.6 3.4 %copy-start.2 = (bf16[512,1024]{1,0:T(8,128)(2,1)S(1)}, bf16[512,1024]{1,0:T(8,128)(2,1)}, u32[]{:S(2)}) copy-start(bf16[512,1024]{1,0:T(8,128)(2,1)} %refs_1_.1) | copy-start | bytes 3145732

commit v4 on v3

--- a/solution.py
+++ b/solution.py
@@ -60,7 +60,7 @@
         copy.wait()
 
 
-def table_kernel(res_ref, decay_ref, skip_ref, lead_hi, lead_lo, tail_hi, tail_lo, ratio_ref, gain_ref, plain_ref, seam_ref, span_ref, reach_ref):
+def table_kernel(res_ref, decay_ref, skip_ref, lead_hi, lead_lo, tail_ref, row_ref, plain_ref, hop_ref, seam_ref, span_ref, reach_ref):
     length, width = lead_hi.shape
     modes = decay_ref.shape[0]
     phases = reach_ref.shape[0]
@@ -76,33 +76,28 @@
         gains = expand(res_ref[...], tile * (LANES // modes), LANES, modes) * norm_of(rates)
         rate = jnp.sum(jnp.where(own, rates, 0.0), axis=0, keepdims=True)
         gain = jnp.sum(jnp.where(own, gains, 0.0), axis=0, keepdims=True)
-        ratio_ref[:, at] = jnp.exp(-rates)
-        gain_ref[:, at] = gains
+        row_ref[0:1, at] = rate
+        row_ref[1:2, at] = gain
+        hop_ref[:, at] = jnp.exp(-rates * float(LANES))
         for i in range(2):
-            seam_ref[i, :, at] = jnp.exp(-rates * (length - 1.0 - i))
+            seam_ref[i, :, at] = jnp.exp(-rates * (LANES - 1.0 - i))
         for b in range(phases):
             upper = jnp.where((me >> b) % 2 == 1, 1.0, 0.0).astype(F32)
             gap = (me % (1 << b) * length).astype(F32)
             if b + 1 < phases:
                 span_ref[b, :, at] = jnp.exp(-rates * float(length << b))
             reach_ref[b, :, at] = jnp.exp(-rates * gap) * upper
+        rate_rows = jnp.transpose(jnp.broadcast_to(rate, (LANES, LANES)))
+        tail_ref[at, 0:LANES], tail_ref[at, LANES:] = split2(jnp.exp(-rate_rows * (LANES - 1.0 - along)))
         lead = gain * jnp.exp(-rate * (down + 1.0))
         hop = jnp.exp(-rate * float(LANES))
-        rate_rows = jnp.transpose(jnp.broadcast_to(rate, (LANES, LANES)))
-        tail = jnp.exp(-rate_rows * (LANES - 1.0 - along))
-        hop_rows = jnp.exp(-rate_rows * float(LANES))
         for c in range(length // LANES):
             rows = slice(c * LANES, (c + 1) * LANES)
-            back = slice(length - (c + 1) * LANES, length - c * LANES)
-            hi, lo = split2(lead)
-            lead_hi[rows, at], lead_lo[rows, at] = hi, lo
-            hi, lo = split2(tail)
-            tail_hi[at, back], tail_lo[at, back] = hi, lo
+            lead_hi[rows, at], lead_lo[rows, at] = split2(lead)
             lead = lead * hop
-            tail = tail * hop_rows
-
-
-def state_kernel(size, k_ref, v_ref, sf_ref, tail_hi, tail_lo, gated_ref, fresh_ref, kf, vf, xh, xl):
+
+
+def state_kernel(size, k_ref, v_ref, sf_ref, tail_ref, hop_ref, gated_ref, fresh_ref, enter_ref, kf, vf):
     length, lanes = k_ref.shape
     modes = fresh_ref.shape[0]
     tile = pl.program_id(0)
@@ -114,28 +109,37 @@
     for part in range(lanes // LANES):
         at = slice(part * LANES, (part + 1) * LANES)
         base = pl.multiple_of(tile * lanes + part * LANES, LANES)
+        own = pl.ds(base, LANES)
         kt = [sf_ref[1, i : i + 1, at] for i in range(3)]
         vt = [sf_ref[2, i : i + 1, at] for i in range(3)]
-        for start in range(0, length, piece):
-            rows = slice(start, start + piece)
-            kf[SUB + start : SUB + start + piece] = k_ref[rows, at].astype(F32)
-            vf[SUB + start : SUB + start + piece] = v_ref[rows, at].astype(F32)
-            gated = short3(kf, start, piece, kt) * short3(vf, start, piece, vt)
-            if start == 0:
-                gated = jnp.where(inner, gated, 0.0)
-            gated_ref[rows, pl.ds(base, LANES)] = gated
-            xh[rows], xl[rows] = split2(gated)
-        table = pl.ds(base, LANES)
-        out = jnp.dot(tail_hi[table, :], xh[...], preferred_element_type=F32)
-        out = out + jnp.dot(tail_lo[table, :], xh[...], preferred_element_type=F32)
-        out = out + jnp.dot(tail_hi[table, :], xl[...], preferred_element_type=F32)
+        hop = hop_ref[:, own]
+        tail, tail_hi = tail_ref[own, :], tail_ref[own, 0:LANES]
         total = jnp.zeros((modes, LANES), F32)
-        for g in range(LANES // size):
-            total = jnp.where(row == g, out[g * modes : (g + 1) * modes], total)
-        fresh_ref[:, pl.ds(base, LANES)] = total
-
-
-def seam_kernel(halo_ref, k_ref, v_ref, sf_ref, seam_ref, fresh_ref, gated_ref, out_ref, whole_ref, kf, vf):
+        for c in range(length // LANES):
+            his, los = [], []
+            for start in range(c * LANES, (c + 1) * LANES, piece):
+                rows = slice(start, start + piece)
+                kf[SUB + start : SUB + start + piece] = k_ref[rows, at].astype(F32)
+                vf[SUB + start : SUB + start + piece] = v_ref[rows, at].astype(F32)
+                gated = short3(kf, start, piece, kt) * short3(vf, start, piece, vt)
+                if start == 0:
+                    gated = jnp.where(inner, gated, 0.0)
+                gated_ref[rows, own] = gated
+                hi, lo = split2(gated)
+                his.append(hi)
+                los.append(lo)
+            out = jnp.dot(tail, jnp.concatenate(his + his, 0), preferred_element_type=F32)
+            out = out + jnp.dot(tail_hi, jnp.concatenate(los, 0), preferred_element_type=F32)
+            fresh = jnp.zeros((modes, LANES), F32)
+            for g in range(LANES // size):
+                fresh = jnp.where(row == g, out[g * modes : (g + 1) * modes], fresh)
+            if c:
+                enter_ref[c - 1, :, own] = total
+            total = total * hop + fresh
+        fresh_ref[:, own] = total
+
+
+def seam_kernel(halo_ref, k_ref, v_ref, sf_ref, seam_ref, hop_ref, fresh_ref, enter_ref, gated_ref, out_ref, into_ref, whole_ref, kf, vf):
     keep = jnp.where(lax.axis_index("ctx") > 0, 1.0, 0.0).astype(F32)
     kf[0:SUB] = halo_ref[RIM : 2 * RIM].astype(F32)[SUB:] * keep
     vf[0:SUB] = halo_ref[2 * RIM : 3 * RIM].astype(F32)[SUB:] * keep
@@ -145,7 +149,11 @@
     vt = [sf_ref[2, i : i + 1, :] for i in range(3)]
     head = short3(kf, 0, SUB, kt) * short3(vf, 0, SUB, vt)
     whole_ref[0:SUB] = head
-    out_ref[...] = fresh_ref[...] + seam_ref[0] * head[0:1] + seam_ref[1] * head[1:2]
+    first = seam_ref[0] * head[0:1] + seam_ref[1] * head[1:2]
+    for c in range(enter_ref.shape[0]):
+        into_ref[c] = enter_ref[c] + first
+        first = first * hop_ref[...]
+    out_ref[...] = fresh_ref[...] + first
 
 
 def merge_kernel(b, total_ref, got_ref, span_ref, out_ref):
@@ -156,42 +164,44 @@
     out_ref[...] = late + span_ref[b] * early
 
 
-def fold8(parts):
-    sub = lax.broadcasted_iota(jnp.int32, parts[0].shape, 0)
-
-    def join(a, b, gap):
-        low = (sub // gap) % 2 == 0
-        return jnp.where(low, a + pltpu.roll(a, SUB - gap, 0), b + pltpu.roll(b, gap, 0))
-
-    parts = [join(parts[t], parts[t + 4], 4) for t in range(4)]
-    parts = [join(parts[t], parts[t + 2], 2) for t in range(2)]
-    return join(parts[0], parts[1], 1)
-
-
-def local_kernel(first, gated_ref, ratio_ref, gain_ref, plain_ref, out_ref):
+def near_kernel(size, first, gated_ref, into_ref, row_ref, plain_ref, lead_hi, lead_lo, out_ref):
     length, lanes = out_ref.shape
-    modes = ratio_ref.shape[0]
-    at = slice(first, first + lanes)
-    ratio = ratio_ref[:, at]
-    weight = gain_ref[:, at]
-    skip = plain_ref[:, at]
-
-    def step(i, state):
-        base = pl.multiple_of(i * SUB, SUB)
-        parts = []
-        for t in range(SUB):
-            x = gated_ref[pl.ds(base + t, 1), at]
-            state = state * ratio + x
-            mixed = state * weight
-            total = mixed[:SUB]
-            for m in range(SUB, modes, SUB):
-                total = total + mixed[m : m + SUB]
-            parts.append(total)
-        rows = pl.ds(base, SUB)
-        out_ref[rows, :] = fold8(parts) + skip * gated_ref[rows, at]
-        return state
-
-    lax.fori_loop(0, length // SUB, step, jnp.zeros((modes, lanes), F32))
+    modes = into_ref.shape[1]
+    chunks = length // LANES
+    groups = LANES // size
+    down = lax.broadcasted_iota(jnp.int32, (LANES, LANES), 0)
+    along = lax.broadcasted_iota(jnp.int32, (LANES, LANES), 1)
+    causal = along >= down
+    block = down // modes == along // size
+
+    for tile in range(lanes // LANES):
+        at = slice(first + tile * LANES, first + (tile + 1) * LANES)
+        to = slice(tile * LANES, (tile + 1) * LANES)
+        rate = jnp.transpose(jnp.broadcast_to(row_ref[0:1, at], (LANES, LANES)))
+        gain = jnp.transpose(jnp.broadcast_to(row_ref[1:2, at], (LANES, LANES)))
+        curve = gain * jnp.exp(-rate * along.astype(F32))
+        halves = [split2(jnp.transpose(gated_ref[c * LANES : (c + 1) * LANES, at])) for c in range(chunks)]
+        outs = []
+        for g in range(groups):
+            rows = slice(g * size, (g + 1) * size)
+            taps = jnp.sum(curve[g * modes : (g + 1) * modes], axis=0, keepdims=True)
+            toe = pltpu.roll(jnp.broadcast_to(taps, (LANES, LANES)), 0, 1, stride=1, stride_axis=0)
+            hi, lo = split2(jnp.where(causal, toe, 0.0))
+            xh = jnp.concatenate([h[rows] for h, _ in halves], 0)
+            xl = jnp.concatenate([l[rows] for _, l in halves], 0)
+            out = jnp.dot(jnp.concatenate([xh, xl], 1), jnp.concatenate([hi, hi], 0), preferred_element_type=F32)
+            outs.append(out + jnp.dot(xh, lo, preferred_element_type=F32))
+        lead = jnp.concatenate([lead_hi[0:LANES, at], lead_lo[0:LANES, at]], 1)
+        for c in range(chunks):
+            rows = slice(c * LANES, (c + 1) * LANES)
+            near = jnp.transpose(jnp.concatenate([o[c * size : (c + 1) * size] for o in outs], 0))
+            near = near + plain_ref[:, at] * gated_ref[rows, at]
+            if c:
+                wide = jnp.where(block, jnp.concatenate([into_ref[c - 1, :, at]] * groups, 0), 0.0)
+                hi, lo = split2(wide)
+                near = near + jnp.dot(lead, jnp.concatenate([hi, hi], 0), preferred_element_type=F32)
+                near = near + jnp.dot(lead[:, :LANES], lo, preferred_element_type=F32)
+            out_ref[rows, to] = near
 
 
 def mix_kernel(size, phases, parts, *refs):
@@ -255,17 +265,24 @@
     halo = lax.ppermute(rims, "ctx", [(i, (i + 1) % ranks) for i in range(ranks)])
 
     lead_shape = jax.ShapeDtypeStruct((length, width), BF16)
-    tail_shape = jax.ShapeDtypeStruct((width, length), BF16)
+    tail_shape = jax.ShapeDtypeStruct((width, 2 * LANES), BF16)
     scan_shape = lambda count: jax.ShapeDtypeStruct((count, modes, width), F32)
     row_shape = jax.ShapeDtypeStruct((modes, width), F32)
-    lead_hi, lead_lo, tail_hi, tail_lo, ratio, gain, plain, seam, span, reach = pl.pallas_call(
+    lead_hi, lead_lo, tail, row, plain, hop, seam, span, reach = pl.pallas_call(
         table_kernel,
         in_specs=[VMEM] * 3,
-        out_specs=[VMEM] * 10,
-        out_shape=[lead_shape] * 2
-        + [tail_shape] * 2
-        + [row_shape] * 2
-        + [jax.ShapeDtypeStruct((1, width), F32), scan_shape(2), scan_shape(max(1, phases - 1)), scan_shape(phases)],
+        out_specs=[VMEM] * 9,
+        out_shape=[
+            lead_shape,
+            lead_shape,
+            tail_shape,
+            jax.ShapeDtypeStruct((2, width), F32),
+            jax.ShapeDtypeStruct((1, width), F32),
+            row_shape,
+            scan_shape(2),
+            scan_shape(max(1, phases - 1)),
+            scan_shape(phases),
+        ],
         compiler_params=PARAMS,
         cost_estimate=pl.CostEstimate(flops=10**7, bytes_accessed=5 << 20, transcendentals=0),
         name="tables",
@@ -273,7 +290,9 @@
 
     tile = min(width, WIDE)
     cols = lambda rows: pl.BlockSpec((rows, tile), lambda j: (0, j))
-    gated, fresh = pl.pallas_call(
+    gated_shape = jax.ShapeDtypeStruct((length, width), F32)
+    enter_shape = scan_shape(length // LANES - 1)
+    gated, fresh, enter = pl.pallas_call(
         functools.partial(state_kernel, size),
         grid=(width // tile,),
         in_specs=[
@@ -283,28 +302,23 @@
             VMEM,
             VMEM,
         ],
-        out_specs=[VMEM] * 2,
-        out_shape=[jax.ShapeDtypeStruct((length, width), F32), row_shape],
-        scratch_shapes=[
-            pltpu.VMEM((SUB + length, LANES), F32),
-            pltpu.VMEM((SUB + length, LANES), F32),
-            pltpu.VMEM((length, LANES), BF16),
-            pltpu.VMEM((length, LANES), BF16),
-        ],
+        out_specs=[VMEM] * 3,
+        out_shape=[gated_shape, row_shape, enter_shape],
+        scratch_shapes=[pltpu.VMEM((SUB + length, LANES), F32)] * 2,
         compiler_params=PARAMS,
         cost_estimate=pl.CostEstimate(flops=10**7, bytes_accessed=5 << 20, transcendentals=0),
         name="state",
-    )(key_in, value_in, short_filter, tail_hi, tail_lo)
-    fresh, gated = pl.pallas_call(
+    )(key_in, value_in, short_filter, tail, hop)
+    fresh, into, gated = pl.pallas_call(
         seam_kernel,
-        in_specs=[VMEM] * 7,
-        out_specs=[VMEM] * 2,
-        out_shape=[row_shape, jax.ShapeDtypeStruct((length, width), F32)],
-        input_output_aliases={6: 1},
+        in_specs=[VMEM] * 9,
+        out_specs=[VMEM] * 3,
+        out_shape=[row_shape, enter_shape, gated_shape],
+        input_output_aliases={8: 2},
         scratch_shapes=[pltpu.VMEM((2 * SUB, width), F32)] * 2,
         compiler_params=PARAMS,
         name="seam",
-    )(halo, key_in, value_in, short_filter, seam, fresh, gated)
+    )(halo, key_in, value_in, short_filter, seam, hop, fresh, enter, gated)
 
     unit = LANES if width // LANES >= 2 * phases else min(width, WIDE)
     cuts = [width // unit * b // phases * unit for b in range(phases + 1)]
@@ -316,14 +330,14 @@
         if lanes:
             nears.append(
                 pl.pallas_call(
-                    functools.partial(local_kernel, cuts[b]),
-                    in_specs=[VMEM] * 4,
+                    functools.partial(near_kernel, size, cuts[b]),
+                    in_specs=[VMEM] * 6,
                     out_specs=VMEM,
                     out_shape=jax.ShapeDtypeStruct((length, lanes), F32),
                     compiler_params=PARAMS,
                     cost_estimate=pl.CostEstimate(flops=10**7, bytes_accessed=4 << 20, transcendentals=0),
                     name="near",
-                )(gated, ratio, gain, plain)
+                )(gated, into, row, plain, lead_hi, lead_lo)
             )
         if b + 1 < phases:
             total = pl.pallas_call(
@@ -360,6 +374,4 @@
         P(None, None, "fsdp"),
         P(None, "fsdp"),
     )
-    return jax.shard_map(
-        body, mesh=mesh, in_specs=placed, out_specs=P("ctx", "fsdp"), check_vma=False
-    )
+    return jax.shard_map(body, mesh=mesh, in_specs=placed, out_specs=P("ctx", "fsdp"), check_vma=False)

time: 32.6 us -> 26.7 us (0.82)
  Pallas kernels: 17.7 us -> 11.4 us
  waiting for transfers between devices: 7.68 us -> 10.9 us
  starting transfers between devices: 6.86 us -> 4.05 us
    pallas_call x5, Pallas kernels: 10.8 us -> 5.15 us  [the longest x3 3.88 us: body(): pl.pallas_call(functools.partial(near_kernel, size, cuts[b]), in_specs=[V...]
    ppermute x3, starting transfers between devices: 3.83 us -> 1.02 us  [body(): got = lax.ppermute(total, 'ctx', [(i, i ^ 1 << b) for i in range(ranks)])]
    ppermute x3, waiting for transfers between devices: 6.91 us -> 9.09 us  [body(): got = lax.ppermute(total, 'ctx', [(i, i ^ 1 << b) for i in range(ranks)])]
    ppermute x1, waiting for transfers between devices: 0.77 us -> 1.79 us  [body(): lax.ppermute(rims, 'ctx', [(i, (i + 1) % ranks) for i in range(ranks)])]
    pallas_call x1, Pallas kernels: 3.49 us -> 2.79 us  [body(): pl.pallas_call(functools.partial(state_kernel, size), grid=(width // tile...]
  transfers between devices with their start and end apart: 4 -> 4, of which waited for: 3 -> 4; matrix products, arithmetic and copies ran while one was open for 0% -> 0% of each run, Pallas kernels for 44% -> 30%
where the time goes in v4:
time: 26.7 us; the launch traced here: 26.5 us
  Pallas kernels  11.4 us (43%)
  waiting for transfers between devices  10.9 us (41%)
  starting transfers between devices  4.05 us (15%)
    ppermute x3, waiting for transfers between devices, body(): got = lax.ppermute(total, 'ctx', [(i, i ^ 1 << b) for i in range(ranks)])  9.09 us
    pallas_call x3, Pallas kernels, body(): pl.pallas_call(functools.partial(near_kernel, size, cuts[b]), in_specs=[V...  3.88 us
    ppermute x1, starting transfers between devices, body(): lax.ppermute(rims, 'ctx', [(i, (i + 1) % ranks) for i in range(ranks)])  3.03 us
    pallas_call x1, Pallas kernels, body(): pl.pallas_call(functools.partial(state_kernel, size), grid=(width // tile...  2.79 us
    pallas_call x1, Pallas kernels, body(): pl.pallas_call(functools.partial(mix_kernel, size, phases, len(nears)), i...  2.5 us
    ppermute x1, waiting for transfers between devices, body(): lax.ppermute(rims, 'ctx', [(i, (i + 1) % ranks) for i in range(ranks)])  1.79 us
    pallas_call x1, Pallas kernels, body(): pl.pallas_call(table_kernel, in_specs=[VMEM] * 3, out_specs=[VMEM] * 9, o...  1.19 us
    ppermute x3, starting transfers between devices, body(): got = lax.ppermute(total, 'ctx', [(i, i ^ 1 << b) for i in range(ranks)])  1.02 us
  transfers between devices with their start and end apart: 4, of which 4 were waited for; matrix products, arithmetic and copies ran while one was open for 0% of the time, Pallas kernels for 30%

profile of v4, /device:TPU:0, one launch (start us, length us, event | category | flops | bytes accessed | tf_op | source)
XLA Modules:
  0.0 26.5 jit_solution(5951724832397069357)
XLA Ops:
  0.0 0.0 copy-start.3
  0.0 1.0 %rim.1 = bf16[48,1024]{1,0:T(8,128)(2,1)S(1)} custom-call(bf16[512,1024]{1,0:T(8,128)(2,1)} %refs_1_.1, bf16[512,1024]{1,0:T(8,128)(2,1)} %k_ref.5, bf16[512,1024]{1,0:T(8,128)(2,1)} %v_ref.5), custom_call_target="tpu_custom_call" | custom-call | tf_op jit(solution)/shard_map/rim/pallas_call | solution.py:256
  1.0 3.0 %collective-permute-start = (bf16[48,1024]{1,0:T(8,128)(2,1)S(1)}, bf16[48,1024]{1,0:T(8,128)(2,1)S(1)}, u32[]{:S(2)}, u32[]{:S(2)}) collective-permute-start(bf16[48,1024]{1,0:T(8,128)(2,1)S(1)} %rim.1), channel_id=1, source_target_pairs={{0,4},{4,8},{8,12},{12,16},{16,20},{20,24},{24,28},{28,0},{1,5},{5... | collective-permute-start | bytes 294920 | tf_op jit(solution)/shard_map/ppermute | solution.py:265
  4.0 0.0 copy-done.6
  4.0 0.0 copy-done.5
  4.0 0.0 copy-done.4
  4.0 1.2 %tables.1 = (bf16[512,1024]{1,0:T(8,128)(2,1)S(1)}, bf16[512,1024]{1,0:T(8,128)(2,1)S(1)}, bf16[1024,256]{1,0:T(8,128)(2,1)S(1)}, f32[2,1024]{1,0:T(2,128)S(1)},...) custom-call(f32[16,64]{1,0:T(8,128)S(1)} %copy-done.4, ...), custom_call_target="tpu_custom_call" | custom-call | flops 10000000 | bytes 5242880 | tf_op jit(solution)/shard_map/tables/pallas_call | solution.py:271
  5.2 0.0 copy-done.1
  5.2 0.0 copy-done
  5.3 2.8 %state.1 = (f32[512,1024]{1,0:T(8,128)S(1)}, f32[16,1024]{1,0:T(8,128)S(1)}, f32[3,16,1024]{2,1,0:T(8,128)S(1)}) custom-call(bf16[512,1024]{1,0:T(8,128)(2,1)S(1)} %copy-done, bf16[512,1024]{1,0:T(8,128)(2,1)S(1)} %copy-done.1, f32[3,3,1024]{2,1,0:T(4,128)S(1)} %copy-done.3, bf16[1024,256]{1,0:T(8,128)(2,1)S(1)} %get-tuple-element.25.tail_ref, ...), custom_call_target="tpu_custom_call" | custom-call | flops 10000000 | bytes 5242880 | tf_op jit(solution)/shard_map/state/pallas_call | solution.py:295
  8.1 1.8 %collective-permute-done.halo_ref.refs_0_ = bf16[48,1024]{1,0:T(8,128)(2,1)S(1)} collective-permute-done((bf16[48,1024]{1,0:T(8,128)(2,1)S(1)}, bf16[48,1024]{1,0:T(8,128)(2,1)S(1)}, u32[]{:S(2)}, u32[]{:S(2)}) %collective-permute-start) | collective-permute-done | bytes 98336 | tf_op jit(solution)/shard_map/ppermute | solution.py:265
  9.9 0.1 seam.1
  9.9 0.1 collective-permute-start.1
  10.0 4.3 %collective-permute-done.1.got_ref.refs_6_ = f32[16,1024]{1,0:T(8,128)S(1)} collective-permute-done((f32[16,1024]{1,0:T(8,128)S(1)}, f32[16,1024]{1,0:T(8,128)S(1)}, u32[]{:S(2)}, u32[]{:S(2)}) %collective-permute-start.1) | collective-permute-done | bytes 65568 | tf_op jit(solution)/shard_map/ppermute | solution.py:327
  14.3 0.1 collective-permute-start.2
  14.4 4.3 %collective-permute-done.2.got_ref.refs_7_ = f32[16,1024]{1,0:T(8,128)S(1)} collective-permute-done((f32[16,1024]{1,0:T(8,128)S(1)}, f32[16,1024]{1,0:T(8,128)S(1)}, u32[]{:S(2)}, u32[]{:S(2)}) %collective-permute-start.2) | collective-permute-done | bytes 65568 | tf_op jit(solution)/shard_map/ppermute | solution.py:327
  18.6 0.9 %collective-permute-start.3 = (f32[16,1024]{1,0:T(8,128)S(1)}, f32[16,1024]{1,0:T(8,128)S(1)}, u32[]{:S(2)}, u32[]{:S(2)}) collective-permute-start(f32[16,1024]{1,0:T(8,128)S(1)} %merge.3), channel_id=1, source_target_pairs={{0,16},{4,20},{8,24},{12,28},{16,0},{20,4},{24,8},{28,12},{1,17},{... | collective-permute-start | bytes 196616 | tf_op jit(solution)/shard_map/ppermute | solution.py:327
  19.5 0.9 %near.3.refs_9_ = f32[512,256]{1,0:T(8,128)S(1)} custom-call(f32[512,1024]{1,0:T(8,128)S(1)} %get-tuple-element.31.gated_ref, f32[3,16,1024]{2,1,0:T(8,128)S(1)} %get-tuple-element.32.into_ref, f32[2,1024]{1,0:T(2,128)S(1)} %get-tuple-element.33.row_ref, f32[1,1024]{1,0:T(1,128)S(1)} %get-tuple-element.34.plain_ref, ...), custom_call_target="tpu_custom_call" | custom-call | flops 10000000 | bytes 4194304 | tf_op jit(solution)/shard_map/near/pallas_call | solution.py:332
  20.4 1.5 %near.5.refs_11_ = f32[512,384]{1,0:T(8,128)S(1)} custom-call(f32[512,1024]{1,0:T(8,128)S(1)} %get-tuple-element.31.gated_ref, f32[3,16,1024]{2,1,0:T(8,128)S(1)} %get-tuple-element.32.into_ref, f32[2,1024]{1,0:T(2,128)S(1)} %get-tuple-element.33.row_ref, f32[1,1024]{1,0:T(1,128)S(1)} %get-tuple-element.34.plain_ref, ...), custom_call_target="tpu_custom_call" | custom-call | flops 10000000 | bytes 4194304 | tf_op jit(solution)/shard_map/near/pallas_call | solution.py:332
  21.9 0.0 copy-start.2
  21.9 1.5 %near.4.refs_10_ = f32[512,384]{1,0:T(8,128)S(1)} custom-call(f32[512,1024]{1,0:T(8,128)S(1)} %get-tuple-element.31.gated_ref, f32[3,16,1024]{2,1,0:T(8,128)S(1)} %get-tuple-element.32.into_ref, f32[2,1024]{1,0:T(2,128)S(1)} %get-tuple-element.33.row_ref, f32[1,1024]{1,0:T(1,128)S(1)} %get-tuple-element.34.plain_ref, ...), custom_call_target="tpu_custom_call" | custom-call | flops 10000000 | bytes 4194304 | tf_op jit(solution)/shard_map/near/pallas_call | solution.py:332
  23.4 0.6 %collective-permute-done.3.refs_8_ = f32[16,1024]{1,0:T(8,128)S(1)} collective-permute-done((f32[16,1024]{1,0:T(8,128)S(1)}, f32[16,1024]{1,0:T(8,128)S(1)}, u32[]{:S(2)}, u32[]{:S(2)}) %collective-permute-start.3) | collective-permute-done | bytes 65568 | tf_op jit(solution)/shard_map/ppermute | solution.py:327
  24.0 0.0 copy-done.2
  24.0 2.5 %mix.1 = bf16[512,1024]{1,0:T(8,128)(2,1)} custom-call(bf16[48,1024]{1,0:T(8,128)(2,1)S(1)} %collective-permute-done.halo_ref.refs_0_, bf16[512,1024]{1,0:T(8,128)(2,1)S(1)} %copy-done.2, f32[3,3,1024]{2,1,0:T(4,128)S(1)} %copy-done.3, f32[3,16,1024]{2,1,0:T(8,128)S(1)} %get-tuple-element.20.refs_3_, ...), custom_call_target="tpu_custom_call" | custom-call | tf_op jit(solution)/shard_map/mix/pallas_call | solution.py:352
  (8 shorter events, 0.0 us)
Async XLA Ops:
  0.0 5.2 %copy-start.1 = (bf16[512,1024]{1,0:T(8,128)(2,1)S(1)}, bf16[512,1024]{1,0:T(8,128)(2,1)}, u32[]{:S(2)}) copy-start(bf16[512,1024]{1,0:T(8,128)(2,1)} %v_ref.5) | copy-start | bytes 3145732
  0.0 5.2 %copy-start = (bf16[512,1024]{1,0:T(8,128)(2,1)S(1)}, bf16[512,1024]{1,0:T(8,128)(2,1)}, u32[]{:S(2)}) copy-start(bf16[512,1024]{1,0:T(8,128)(2,1)} %k_ref.5) | copy-start | bytes 3145732
  0.0 4.0 %copy-start.6 = (f32[1,1024]{1,0:T(1,128)S(1)}, f32[1,1024]{1,0:T(1,128)}, u32[]{:S(2)}) copy-start(f32[1,1024]{1,0:T(1,128)} %skip_ref.1) | copy-start | bytes 12292
  0.0 4.0 %copy-start.5 = (f32[16,64]{1,0:T(8,128)S(1)}, f32[16,64]{1,0:T(8,128)}, u32[]{:S(2)}) copy-start(f32[16,64]{1,0:T(8,128)} %decay_ref.1) | copy-start | bytes 12292
  0.0 4.0 %copy-start.4 = (f32[16,64]{1,0:T(8,128)S(1)}, f32[16,64]{1,0:T(8,128)}, u32[]{:S(2)}) copy-start(f32[16,64]{1,0:T(8,128)} %res_ref.1) | copy-start | bytes 12292
  0.0 5.2 %copy-start.3 = (f32[3,3,1024]{2,1,0:T(4,128)S(1)}, f32[3,3,1024]{2,1,0:T(4,128)}, u32[]{:S(2)}) copy-start(f32[3,3,1024]{2,1,0:T(4,128)} %refs_2_.1) | copy-start | bytes 110596
  1.0 8.9 %collective-permute-start = (bf16[48,1024]{1,0:T(8,128)(2,1)S(1)}, bf16[48,1024]{1,0:T(8,128)(2,1)S(1)}, u32[]{:S(2)}, u32[]{:S(2)}) collective-permute-start(bf16[48,1024]{1,0:T(8,128)(2,1)S(1)} %rim.1), channel_id=1, source_target_pairs={{0,4},{4,8},{8,12},{12,16},{16,20},{20,24},{24,28},{28,0},{1,5},{5... | collective-permute-start | bytes 294920 | tf_op jit(solution)/shard_map/ppermute | solution.py:265
  9.9 4.3 %collective-permute-start.1 = (f32[16,1024]{1,0:T(8,128)S(1)}, f32[16,1024]{1,0:T(8,128)S(1)}, u32[]{:S(2)}, u32[]{:S(2)}) collective-permute-start(f32[16,1024]{1,0:T(8,128)S(1)} %get-tuple-element.29.total_ref), channel_id=1, source_target_pairs={{0,4},{4,0},{8,12},{12,8},{16,20},{20,16},{24,28},{28,24},{1,5},{5... | collective-permute-start | bytes 196616 | tf_op jit(solution)/shard_map/ppermute | solution.py:327
  14.3 4.3 %collective-permute-start.2 = (f32[16,1024]{1,0:T(8,128)S(1)}, f32[16,1024]{1,0:T(8,128)S(1)}, u32[]{:S(2)}, u32[]{:S(2)}) collective-permute-start(f32[16,1024]{1,0:T(8,128)S(1)} %merge.2.total_ref), channel_id=1, source_target_pairs={{0,8},{4,12},{8,0},{12,4},{16,24},{20,28},{24,16},{28,20},{1,9},{5... | collective-permute-start | bytes 196616 | tf_op jit(solution)/shard_map/ppermute | solution.py:327
  18.6 5.4 %collective-permute-start.3 = (f32[16,1024]{1,0:T(8,128)S(1)}, f32[16,1024]{1,0:T(8,128)S(1)}, u32[]{:S(2)}, u32[]{:S(2)}) collective-permute-start(f32[16,1024]{1,0:T(8,128)S(1)} %merge.3), channel_id=1, source_target_pairs={{0,16},{4,20},{8,24},{12,28},{16,0},{20,4},{24,8},{28,12},{1,17},{... | collective-permute-start | bytes 196616 | tf_op jit(solution)/shard_map/ppermute | solution.py:327
  21.9 2.1 %copy-start.2 = (bf16[512,1024]{1,0:T(8,128)(2,1)S(1)}, bf16[512,1024]{1,0:T(8,128)(2,1)}, u32[]{:S(2)}) copy-start(bf16[512,1024]{1,0:T(8,128)(2,1)} %refs_1_.1) | copy-start | bytes 3145732

commit v5 on v4

--- a/solution.py
+++ b/solution.py
@@ -11,7 +11,7 @@
 LANES = 128
 WIDE = 256
 SUB = 8
-RIM = 16
+RIM = 8
 F32 = jnp.float32
 BF16 = jnp.bfloat16
 VMEM = pl.BlockSpec(memory_space=pltpu.VMEM)
@@ -141,10 +141,10 @@
 
 def seam_kernel(halo_ref, k_ref, v_ref, sf_ref, seam_ref, hop_ref, fresh_ref, enter_ref, gated_ref, out_ref, into_ref, whole_ref, kf, vf):
     keep = jnp.where(lax.axis_index("ctx") > 0, 1.0, 0.0).astype(F32)
-    kf[0:SUB] = halo_ref[RIM : 2 * RIM].astype(F32)[SUB:] * keep
-    vf[0:SUB] = halo_ref[2 * RIM : 3 * RIM].astype(F32)[SUB:] * keep
-    kf[SUB:] = k_ref[0:RIM].astype(F32)[:SUB]
-    vf[SUB:] = v_ref[0:RIM].astype(F32)[:SUB]
+    kf[0:SUB] = halo_ref[RIM : 2 * RIM].astype(F32) * keep
+    vf[0:SUB] = halo_ref[2 * RIM : 3 * RIM].astype(F32) * keep
+    kf[SUB:] = k_ref[0:SUB].astype(F32)
+    vf[SUB:] = v_ref[0:SUB].astype(F32)
     kt = [sf_ref[1, i : i + 1, :] for i in range(3)]
     vt = [sf_ref[2, i : i + 1, :] for i in range(3)]
     head = short3(kf, 0, SUB, kt) * short3(vf, 0, SUB, vt)
@@ -164,7 +164,21 @@
     out_ref[...] = late + span_ref[b] * early
 
 
-def near_kernel(size, first, gated_ref, into_ref, row_ref, plain_ref, lead_hi, lead_lo, out_ref):
+def query_kernel(halo_ref, q_ref, sf_ref, out_ref, qf):
+    length, width = q_ref.shape
+    keep = jnp.where(lax.axis_index("ctx") > 0, 1.0, 0.0).astype(F32)
+    for lane in range(0, width, LANES):
+        at = slice(lane, lane + LANES)
+        taps = [sf_ref[0, i : i + 1, at] for i in range(3)]
+        qf[0:SUB] = halo_ref[0:RIM, at].astype(F32) * keep
+        piece = 64
+        for start in range(0, length, piece):
+            rows = slice(start, start + piece)
+            qf[SUB + start : SUB + start + piece] = q_ref[rows, at].astype(F32)
+            out_ref[rows, at] = short3(qf, start, piece, taps)
+
+
+def near_kernel(size, first, gated_ref, query_ref, into_ref, row_ref, plain_ref, lead_hi, lead_lo, out_ref):
     length, lanes = out_ref.shape
     modes = into_ref.shape[1]
     chunks = length // LANES
@@ -201,19 +215,18 @@
                 hi, lo = split2(wide)
                 near = near + jnp.dot(lead, jnp.concatenate([hi, hi], 0), preferred_element_type=F32)
                 near = near + jnp.dot(lead[:, :LANES], lo, preferred_element_type=F32)
-            out_ref[rows, to] = near
+            out_ref[rows, to] = query_ref[rows, at] * near
 
 
 def mix_kernel(size, phases, parts, *refs):
-    halo_ref, q_ref, sf_ref, reach_ref, lead_hi, lead_lo = refs[:6]
-    gots = refs[6 : 6 + phases]
-    locals_ = refs[6 + phases : 6 + phases + parts]
-    out_ref, qf, stage, sem = refs[6 + phases + parts :]
-    length, width = q_ref.shape
+    query_ref, reach_ref, lead_hi, lead_lo = refs[:4]
+    gots = refs[4 : 4 + phases]
+    nears = refs[4 + phases : 4 + phases + parts]
+    out_ref, stage, sem = refs[4 + phases + parts :]
+    _, width = query_ref.shape
     modes = reach_ref.shape[1]
-    keep = jnp.where(lax.axis_index("ctx") > 0, 1.0, 0.0).astype(F32)
     where = []
-    for ref in locals_:
+    for ref in nears:
         where += [(ref, c) for c in range(0, ref.shape[1], LANES)]
     span = min(WIDE, width)
     groups = span // size
@@ -234,12 +247,9 @@
         for half in range(span // LANES):
             lane = tile * span + half * LANES
             cut = slice(lane, lane + LANES)
-            qf[0:SUB] = halo_ref[0:RIM, cut].astype(F32)[SUB:] * keep
-            qf[SUB:] = q_ref[:, cut].astype(F32)
-            taps = [sf_ref[0, i : i + 1, cut] for i in range(3)]
             near, c = where[lane // LANES]
-            own = near[:, c : c + LANES] + term[:, half * LANES : (half + 1) * LANES]
-            stage[:, cut] = (short3(qf, 0, length, taps) * own).astype(BF16)
+            far = query_ref[:, cut] * term[:, half * LANES : (half + 1) * LANES]
+            stage[:, cut] = (near[:, c : c + LANES] + far).astype(BF16)
         copy = pltpu.make_async_copy(stage.at[:, at], out_ref.at[:, at], sem.at[tile])
         copy.start()
         copies.append(copy)
@@ -320,6 +330,17 @@
         name="seam",
     )(halo, key_in, value_in, short_filter, seam, hop, fresh, enter, gated)
 
+    query = pl.pallas_call(
+        query_kernel,
+        in_specs=[VMEM] * 3,
+        out_specs=VMEM,
+        out_shape=gated_shape,
+        scratch_shapes=[pltpu.VMEM((SUB + length, LANES), F32)],
+        compiler_params=PARAMS,
+        cost_estimate=pl.CostEstimate(flops=10**7, bytes_accessed=4 << 20, transcendentals=0),
+        name="query",
+    )(halo, query_in, short_filter)
+
     unit = LANES if width // LANES >= 2 * phases else min(width, WIDE)
     cuts = [width // unit * b // phases * unit for b in range(phases + 1)]
     nears, gots, total = [], [], fresh
@@ -331,13 +352,13 @@
             nears.append(
                 pl.pallas_call(
                     functools.partial(near_kernel, size, cuts[b]),
-                    in_specs=[VMEM] * 6,
+                    in_specs=[VMEM] * 7,
                     out_specs=VMEM,
                     out_shape=jax.ShapeDtypeStruct((length, lanes), F32),
                     compiler_params=PARAMS,
                     cost_estimate=pl.CostEstimate(flops=10**7, bytes_accessed=4 << 20, transcendentals=0),
                     name="near",
-                )(gated, into, row, plain, lead_hi, lead_lo)
+                )(gated, query, into, row, plain, lead_hi, lead_lo)
             )
         if b + 1 < phases:
             total = pl.pallas_call(
@@ -351,17 +372,16 @@
 
     return pl.pallas_call(
         functools.partial(mix_kernel, size, phases, len(nears)),
-        in_specs=[VMEM] * (6 + phases + len(nears)),
+        in_specs=[VMEM] * (4 + phases + len(nears)),
         out_specs=pl.BlockSpec(memory_space=pl.ANY),
         out_shape=jax.ShapeDtypeStruct((length, width), BF16),
         scratch_shapes=[
-            pltpu.VMEM((SUB + length, LANES), F32),
             pltpu.VMEM((length, width), BF16),
             pltpu.SemaphoreType.DMA((max(1, width // WIDE),)),
         ],
         compiler_params=PARAMS,
         name="mix",
-    )(halo, query_in, short_filter, reach, lead_hi, lead_lo, *gots, *nears)
+    )(query, reach, lead_hi, lead_lo, *gots, *nears)
 
 
 def solution(mesh):

time: 26.7 us -> 26.4 us (0.989)
  waiting for transfers between devices: 10.9 us -> 8.72 us
  starting transfers between devices: 4.05 us -> 5.82 us
    ppermute x3, starting transfers between devices: 1.02 us -> 2.79 us  [body(): got = lax.ppermute(total, 'ctx', [(i, i ^ 1 << b) for i in range(ranks)])]
    ppermute x3, waiting for transfers between devices: 9.09 us -> 7.6 us  [body(): got = lax.ppermute(total, 'ctx', [(i, i ^ 1 << b) for i in range(ranks)])]
    ppermute x1, waiting for transfers between devices: 1.79 us -> 1.12 us  [body(): lax.ppermute(rims, 'ctx', [(i, (i + 1) % ranks) for i in range(ranks)])]
    pallas_call x0 -> x1, Pallas kernels: none -> 0.61 us  [body(): pl.pallas_call(query_kernel, in_specs=[VMEM] * 3, out_specs=VMEM, out_sha...]
    pallas_call x1, Pallas kernels: 2.5 us -> 2.01 us  [body(): pl.pallas_call(functools.partial(mix_kernel, size, phases, len(nears)), i...]
  transfers between devices with their start and end apart: 4 -> 4, of which waited for: 4 -> 3; matrix products, arithmetic and copies ran while one was open for 0% -> 0% of each run, Pallas kernels for 30% -> 32%
where the time goes in v5:
time: 26.4 us; the launch traced here: 26.2 us
  Pallas kernels  11.5 us (44%)
  waiting for transfers between devices  8.72 us (33%)
  starting transfers between devices  5.82 us (22%)
    ppermute x3, waiting for transfers between devices, body(): got = lax.ppermute(total, 'ctx', [(i, i ^ 1 << b) for i in range(ranks)])  7.6 us
    pallas_call x3, Pallas kernels, body(): pl.pallas_call(functools.partial(near_kernel, size, cuts[b]), in_specs=[V...  3.92 us
    ppermute x1, starting transfers between devices, body(): lax.ppermute(rims, 'ctx', [(i, (i + 1) % ranks) for i in range(ranks)])  3.03 us
    ppermute x3, starting transfers between devices, body(): got = lax.ppermute(total, 'ctx', [(i, i ^ 1 << b) for i in range(ranks)])  2.79 us
    pallas_call x1, Pallas kernels, body(): pl.pallas_call(functools.partial(state_kernel, size), grid=(width // tile...  2.74 us
    pallas_call x1, Pallas kernels, body(): pl.pallas_call(functools.partial(mix_kernel, size, phases, len(nears)), i...  2.01 us
    pallas_call x1, Pallas kernels, body(): pl.pallas_call(table_kernel, in_specs=[VMEM] * 3, out_specs=[VMEM] * 9, o...  1.19 us
    ppermute x1, waiting for transfers between devices, body(): lax.ppermute(rims, 'ctx', [(i, (i + 1) % ranks) for i in range(ranks)])  1.12 us
  transfers between devices with their start and end apart: 4, of which 3 were waited for; matrix products, arithmetic and copies ran while one was open for 0% of the time, Pallas kernels for 32%

profile of v5, /device:TPU:0, one launch (start us, length us, event | category | flops | bytes accessed | tf_op | source)
XLA Modules:
  0.0 26.2 jit_solution(7111670787729382431)
XLA Ops:
  0.0 0.0 copy-start.3
  0.0 0.9 %rim.1 = bf16[24,1024]{1,0:T(8,128)(2,1)S(1)} custom-call(bf16[512,1024]{1,0:T(8,128)(2,1)} %q_ref.3, bf16[512,1024]{1,0:T(8,128)(2,1)} %k_ref.5, bf16[512,1024]{1,0:T(8,128)(2,1)} %v_ref.5), custom_call_target="tpu_custom_call" | custom-call | tf_op jit(solution)/shard_map/rim/pallas_call | solution.py:266
  1.0 3.0 %collective-permute-start = (bf16[24,1024]{1,0:T(8,128)(2,1)S(1)}, bf16[24,1024]{1,0:T(8,128)(2,1)S(1)}, u32[]{:S(2)}, u32[]{:S(2)}) collective-permute-start(bf16[24,1024]{1,0:T(8,128)(2,1)S(1)} %rim.1), channel_id=1, source_target_pairs={{0,4},{4,8},{8,12},{12,16},{16,20},{20,24},{24,28},{28,0},{1,5},{5... | collective-permute-start | bytes 147464 | tf_op jit(solution)/shard_map/ppermute | solution.py:275
  4.0 0.0 copy-done.4
  4.0 0.0 copy-done.5
  4.0 0.0 copy-done.6
  4.0 1.2 %tables.1 = (bf16[512,1024]{1,0:T(8,128)(2,1)S(1)}, bf16[512,1024]{1,0:T(8,128)(2,1)S(1)}, bf16[1024,256]{1,0:T(8,128)(2,1)S(1)}, f32[2,1024]{1,0:T(2,128)S(1)},...) custom-call(f32[16,64]{1,0:T(8,128)S(1)} %copy-done.4, ...), custom_call_target="tpu_custom_call" | custom-call | flops 10000000 | bytes 5242880 | tf_op jit(solution)/shard_map/tables/pallas_call | solution.py:281
  5.2 0.0 copy-done
  5.2 0.0 copy-done.1
  5.2 0.0 copy-done.3
  5.2 2.7 %state.1 = (f32[512,1024]{1,0:T(8,128)S(1)}, f32[16,1024]{1,0:T(8,128)S(1)}, f32[3,16,1024]{2,1,0:T(8,128)S(1)}) custom-call(bf16[512,1024]{1,0:T(8,128)(2,1)S(1)} %copy-done, bf16[512,1024]{1,0:T(8,128)(2,1)S(1)} %copy-done.1, f32[3,3,1024]{2,1,0:T(4,128)S(1)} %copy-done.3, bf16[1024,256]{1,0:T(8,128)(2,1)S(1)} %get-tuple-element.25.tail_ref, ...), custom_call_target="tpu_custom_call" | custom-call | flops 10000000 | bytes 5242880 | tf_op jit(solution)/shard_map/state/pallas_call | solution.py:305
  8.0 1.1 %collective-permute-done.halo_ref = bf16[24,1024]{1,0:T(8,128)(2,1)S(1)} collective-permute-done((bf16[24,1024]{1,0:T(8,128)(2,1)S(1)}, bf16[24,1024]{1,0:T(8,128)(2,1)S(1)}, u32[]{:S(2)}, u32[]{:S(2)}) %collective-permute-start) | collective-permute-done | bytes 49184 | tf_op jit(solution)/shard_map/ppermute | solution.py:275
  9.1 0.1 seam.1
  9.2 0.5 %collective-permute-start.1 = (f32[16,1024]{1,0:T(8,128)S(1)}, f32[16,1024]{1,0:T(8,128)S(1)}, u32[]{:S(2)}, u32[]{:S(2)}) collective-permute-start(f32[16,1024]{1,0:T(8,128)S(1)} %get-tuple-element.29.total_ref), channel_id=1, source_target_pairs={{0,4},{4,0},{8,12},{12,8},{16,20},{20,16},{24,28},{28,24},{1,5},{5... | collective-permute-start | bytes 196616 | tf_op jit(solution)/shard_map/ppermute | solution.py:348
  9.7 3.8 %collective-permute-done.1.got_ref.refs_4_ = f32[16,1024]{1,0:T(8,128)S(1)} collective-permute-done((f32[16,1024]{1,0:T(8,128)S(1)}, f32[16,1024]{1,0:T(8,128)S(1)}, u32[]{:S(2)}, u32[]{:S(2)}) %collective-permute-start.1) | collective-permute-done | bytes 65568 | tf_op jit(solution)/shard_map/ppermute | solution.py:348
  13.5 0.5 %collective-permute-start.2 = (f32[16,1024]{1,0:T(8,128)S(1)}, f32[16,1024]{1,0:T(8,128)S(1)}, u32[]{:S(2)}, u32[]{:S(2)}) collective-permute-start(f32[16,1024]{1,0:T(8,128)S(1)} %merge.2.total_ref), channel_id=1, source_target_pairs={{0,8},{4,12},{8,0},{12,4},{16,24},{20,28},{24,16},{28,20},{1,9},{5... | collective-permute-start | bytes 196616 | tf_op jit(solution)/shard_map/ppermute | solution.py:348
  14.1 3.8 %collective-permute-done.2.got_ref.refs_5_ = f32[16,1024]{1,0:T(8,128)S(1)} collective-permute-done((f32[16,1024]{1,0:T(8,128)S(1)}, f32[16,1024]{1,0:T(8,128)S(1)}, u32[]{:S(2)}, u32[]{:S(2)}) %collective-permute-start.2) | collective-permute-done | bytes 65568 | tf_op jit(solution)/shard_map/ppermute | solution.py:348
  17.9 1.7 %collective-permute-start.3 = (f32[16,1024]{1,0:T(8,128)S(1)}, f32[16,1024]{1,0:T(8,128)S(1)}, u32[]{:S(2)}, u32[]{:S(2)}) collective-permute-start(f32[16,1024]{1,0:T(8,128)S(1)} %merge.3), channel_id=1, source_target_pairs={{0,16},{4,20},{8,24},{12,28},{16,0},{20,4},{24,8},{28,12},{1,17},{... | collective-permute-start | bytes 196616 | tf_op jit(solution)/shard_map/ppermute | solution.py:348
  19.6 0.6 %query.1.query_ref.refs_0_ = f32[512,1024]{1,0:T(8,128)S(1)} custom-call(bf16[24,1024]{1,0:T(8,128)(2,1)S(1)} %collective-permute-done.halo_ref, bf16[512,1024]{1,0:T(8,128)(2,1)S(1)} %copy-done.2, f32[3,3,1024]{2,1,0:T(4,128)S(1)} %copy-done.3), custom_call_target="tpu_custom_call" | custom-call | flops 10000000 | bytes 4194304 | tf_op jit(solution)/shard_map/query/pallas_call | solution.py:333
  20.2 1.5 %near.5.refs_9_ = f32[512,384]{1,0:T(8,128)S(1)} custom-call(f32[512,1024]{1,0:T(8,128)S(1)} %get-tuple-element.31.gated_ref, f32[512,1024]{1,0:T(8,128)S(1)} %query.1.query_ref.refs_0_, f32[3,16,1024]{2,1,0:T(8,128)S(1)} %get-tuple-element.32.into_ref, f32[2,1024]{1,0:T(2,128)S(1)} %get-tuple-element.33.row_ref, f32[1,1024]{1,0:T(1,128)S(1)} %get-tuple-element.34.plain_ref, ...), custom_call_target="tpu_custom_call" | custom-call | flops 10000000 | bytes 4194304 | tf_op jit(solution)/shard_map/near/pallas_call | solution.py:353
  21.7 1.5 %near.4.refs_8_ = f32[512,384]{1,0:T(8,128)S(1)} custom-call(f32[512,1024]{1,0:T(8,128)S(1)} %get-tuple-element.31.gated_ref, f32[512,1024]{1,0:T(8,128)S(1)} %query.1.query_ref.refs_0_, f32[3,16,1024]{2,1,0:T(8,128)S(1)} %get-tuple-element.32.into_ref, f32[2,1024]{1,0:T(2,128)S(1)} %get-tuple-element.33.row_ref, f32[1,1024]{1,0:T(1,128)S(1)} %get-tuple-element.34.plain_ref, ...), custom_call_target="tpu_custom_call" | custom-call | flops 10000000 | bytes 4194304 | tf_op jit(solution)/shard_map/near/pallas_call | solution.py:353
  23.2 0.9 %near.3.refs_7_ = f32[512,256]{1,0:T(8,128)S(1)} custom-call(f32[512,1024]{1,0:T(8,128)S(1)} %get-tuple-element.31.gated_ref, f32[512,1024]{1,0:T(8,128)S(1)} %query.1.query_ref.refs_0_, f32[3,16,1024]{2,1,0:T(8,128)S(1)} %get-tuple-element.32.into_ref, f32[2,1024]{1,0:T(2,128)S(1)} %get-tuple-element.33.row_ref, f32[1,1024]{1,0:T(1,128)S(1)} %get-tuple-element.34.plain_ref, ...), custom_call_target="tpu_custom_call" | custom-call | flops 10000000 | bytes 4194304 | tf_op jit(solution)/shard_map/near/pallas_call | solution.py:353
  24.2 0.0 collective-permute-done.3.refs_6_
  24.2 2.0 %mix.1 = bf16[512,1024]{1,0:T(8,128)(2,1)} custom-call(f32[512,1024]{1,0:T(8,128)S(1)} %query.1.query_ref.refs_0_, f32[3,16,1024]{2,1,0:T(8,128)S(1)} %get-tuple-element.20.refs_1_, bf16[512,1024]{1,0:T(8,128)(2,1)S(1)} %get-tuple-element.21.lead_hi.refs_2_, bf16[512,1024]{1,0:T(8,128)(2,1)S(1)} %get-tuple-element.22.lead_lo.refs_3_, ...), custom_call_target="tpu_custom_call" | custom-call | tf_op jit(solution)/shard_map/mix/pallas_call | solution.py:373
  (9 shorter events, 0.0 us)
Async XLA Ops:
  0.0 5.2 %copy-start = (bf16[512,1024]{1,0:T(8,128)(2,1)S(1)}, bf16[512,1024]{1,0:T(8,128)(2,1)}, u32[]{:S(2)}) copy-start(bf16[512,1024]{1,0:T(8,128)(2,1)} %k_ref.5) | copy-start | bytes 3145732
  0.0 5.2 %copy-start.1 = (bf16[512,1024]{1,0:T(8,128)(2,1)S(1)}, bf16[512,1024]{1,0:T(8,128)(2,1)}, u32[]{:S(2)}) copy-start(bf16[512,1024]{1,0:T(8,128)(2,1)} %v_ref.5) | copy-start | bytes 3145732
  0.0 4.0 %copy-start.4 = (f32[16,64]{1,0:T(8,128)S(1)}, f32[16,64]{1,0:T(8,128)}, u32[]{:S(2)}) copy-start(f32[16,64]{1,0:T(8,128)} %res_ref.1) | copy-start | bytes 12292
  0.0 4.0 %copy-start.5 = (f32[16,64]{1,0:T(8,128)S(1)}, f32[16,64]{1,0:T(8,128)}, u32[]{:S(2)}) copy-start(f32[16,64]{1,0:T(8,128)} %decay_ref.1) | copy-start | bytes 12292
  0.0 4.0 %copy-start.6 = (f32[1,1024]{1,0:T(1,128)S(1)}, f32[1,1024]{1,0:T(1,128)}, u32[]{:S(2)}) copy-start(f32[1,1024]{1,0:T(1,128)} %skip_ref.1) | copy-start | bytes 12292
  0.0 5.2 %copy-start.3 = (f32[3,3,1024]{2,1,0:T(4,128)S(1)}, f32[3,3,1024]{2,1,0:T(4,128)}, u32[]{:S(2)}) copy-start(f32[3,3,1024]{2,1,0:T(4,128)} %sf_ref.5) | copy-start | bytes 110596
  1.0 8.1 %collective-permute-start = (bf16[24,1024]{1,0:T(8,128)(2,1)S(1)}, bf16[24,1024]{1,0:T(8,128)(2,1)S(1)}, u32[]{:S(2)}, u32[]{:S(2)}) collective-permute-start(bf16[24,1024]{1,0:T(8,128)(2,1)S(1)} %rim.1), channel_id=1, source_target_pairs={{0,4},{4,8},{8,12},{12,16},{16,20},{20,24},{24,28},{28,0},{1,5},{5... | collective-permute-start | bytes 147464 | tf_op jit(solution)/shard_map/ppermute | solution.py:275
  9.1 10.5 %copy-start.2 = (bf16[512,1024]{1,0:T(8,128)(2,1)S(1)}, bf16[512,1024]{1,0:T(8,128)(2,1)}, u32[]{:S(2)}) copy-start(bf16[512,1024]{1,0:T(8,128)(2,1)} %q_ref.3) | copy-start | bytes 3145732
  9.2 4.3 %collective-permute-start.1 = (f32[16,1024]{1,0:T(8,128)S(1)}, f32[16,1024]{1,0:T(8,128)S(1)}, u32[]{:S(2)}, u32[]{:S(2)}) collective-permute-start(f32[16,1024]{1,0:T(8,128)S(1)} %get-tuple-element.29.total_ref), channel_id=1, source_target_pairs={{0,4},{4,0},{8,12},{12,8},{16,20},{20,16},{24,28},{28,24},{1,5},{5... | collective-permute-start | bytes 196616 | tf_op jit(solution)/shard_map/ppermute | solution.py:348
  13.5 4.3 %collective-permute-start.2 = (f32[16,1024]{1,0:T(8,128)S(1)}, f32[16,1024]{1,0:T(8,128)S(1)}, u32[]{:S(2)}, u32[]{:S(2)}) collective-permute-start(f32[16,1024]{1,0:T(8,128)S(1)} %merge.2.total_ref), channel_id=1, source_target_pairs={{0,8},{4,12},{8,0},{12,4},{16,24},{20,28},{24,16},{28,20},{1,9},{5... | collective-permute-start | bytes 196616 | tf_op jit(solution)/shard_map/ppermute | solution.py:348
  17.9 6.3 %collective-permute-start.3 = (f32[16,1024]{1,0:T(8,128)S(1)}, f32[16,1024]{1,0:T(8,128)S(1)}, u32[]{:S(2)}, u32[]{:S(2)}) collective-permute-start(f32[16,1024]{1,0:T(8,128)S(1)} %merge.3), channel_id=1, source_target_pairs={{0,16},{4,20},{8,24},{12,28},{16,0},{20,4},{24,8},{28,12},{1,17},{... | collective-permute-start | bytes 196616 | tf_op jit(solution)/shard_map/ppermute | solution.py:348

commit v6 on v5

--- a/solution.py
+++ b/solution.py
@@ -60,12 +60,33 @@
         copy.wait()
 
 
-def table_kernel(res_ref, decay_ref, skip_ref, lead_hi, lead_lo, tail_ref, row_ref, plain_ref, hop_ref, seam_ref, span_ref, reach_ref):
+def steps_of(ranks):
+    bits = ranks.bit_length() - 1
+    return [(low, min(2, bits - low)) for low in range(0, bits, 2)]
+
+
+def gaps_of(ranks, length):
+    me = lax.axis_index("ctx")
+    table = []
+    for low, count in steps_of(ranks):
+        mine = (me >> low) % (1 << count)
+        inner = me % (1 << low) * length
+        size = length << low
+        row = []
+        for m in range(1 << count):
+            other = mine ^ m
+            reach = size * (mine - 1 - other) + inner
+            after = size * ((1 << count) - 1 - other)
+            row.append((other < mine, jnp.maximum(reach, 0).astype(F32), after.astype(F32)))
+        table.append(row)
+    return table
+
+
+def table_kernel(ranks, res_ref, decay_ref, skip_ref, lead_hi, lead_lo, tail_ref, row_ref, plain_ref, hop_ref, seam_ref, span_ref, reach_ref):
     length, width = lead_hi.shape
     modes = decay_ref.shape[0]
-    phases = reach_ref.shape[0]
+    gaps = gaps_of(ranks, length)
     plain_ref[...] = skip_ref[...]
-    me = lax.axis_index("ctx")
     lane = lax.broadcasted_iota(jnp.int32, (modes, LANES), 1)
     own = lane % modes == lax.broadcasted_iota(jnp.int32, (modes, LANES), 0)
     down = lax.broadcasted_iota(jnp.int32, (LANES, LANES), 0).astype(F32)
@@ -81,12 +102,15 @@
         hop_ref[:, at] = jnp.exp(-rates * float(LANES))
         for i in range(2):
             seam_ref[i, :, at] = jnp.exp(-rates * (LANES - 1.0 - i))
-        for b in range(phases):
-            upper = jnp.where((me >> b) % 2 == 1, 1.0, 0.0).astype(F32)
-            gap = (me % (1 << b) * length).astype(F32)
-            if b + 1 < phases:
-                span_ref[b, :, at] = jnp.exp(-rates * float(length << b))
-            reach_ref[b, :, at] = jnp.exp(-rates * gap) * upper
+        e = f = 0
+        for step, row in enumerate(gaps):
+            for m, (before, gap, after) in enumerate(row):
+                if m:
+                    reach_ref[e, :, at] = jnp.where(before, jnp.exp(-rates * gap), 0.0)
+                    e += 1
+                if step + 1 < len(gaps):
+                    span_ref[f, :, at] = jnp.exp(-rates * after)
+                    f += 1
         rate_rows = jnp.transpose(jnp.broadcast_to(rate, (LANES, LANES)))
         tail_ref[at, 0:LANES], tail_ref[at, LANES:] = split2(jnp.exp(-rate_rows * (LANES - 1.0 - along)))
         lead = gain * jnp.exp(-rate * (down + 1.0))
@@ -97,7 +121,7 @@
             lead = lead * hop
 
 
-def state_kernel(size, k_ref, v_ref, sf_ref, tail_ref, hop_ref, gated_ref, fresh_ref, enter_ref, kf, vf):
+def state_kernel(size, k_ref, v_ref, sf_ref, tail_ref, hop_ref, q_ref, gated_ref, fresh_ref, enter_ref, kf, vf):
     length, lanes = k_ref.shape
     modes = fresh_ref.shape[0]
     tile = pl.program_id(0)
@@ -156,12 +180,17 @@
     out_ref[...] = fresh_ref[...] + first
 
 
-def merge_kernel(b, total_ref, got_ref, span_ref, out_ref):
-    upper = (lax.axis_index("ctx") >> b) % 2 == 1
-    total, got = total_ref[...], got_ref[...]
-    late = jnp.where(upper, total, got)
-    early = jnp.where(upper, got, total)
-    out_ref[...] = late + span_ref[b] * early
+def merge_kernel(first, at, *refs):
+    span_ref, reach_ref, total_ref, next_ref = refs[-4:]
+    got = refs[1 : -4 if first == 0 else -5]
+    total = span_ref[at] * refs[0][...]
+    prefix = 0.0 if first == 0 else refs[-5][...]
+    for m, ref in enumerate(got):
+        value = ref[...]
+        total = total + span_ref[at + 1 + m] * value
+        prefix = prefix + reach_ref[first + m] * value
+    total_ref[...] = total
+    next_ref[...] = prefix
 
 
 def query_kernel(halo_ref, q_ref, sf_ref, out_ref, qf):
@@ -218,11 +247,12 @@
             out_ref[rows, to] = query_ref[rows, at] * near
 
 
-def mix_kernel(size, phases, parts, *refs):
+def mix_kernel(size, first, count, parts, *refs):
     query_ref, reach_ref, lead_hi, lead_lo = refs[:4]
-    gots = refs[4 : 4 + phases]
-    nears = refs[4 + phases : 4 + phases + parts]
-    out_ref, stage, sem = refs[4 + phases + parts :]
+    gots = refs[4 : 4 + count]
+    nears = refs[4 + count : 4 + count + parts]
+    prefix = refs[4 + count + parts : -3]
+    out_ref, stage, sem = refs[-3:]
     _, width = query_ref.shape
     modes = reach_ref.shape[1]
     where = []
@@ -236,9 +266,9 @@
     copies = []
     for tile in range(width // span):
         at = slice(tile * span, (tile + 1) * span)
-        state = reach_ref[0, :, at] * gots[0][:, at]
-        for b in range(1, phases):
-            state = state + reach_ref[b, :, at] * gots[b][:, at]
+        state = prefix[0][:, at] if prefix else 0.0
+        for m in range(count):
+            state = state + reach_ref[first + m, :, at] * gots[m][:, at]
         wide = jnp.where(block, jnp.concatenate([state] * groups, 0), 0.0)
         hi, lo = split2(wide)
         term = jnp.dot(lead_hi[:, at], hi, preferred_element_type=F32)
@@ -262,7 +292,9 @@
     modes, groups = residues.shape
     size = width // groups
     ranks = lax.axis_size("ctx")
-    phases = ranks.bit_length() - 1
+    steps = steps_of(ranks)
+    reaches = sum((1 << count) - 1 for _, count in steps)
+    spans = sum(1 << count for _, count in steps[:-1])
     rims = pl.pallas_call(
         rim_kernel,
         in_specs=[pl.BlockSpec(memory_space=pltpu.HBM)] * 3,
@@ -279,7 +311,7 @@
     scan_shape = lambda count: jax.ShapeDtypeStruct((count, modes, width), F32)
     row_shape = jax.ShapeDtypeStruct((modes, width), F32)
     lead_hi, lead_lo, tail, row, plain, hop, seam, span, reach = pl.pallas_call(
-        table_kernel,
+        functools.partial(table_kernel, ranks),
         in_specs=[VMEM] * 3,
         out_specs=[VMEM] * 9,
         out_shape=[
@@ -290,8 +322,8 @@
             jax.ShapeDtypeStruct((1, width), F32),
             row_shape,
             scan_shape(2),
-            scan_shape(max(1, phases - 1)),
-            scan_shape(phases),
+            scan_shape(max(1, spans)),
+            scan_shape(reaches),
         ],
         compiler_params=PARAMS,
         cost_estimate=pl.CostEstimate(flops=10**7, bytes_accessed=5 << 20, transcendentals=0),
@@ -311,6 +343,7 @@
             pl.BlockSpec((3, 3, tile), lambda j: (0, 0, j)),
             VMEM,
             VMEM,
+            VMEM,
         ],
         out_specs=[VMEM] * 3,
         out_shape=[gated_shape, row_shape, enter_shape],
@@ -318,7 +351,7 @@
         compiler_params=PARAMS,
         cost_estimate=pl.CostEstimate(flops=10**7, bytes_accessed=5 << 20, transcendentals=0),
         name="state",
-    )(key_in, value_in, short_filter, tail, hop)
+    )(key_in, value_in, short_filter, tail, hop, query_in)
     fresh, into, gated = pl.pallas_call(
         seam_kernel,
         in_specs=[VMEM] * 9,
@@ -341,12 +374,12 @@
         name="query",
     )(halo, query_in, short_filter)
 
-    unit = LANES if width // LANES >= 2 * phases else min(width, WIDE)
-    cuts = [width // unit * b // phases * unit for b in range(phases + 1)]
-    nears, gots, total = [], [], fresh
-    for b in range(phases):
-        got = lax.ppermute(total, "ctx", [(i, i ^ (1 << b)) for i in range(ranks)])
-        gots.append(got)
+    cuts = [width // LANES * b // len(steps) * LANES for b in range(len(steps) + 1)]
+    nears, total, prefix, first, at = [], fresh, [], 0, 0
+    for b, (low, count) in enumerate(steps):
+        gots = []
+        for m in range(1, 1 << count):
+            gots.append(lax.ppermute(total, "ctx", [(i, i ^ (m << low)) for i in range(ranks)]))
         lanes = cuts[b + 1] - cuts[b]
         if lanes:
             nears.append(
@@ -360,19 +393,22 @@
                     name="near",
                 )(gated, query, into, row, plain, lead_hi, lead_lo)
             )
-        if b + 1 < phases:
-            total = pl.pallas_call(
-                functools.partial(merge_kernel, b),
-                in_specs=[VMEM] * 3,
-                out_specs=VMEM,
-                out_shape=row_shape,
+        if b + 1 < len(steps):
+            total, ahead = pl.pallas_call(
+                functools.partial(merge_kernel, first, at),
+                in_specs=[VMEM] * (3 + len(gots) + len(prefix)),
+                out_specs=[VMEM] * 2,
+                out_shape=[row_shape] * 2,
                 compiler_params=PARAMS,
                 name="merge",
-            )(total, got, span)
+            )(total, *gots, *prefix, span, reach)
+            prefix = [ahead]
+            first += len(gots)
+            at += 1 << count
 
     return pl.pallas_call(
-        functools.partial(mix_kernel, size, phases, len(nears)),
-        in_specs=[VMEM] * (4 + phases + len(nears)),
+        functools.partial(mix_kernel, size, first, len(gots), len(nears)),
+        in_specs=[VMEM] * (4 + len(gots) + len(nears) + len(prefix)),
         out_specs=pl.BlockSpec(memory_space=pl.ANY),
         out_shape=jax.ShapeDtypeStruct((length, width), BF16),
         scratch_shapes=[
@@ -381,7 +417,7 @@
         ],
         compiler_params=PARAMS,
         name="mix",
-    )(query, reach, lead_hi, lead_lo, *gots, *nears)
+    )(query, reach, lead_hi, lead_lo, *gots, *nears, *prefix)
 
 
 def solution(mesh):

time: 26.4 us -> 24.6 us (0.932)
  waiting for transfers between devices: 8.72 us -> 4.81 us
  starting transfers between devices: 5.82 us -> 7.78 us
    ppermute x3 -> x4, waiting for transfers between devices: 7.6 us -> 3.73 us  [body(): lax.ppermute(total, 'ctx', [(i, i ^ m << low) for i in range(ranks)])]
    ppermute x3 -> x4, starting transfers between devices: 2.79 us -> 4.74 us  [body(): lax.ppermute(total, 'ctx', [(i, i ^ m << low) for i in range(ranks)])]
    pallas_call x3 -> x2, Pallas kernels: 3.92 us -> 4.06 us  [body(): pl.pallas_call(functools.partial(near_kernel, size, cuts[b]), in_specs=[V...]
    pallas_call x4 -> x3, Pallas kernels: 3.25 us -> 3.3 us  [the longest x1 2.03 us: body(): pl.pallas_call(functools.partial(mix_kernel, size, first, len(gots), len(...]
  transfers between devices with their start and end apart: 4 -> 5, of which waited for: 3 -> 4; matrix products, arithmetic and copies ran while one was open for 0% -> 0% of each run, Pallas kernels for 32% -> 35%
where the time goes in v6:
time: 24.6 us; the launch traced here: 24.4 us
  Pallas kernels  11.7 us (48%)
  starting transfers between devices  7.78 us (32%)
  waiting for transfers between devices  4.81 us (20%)
    ppermute x4, starting transfers between devices, body(): lax.ppermute(total, 'ctx', [(i, i ^ m << low) for i in range(ranks)])  4.74 us
    pallas_call x2, Pallas kernels, body(): pl.pallas_call(functools.partial(near_kernel, size, cuts[b]), in_specs=[V...  4.06 us
    ppermute x4, waiting for transfers between devices, body(): lax.ppermute(total, 'ctx', [(i, i ^ m << low) for i in range(ranks)])  3.73 us
    ppermute x1, starting transfers between devices, body(): lax.ppermute(rims, 'ctx', [(i, (i + 1) % ranks) for i in range(ranks)])  3.03 us
    pallas_call x1, Pallas kernels, body(): pl.pallas_call(functools.partial(state_kernel, size), grid=(width // tile...  2.74 us
    pallas_call x1, Pallas kernels, body(): pl.pallas_call(functools.partial(mix_kernel, size, first, len(gots), len(...  2.03 us
    pallas_call x1, Pallas kernels, body(): pl.pallas_call(functools.partial(table_kernel, ranks), in_specs=[VMEM] *...  1.22 us
    ppermute x1, waiting for transfers between devices, body(): lax.ppermute(rims, 'ctx', [(i, (i + 1) % ranks) for i in range(ranks)])  1.08 us
  transfers between devices with their start and end apart: 5, of which 4 were waited for; matrix products, arithmetic and copies ran while one was open for 0% of the time, Pallas kernels for 35%

profile of v6, /device:TPU:0, one launch (start us, length us, event | category | flops | bytes accessed | tf_op | source)
XLA Modules:
  0.0 24.4 jit_solution(9120278174330681423)
XLA Ops:
  0.0 0.0 copy-start.6
  0.0 0.0 copy-start.3
  0.0 0.9 %rim.1 = bf16[24,1024]{1,0:T(8,128)(2,1)S(1)} custom-call(bf16[512,1024]{1,0:T(8,128)(2,1)} %q_ref.5, bf16[512,1024]{1,0:T(8,128)(2,1)} %k_ref.5, bf16[512,1024]{1,0:T(8,128)(2,1)} %v_ref.5), custom_call_target="tpu_custom_call" | custom-call | tf_op jit(solution)/shard_map/rim/pallas_call | solution.py:298
  1.0 3.0 %collective-permute-start = (bf16[24,1024]{1,0:T(8,128)(2,1)S(1)}, bf16[24,1024]{1,0:T(8,128)(2,1)S(1)}, u32[]{:S(2)}, u32[]{:S(2)}) collective-permute-start(bf16[24,1024]{1,0:T(8,128)(2,1)S(1)} %rim.1), channel_id=1, source_target_pairs={{0,4},{4,8},{8,12},{12,16},{16,20},{20,24},{24,28},{28,0},{1,5},{5... | collective-permute-start | bytes 147464 | tf_op jit(solution)/shard_map/ppermute | solution.py:307
  4.0 1.2 %tables.1 = (bf16[512,1024]{1,0:T(8,128)(2,1)S(1)}, bf16[512,1024]{1,0:T(8,128)(2,1)S(1)}, bf16[1024,256]{1,0:T(8,128)(2,1)S(1)}, f32[2,1024]{1,0:T(2,128)S(1)},...) custom-call(f32[16,64]{1,0:T(8,128)S(1)} %copy-done.4, ...), custom_call_target="tpu_custom_call" | custom-call | flops 10000000 | bytes 5242880 | tf_op jit(solution)/shard_map/tables/pallas_call | solution.py:313
  5.2 0.0 copy-done
  5.2 0.0 copy-done.1
  5.3 0.0 copy-done.2
  5.3 0.0 copy-done.3
  5.3 2.7 %state.1 = (f32[512,1024]{1,0:T(8,128)S(1)}, f32[16,1024]{1,0:T(8,128)S(1)}, f32[3,16,1024]{2,1,0:T(8,128)S(1)}) custom-call(bf16[512,1024]{1,0:T(8,128)(2,1)S(1)} %copy-done.1, bf16[512,1024]{1,0:T(8,128)(2,1)S(1)} %copy-done.2, f32[3,3,1024]{2,1,0:T(4,128)S(1)} %copy-done.3, bf16[1024,256]{1,0:T(8,128)(2,1)S(1)} %get-tuple-element.27.tail_ref, ...), custom_call_target="tpu_custom_call" | custom-call | flops 10000000 | bytes 5242880 | tf_op jit(solution)/shard_map/state/pallas_call | solution.py:337
  8.0 1.1 %collective-permute-done.halo_ref = bf16[24,1024]{1,0:T(8,128)(2,1)S(1)} collective-permute-done((bf16[24,1024]{1,0:T(8,128)(2,1)S(1)}, bf16[24,1024]{1,0:T(8,128)(2,1)S(1)}, u32[]{:S(2)}, u32[]{:S(2)}) %collective-permute-start) | collective-permute-done | bytes 49184 | tf_op jit(solution)/shard_map/ppermute | solution.py:307
  9.1 0.1 seam.1
  9.2 0.6 %collective-permute-start.1 = (f32[16,1024]{1,0:T(8,128)S(1)}, f32[16,1024]{1,0:T(8,128)S(1)}, u32[]{:S(2)}, u32[]{:S(2)}) collective-permute-start(f32[16,1024]{1,0:T(8,128)S(1)} %get-tuple-element.31.refs_0_), channel_id=1, source_target_pairs={{0,4},{4,0},{8,12},{12,8},{16,20},{20,16},{24,28},{28,24},{1,5},{5... | collective-permute-start | bytes 196616 | tf_op jit(solution)/shard_map/ppermute | solution.py:382
  9.7 1.6 %collective-permute-start.2 = (f32[16,1024]{1,0:T(8,128)S(1)}, f32[16,1024]{1,0:T(8,128)S(1)}, u32[]{:S(2)}, u32[]{:S(2)}) collective-permute-start(f32[16,1024]{1,0:T(8,128)S(1)} %get-tuple-element.31.refs_0_), channel_id=1, source_target_pairs={{0,8},{4,12},{8,0},{12,4},{16,24},{20,28},{24,16},{28,20},{1,9},{5... | collective-permute-start | bytes 196616 | tf_op jit(solution)/shard_map/ppermute | solution.py:382
  11.3 1.4 %collective-permute-start.3 = (f32[16,1024]{1,0:T(8,128)S(1)}, f32[16,1024]{1,0:T(8,128)S(1)}, u32[]{:S(2)}, u32[]{:S(2)}) collective-permute-start(f32[16,1024]{1,0:T(8,128)S(1)} %get-tuple-element.31.refs_0_), channel_id=1, source_target_pairs={{0,12},{4,8},{8,4},{12,0},{16,28},{20,24},{24,20},{28,16},{1,13},{... | collective-permute-start | bytes 196616 | tf_op jit(solution)/shard_map/ppermute | solution.py:382
  12.7 0.8 %collective-permute-done.1.refs_1_ = f32[16,1024]{1,0:T(8,128)S(1)} collective-permute-done((f32[16,1024]{1,0:T(8,128)S(1)}, f32[16,1024]{1,0:T(8,128)S(1)}, u32[]{:S(2)}, u32[]{:S(2)}) %collective-permute-start.1) | collective-permute-done | bytes 65568 | tf_op jit(solution)/shard_map/ppermute | solution.py:382
  13.5 0.7 %collective-permute-done.2.refs_2_ = f32[16,1024]{1,0:T(8,128)S(1)} collective-permute-done((f32[16,1024]{1,0:T(8,128)S(1)}, f32[16,1024]{1,0:T(8,128)S(1)}, u32[]{:S(2)}, u32[]{:S(2)}) %collective-permute-start.2) | collective-permute-done | bytes 65568 | tf_op jit(solution)/shard_map/ppermute | solution.py:382
  14.2 2.3 %collective-permute-done.3.refs_3_ = f32[16,1024]{1,0:T(8,128)S(1)} collective-permute-done((f32[16,1024]{1,0:T(8,128)S(1)}, f32[16,1024]{1,0:T(8,128)S(1)}, u32[]{:S(2)}, u32[]{:S(2)}) %collective-permute-start.3) | collective-permute-done | bytes 65568 | tf_op jit(solution)/shard_map/ppermute | solution.py:382
  16.5 1.2 %collective-permute-start.4 = (f32[16,1024]{1,0:T(8,128)S(1)}, f32[16,1024]{1,0:T(8,128)S(1)}, u32[]{:S(2)}, u32[]{:S(2)}) collective-permute-start(f32[16,1024]{1,0:T(8,128)S(1)} %get-tuple-element.33), channel_id=1, source_target_pairs={{0,16},{4,20},{8,24},{12,28},{16,0},{20,4},{24,8},{28,12},{1,17},{... | collective-permute-start | bytes 196616 | tf_op jit(solution)/shard_map/ppermute | solution.py:382
  17.7 0.6 %query.1.query_ref.refs_0_ = f32[512,1024]{1,0:T(8,128)S(1)} custom-call(bf16[24,1024]{1,0:T(8,128)(2,1)S(1)} %collective-permute-done.halo_ref, bf16[512,1024]{1,0:T(8,128)(2,1)S(1)} %copy-done, f32[3,3,1024]{2,1,0:T(4,128)S(1)} %copy-done.3), custom_call_target="tpu_custom_call" | custom-call | flops 10000000 | bytes 4194304 | tf_op jit(solution)/shard_map/query/pallas_call | solution.py:366
  18.3 2.0 %near.3.refs_6_ = f32[512,512]{1,0:T(8,128)S(1)} custom-call(f32[512,1024]{1,0:T(8,128)S(1)} %get-tuple-element.34.gated_ref, f32[512,1024]{1,0:T(8,128)S(1)} %query.1.query_ref.refs_0_, f32[3,16,1024]{2,1,0:T(8,128)S(1)} %get-tuple-element.35.into_ref, f32[2,1024]{1,0:T(2,128)S(1)} %get-tuple-element.36.row_ref, f32[1,1024]{1,0:T(1,128)S(1)} %get-tuple-element.37.plain_ref, ...), custom_call_target="tpu_custom_call" | custom-call | flops 10000000 | bytes 4194304 | tf_op jit(solution)/shard_map/near/pallas_call | solution.py:386
  20.4 2.0 %near.2.refs_5_ = f32[512,512]{1,0:T(8,128)S(1)} custom-call(f32[512,1024]{1,0:T(8,128)S(1)} %get-tuple-element.34.gated_ref, f32[512,1024]{1,0:T(8,128)S(1)} %query.1.query_ref.refs_0_, f32[3,16,1024]{2,1,0:T(8,128)S(1)} %get-tuple-element.35.into_ref, f32[2,1024]{1,0:T(2,128)S(1)} %get-tuple-element.36.row_ref, f32[1,1024]{1,0:T(1,128)S(1)} %get-tuple-element.37.plain_ref, ...), custom_call_target="tpu_custom_call" | custom-call | flops 10000000 | bytes 4194304 | tf_op jit(solution)/shard_map/near/pallas_call | solution.py:386
  22.4 0.0 collective-permute-done.4.refs_4_
  22.4 2.0 %mix.1 = bf16[512,1024]{1,0:T(8,128)(2,1)} custom-call(f32[512,1024]{1,0:T(8,128)S(1)} %query.1.query_ref.refs_0_, f32[4,16,1024]{2,1,0:T(8,128)S(1)} %get-tuple-element.22.refs_5_.refs_1_, bf16[512,1024]{1,0:T(8,128)(2,1)S(1)} %get-tuple-element.23.lead_hi.refs_2_, bf16[512,1024]{1,0:T(8,128)(2,1)S(1)} %get-tuple-element.24.lead_lo.refs_3_, ...), custom_call_target="tpu_custom_call" | custom-call | tf_op jit(solution)/shard_map/mix/pallas_call | solution.py:409
  (9 shorter events, 0.1 us)
Async XLA Ops:
  0.0 5.2 %copy-start = (bf16[512,1024]{1,0:T(8,128)(2,1)S(1)}, bf16[512,1024]{1,0:T(8,128)(2,1)}, u32[]{:S(2)}) copy-start(bf16[512,1024]{1,0:T(8,128)(2,1)} %q_ref.5) | copy-start | bytes 3145732
  0.0 5.2 %copy-start.1 = (bf16[512,1024]{1,0:T(8,128)(2,1)S(1)}, bf16[512,1024]{1,0:T(8,128)(2,1)}, u32[]{:S(2)}) copy-start(bf16[512,1024]{1,0:T(8,128)(2,1)} %k_ref.5) | copy-start | bytes 3145732
  0.0 5.2 %copy-start.2 = (bf16[512,1024]{1,0:T(8,128)(2,1)S(1)}, bf16[512,1024]{1,0:T(8,128)(2,1)}, u32[]{:S(2)}) copy-start(bf16[512,1024]{1,0:T(8,128)(2,1)} %v_ref.5) | copy-start | bytes 3145732
  0.0 4.0 %copy-start.4 = (f32[16,64]{1,0:T(8,128)S(1)}, f32[16,64]{1,0:T(8,128)}, u32[]{:S(2)}) copy-start(f32[16,64]{1,0:T(8,128)} %res_ref.1) | copy-start | bytes 12292
  0.0 4.0 %copy-start.5 = (f32[16,64]{1,0:T(8,128)S(1)}, f32[16,64]{1,0:T(8,128)}, u32[]{:S(2)}) copy-start(f32[16,64]{1,0:T(8,128)} %decay_ref.1) | copy-start | bytes 12292
  0.0 4.0 %copy-start.6 = (f32[1,1024]{1,0:T(1,128)S(1)}, f32[1,1024]{1,0:T(1,128)}, u32[]{:S(2)}) copy-start(f32[1,1024]{1,0:T(1,128)} %skip_ref.1) | copy-start | bytes 12292
  0.0 5.2 %copy-start.3 = (f32[3,3,1024]{2,1,0:T(4,128)S(1)}, f32[3,3,1024]{2,1,0:T(4,128)}, u32[]{:S(2)}) copy-start(f32[3,3,1024]{2,1,0:T(4,128)} %sf_ref.5) | copy-start | bytes 110596
  1.0 8.1 %collective-permute-start = (bf16[24,1024]{1,0:T(8,128)(2,1)S(1)}, bf16[24,1024]{1,0:T(8,128)(2,1)S(1)}, u32[]{:S(2)}, u32[]{:S(2)}) collective-permute-start(bf16[24,1024]{1,0:T(8,128)(2,1)S(1)} %rim.1), channel_id=1, source_target_pairs={{0,4},{4,8},{8,12},{12,16},{16,20},{20,24},{24,28},{28,0},{1,5},{5... | collective-permute-start | bytes 147464 | tf_op jit(solution)/shard_map/ppermute | solution.py:307
  9.2 4.3 %collective-permute-start.1 = (f32[16,1024]{1,0:T(8,128)S(1)}, f32[16,1024]{1,0:T(8,128)S(1)}, u32[]{:S(2)}, u32[]{:S(2)}) collective-permute-start(f32[16,1024]{1,0:T(8,128)S(1)} %get-tuple-element.31.refs_0_), channel_id=1, source_target_pairs={{0,4},{4,0},{8,12},{12,8},{16,20},{20,16},{24,28},{28,24},{1,5},{5... | collective-permute-start | bytes 196616 | tf_op jit(solution)/shard_map/ppermute | solution.py:382
  9.7 4.5 %collective-permute-start.2 = (f32[16,1024]{1,0:T(8,128)S(1)}, f32[16,1024]{1,0:T(8,128)S(1)}, u32[]{:S(2)}, u32[]{:S(2)}) collective-permute-start(f32[16,1024]{1,0:T(8,128)S(1)} %get-tuple-element.31.refs_0_), channel_id=1, source_target_pairs={{0,8},{4,12},{8,0},{12,4},{16,24},{20,28},{24,16},{28,20},{1,9},{5... | collective-permute-start | bytes 196616 | tf_op jit(solution)/shard_map/ppermute | solution.py:382
  11.3 5.2 %collective-permute-start.3 = (f32[16,1024]{1,0:T(8,128)S(1)}, f32[16,1024]{1,0:T(8,128)S(1)}, u32[]{:S(2)}, u32[]{:S(2)}) collective-permute-start(f32[16,1024]{1,0:T(8,128)S(1)} %get-tuple-element.31.refs_0_), channel_id=1, source_target_pairs={{0,12},{4,8},{8,4},{12,0},{16,28},{20,24},{24,20},{28,16},{1,13},{... | collective-permute-start | bytes 196616 | tf_op jit(solution)/shard_map/ppermute | solution.py:382
  16.5 5.9 %collective-permute-start.4 = (f32[16,1024]{1,0:T(8,128)S(1)}, f32[16,1024]{1,0:T(8,128)S(1)}, u32[]{:S(2)}, u32[]{:S(2)}) collective-permute-start(f32[16,1024]{1,0:T(8,128)S(1)} %get-tuple-element.33), channel_id=1, source_target_pairs={{0,16},{4,20},{8,24},{12,28},{16,0},{20,4},{24,8},{28,12},{1,17},{... | collective-permute-start | bytes 196616 | tf_op jit(solution)/shard_map/ppermute | solution.py:382

commit v7 on v6

--- a/solution.py
+++ b/solution.py
@@ -11,7 +11,6 @@
 LANES = 128
 WIDE = 256
 SUB = 8
-RIM = 8
 F32 = jnp.float32
 BF16 = jnp.bfloat16
 VMEM = pl.BlockSpec(memory_space=pltpu.VMEM)
@@ -21,6 +20,15 @@
 def split2(x):
     hi = x.astype(BF16)
     return hi, (x - hi.astype(F32)).astype(BF16)
+
+
+def pair(hi, lo):
+    return jnp.concatenate([jnp.concatenate([hi, lo], 1), jnp.concatenate([hi, jnp.zeros_like(lo)], 1)], 0)
+
+
+def dot3(left, right):
+    out = jnp.dot(left, right, preferred_element_type=F32)
+    return out[:, :LANES] + out[:, LANES:]
 
 
 def expand(table, first, lanes, size):
@@ -50,14 +58,22 @@
     return out + taps[2] * ref[at - 2 : at - 2 + count]
 
 
-def rim_kernel(q_ref, k_ref, v_ref, out_ref, sem):
-    copies = []
-    for i, ref in enumerate((q_ref, k_ref, v_ref)):
-        rim = ref.at[ref.shape[0] - RIM :]
-        copies.append(pltpu.make_async_copy(rim, out_ref.at[i * RIM : (i + 1) * RIM], sem.at[i]))
-        copies[i].start()
+def rim_kernel(q_ref, k_ref, v_ref, *refs):
+    small, out_ref, loaded, rows, sem = refs[:3], refs[3], refs[4:7], refs[7], refs[8]
+    pairs = [(ref.at[ref.shape[0] - SUB :], rows.at[i]) for i, ref in enumerate((q_ref, k_ref, v_ref))]
+    pairs += list(zip(small, loaded))
+    copies = [pltpu.make_async_copy(src, dst, sem.at[i]) for i, (src, dst) in enumerate(pairs)]
+    for copy in copies:
+        copy.start()
     for copy in copies:
         copy.wait()
+    ends = [rows[i].astype(F32)[SUB - 2 :] for i in range(3)]
+    out_ref[...] = jnp.concatenate(ends + ends[:1], 0).astype(BF16)
+
+
+def past(halo_ref, which, at=slice(None)):
+    keep = jnp.where(lax.axis_index("ctx") > 0, 1.0, 0.0).astype(F32)
+    return halo_ref[:, at].astype(F32)[2 * which : 2 * which + 2] * keep
 
 
 def steps_of(ranks):
@@ -82,8 +98,8 @@
     return table
 
 
-def table_kernel(ranks, res_ref, decay_ref, skip_ref, lead_hi, lead_lo, tail_ref, row_ref, plain_ref, hop_ref, seam_ref, span_ref, reach_ref):
-    length, width = lead_hi.shape
+def table_kernel(ranks, res_ref, decay_ref, skip_ref, lead_ref, tail_ref, row_ref, plain_ref, hop_ref, seam_ref, span_ref, reach_ref):
+    length, width = lead_ref.shape[0], skip_ref.shape[1]
     modes = decay_ref.shape[0]
     gaps = gaps_of(ranks, length)
     plain_ref[...] = skip_ref[...]
@@ -117,7 +133,8 @@
         hop = jnp.exp(-rate * float(LANES))
         for c in range(length // LANES):
             rows = slice(c * LANES, (c + 1) * LANES)
-            lead_hi[rows, at], lead_lo[rows, at] = split2(lead)
+            mid = 2 * tile * LANES + LANES
+            lead_ref[rows, mid - LANES : mid], lead_ref[rows, mid : mid + LANES] = split2(lead)
             lead = lead * hop
 
 
@@ -137,7 +154,7 @@
         kt = [sf_ref[1, i : i + 1, at] for i in range(3)]
         vt = [sf_ref[2, i : i + 1, at] for i in range(3)]
         hop = hop_ref[:, own]
-        tail, tail_hi = tail_ref[own, :], tail_ref[own, 0:LANES]
+        tail = tail_ref[own, :]
         total = jnp.zeros((modes, LANES), F32)
         for c in range(length // LANES):
             his, los = [], []
@@ -152,8 +169,7 @@
                 hi, lo = split2(gated)
                 his.append(hi)
                 los.append(lo)
-            out = jnp.dot(tail, jnp.concatenate(his + his, 0), preferred_element_type=F32)
-            out = out + jnp.dot(tail_hi, jnp.concatenate(los, 0), preferred_element_type=F32)
+            out = dot3(tail, pair(jnp.concatenate(his, 0), jnp.concatenate(los, 0)))
             fresh = jnp.zeros((modes, LANES), F32)
             for g in range(LANES // size):
                 fresh = jnp.where(row == g, out[g * modes : (g + 1) * modes], fresh)
@@ -164,9 +180,8 @@
 
 
 def seam_kernel(halo_ref, k_ref, v_ref, sf_ref, seam_ref, hop_ref, fresh_ref, enter_ref, gated_ref, out_ref, into_ref, whole_ref, kf, vf):
-    keep = jnp.where(lax.axis_index("ctx") > 0, 1.0, 0.0).astype(F32)
-    kf[0:SUB] = halo_ref[RIM : 2 * RIM].astype(F32) * keep
-    vf[0:SUB] = halo_ref[2 * RIM : 3 * RIM].astype(F32) * keep
+    kf[SUB - 2 : SUB] = past(halo_ref, 1)
+    vf[SUB - 2 : SUB] = past(halo_ref, 2)
     kf[SUB:] = k_ref[0:SUB].astype(F32)
     vf[SUB:] = v_ref[0:SUB].astype(F32)
     kt = [sf_ref[1, i : i + 1, :] for i in range(3)]
@@ -195,11 +210,10 @@
 
 def query_kernel(halo_ref, q_ref, sf_ref, out_ref, qf):
     length, width = q_ref.shape
-    keep = jnp.where(lax.axis_index("ctx") > 0, 1.0, 0.0).astype(F32)
     for lane in range(0, width, LANES):
         at = slice(lane, lane + LANES)
         taps = [sf_ref[0, i : i + 1, at] for i in range(3)]
-        qf[0:SUB] = halo_ref[0:RIM, at].astype(F32) * keep
+        qf[SUB - 2 : SUB] = past(halo_ref, 0, at)
         piece = 64
         for start in range(0, length, piece):
             rows = slice(start, start + piece)
@@ -207,7 +221,7 @@
             out_ref[rows, at] = short3(qf, start, piece, taps)
 
 
-def near_kernel(size, first, gated_ref, query_ref, into_ref, row_ref, plain_ref, lead_hi, lead_lo, out_ref):
+def near_kernel(size, first, gated_ref, query_ref, into_ref, row_ref, plain_ref, lead_ref, out_ref):
     length, lanes = out_ref.shape
     modes = into_ref.shape[1]
     chunks = length // LANES
@@ -232,54 +246,46 @@
             hi, lo = split2(jnp.where(causal, toe, 0.0))
             xh = jnp.concatenate([h[rows] for h, _ in halves], 0)
             xl = jnp.concatenate([l[rows] for _, l in halves], 0)
-            out = jnp.dot(jnp.concatenate([xh, xl], 1), jnp.concatenate([hi, hi], 0), preferred_element_type=F32)
-            outs.append(out + jnp.dot(xh, lo, preferred_element_type=F32))
-        lead = jnp.concatenate([lead_hi[0:LANES, at], lead_lo[0:LANES, at]], 1)
+            outs.append(dot3(jnp.concatenate([xh, xl], 1), pair(hi, lo)))
+        lead = lead_ref[0:LANES, 2 * at.start : 2 * at.stop]
         for c in range(chunks):
             rows = slice(c * LANES, (c + 1) * LANES)
             near = jnp.transpose(jnp.concatenate([o[c * size : (c + 1) * size] for o in outs], 0))
             near = near + plain_ref[:, at] * gated_ref[rows, at]
             if c:
                 wide = jnp.where(block, jnp.concatenate([into_ref[c - 1, :, at]] * groups, 0), 0.0)
-                hi, lo = split2(wide)
-                near = near + jnp.dot(lead, jnp.concatenate([hi, hi], 0), preferred_element_type=F32)
-                near = near + jnp.dot(lead[:, :LANES], lo, preferred_element_type=F32)
+                near = near + dot3(lead, pair(*split2(wide)))
             out_ref[rows, to] = query_ref[rows, at] * near
 
 
 def mix_kernel(size, first, count, parts, *refs):
-    query_ref, reach_ref, lead_hi, lead_lo = refs[:4]
-    gots = refs[4 : 4 + count]
-    nears = refs[4 + count : 4 + count + parts]
-    prefix = refs[4 + count + parts : -3]
+    query_ref, reach_ref, lead_ref = refs[:3]
+    gots = refs[3 : 3 + count]
+    nears = refs[3 + count : 3 + count + parts]
+    prefix = refs[3 + count + parts : -3]
     out_ref, stage, sem = refs[-3:]
-    _, width = query_ref.shape
+    length, width = query_ref.shape
     modes = reach_ref.shape[1]
     where = []
     for ref in nears:
         where += [(ref, c) for c in range(0, ref.shape[1], LANES)]
-    span = min(WIDE, width)
-    groups = span // size
-    row = lax.broadcasted_iota(jnp.int32, (groups * modes, span), 0)
-    col = lax.broadcasted_iota(jnp.int32, (groups * modes, span), 1)
+    groups = LANES // size
+    row = lax.broadcasted_iota(jnp.int32, (groups * modes, LANES), 0)
+    col = lax.broadcasted_iota(jnp.int32, (groups * modes, LANES), 1)
     block = row // modes == col // size
     copies = []
-    for tile in range(width // span):
-        at = slice(tile * span, (tile + 1) * span)
+    for tile in range(width // LANES):
+        at = slice(tile * LANES, (tile + 1) * LANES)
         state = prefix[0][:, at] if prefix else 0.0
         for m in range(count):
             state = state + reach_ref[first + m, :, at] * gots[m][:, at]
         wide = jnp.where(block, jnp.concatenate([state] * groups, 0), 0.0)
-        hi, lo = split2(wide)
-        term = jnp.dot(lead_hi[:, at], hi, preferred_element_type=F32)
-        term = term + jnp.dot(lead_lo[:, at], hi, preferred_element_type=F32)
-        term = term + jnp.dot(lead_hi[:, at], lo, preferred_element_type=F32)
-        for half in range(span // LANES):
-            lane = tile * span + half * LANES
-            cut = slice(lane, lane + LANES)
-            near, c = where[lane // LANES]
-            far = query_ref[:, cut] * term[:, half * LANES : (half + 1) * LANES]
-            stage[:, cut] = (near[:, c : c + LANES] + far).astype(BF16)
+        right = pair(*split2(wide))
+        near, c = where[tile]
+        for start in range(0, length, LANES):
+            rows = slice(start, start + LANES)
+            term = dot3(lead_ref[rows, 2 * at.start : 2 * at.stop], right)
+            stage[rows, at] = (near[rows, c : c + LANES] + query_ref[rows, at] * term).astype(BF16)
         copy = pltpu.make_async_copy(stage.at[:, at], out_ref.at[:, at], sem.at[tile])
         copy.start()
         copies.append(copy)
@@ -295,27 +301,28 @@
     steps = steps_of(ranks)
     reaches = sum((1 << count) - 1 for _, count in steps)
     spans = sum(1 << count for _, count in steps[:-1])
-    rims = pl.pallas_call(
+    small = (residues, decay_rate, skip_gain)
+    sources = [pltpu.with_memory_space_constraint(a, pltpu.HBM) for a in (query_in, key_in, value_in) + small]
+    rims, residues, decay_rate, skip_gain = pl.pallas_call(
         rim_kernel,
-        in_specs=[pl.BlockSpec(memory_space=pltpu.HBM)] * 3,
-        out_specs=VMEM,
-        out_shape=jax.ShapeDtypeStruct((3 * RIM, width), BF16),
-        scratch_shapes=[pltpu.SemaphoreType.DMA((3,))],
-        compiler_params=pltpu.CompilerParams(vmem_limit_bytes=4 << 20),
+        in_specs=[pl.BlockSpec(memory_space=pltpu.HBM)] * 6,
+        out_specs=[VMEM] * 4,
+        out_shape=[jax.ShapeDtypeStruct((SUB, width), BF16)] + [jax.ShapeDtypeStruct(a.shape, F32) for a in small],
+        scratch_shapes=[pltpu.VMEM((3, SUB, width), BF16), pltpu.SemaphoreType.DMA((6,))],
+        compiler_params=PARAMS,
         name="rim",
-    )(*[pltpu.with_memory_space_constraint(a, pltpu.HBM) for a in (query_in, key_in, value_in)])
+    )(*sources)
     halo = lax.ppermute(rims, "ctx", [(i, (i + 1) % ranks) for i in range(ranks)])
 
-    lead_shape = jax.ShapeDtypeStruct((length, width), BF16)
+    lead_shape = jax.ShapeDtypeStruct((length, 2 * width), BF16)
     tail_shape = jax.ShapeDtypeStruct((width, 2 * LANES), BF16)
     scan_shape = lambda count: jax.ShapeDtypeStruct((count, modes, width), F32)
     row_shape = jax.ShapeDtypeStruct((modes, width), F32)
-    lead_hi, lead_lo, tail, row, plain, hop, seam, span, reach = pl.pallas_call(
+    lead, tail, row, plain, hop, seam, span, reach = pl.pallas_call(
         functools.partial(table_kernel, ranks),
         in_specs=[VMEM] * 3,
-        out_specs=[VMEM] * 9,
+        out_specs=[VMEM] * 8,
         out_shape=[
-            lead_shape,
             lead_shape,
             tail_shape,
             jax.ShapeDtypeStruct((2, width), F32),
@@ -385,13 +392,13 @@
             nears.append(
                 pl.pallas_call(
                     functools.partial(near_kernel, size, cuts[b]),
-                    in_specs=[VMEM] * 7,
+                    in_specs=[VMEM] * 6,
                     out_specs=VMEM,
                     out_shape=jax.ShapeDtypeStruct((length, lanes), F32),
                     compiler_params=PARAMS,
                     cost_estimate=pl.CostEstimate(flops=10**7, bytes_accessed=4 << 20, transcendentals=0),
                     name="near",
-                )(gated, query, into, row, plain, lead_hi, lead_lo)
+                )(gated, query, into, row, plain, lead)
             )
         if b + 1 < len(steps):
             total, ahead = pl.pallas_call(
@@ -408,16 +415,16 @@
 
     return pl.pallas_call(
         functools.partial(mix_kernel, size, first, len(gots), len(nears)),
-        in_specs=[VMEM] * (4 + len(gots) + len(nears) + len(prefix)),
+        in_specs=[VMEM] * (3 + len(gots) + len(nears) + len(prefix)),
         out_specs=pl.BlockSpec(memory_space=pl.ANY),
         out_shape=jax.ShapeDtypeStruct((length, width), BF16),
         scratch_shapes=[
             pltpu.VMEM((length, width), BF16),
-            pltpu.SemaphoreType.DMA((max(1, width // WIDE),)),
+            pltpu.SemaphoreType.DMA((width // LANES,)),
         ],
         compiler_params=PARAMS,
         name="mix",
-    )(query, reach, lead_hi, lead_lo, *gots, *nears, *prefix)
+    )(query, reach, lead, *gots, *nears, *prefix)
 
 
 def solution(mesh):

time: 24.6 us -> 24.2 us (0.984)
  Pallas kernels: 11.7 us -> 11.3 us
    pallas_call x1, Pallas kernels: 2.03 us -> 1.51 us  [body(): pl.pallas_call(functools.partial(mix_kernel, size, first, len(gots), len(...]
  transfers between devices with their start and end apart: 5 -> 5, of which waited for: 4 -> 4; matrix products, arithmetic and copies ran while one was open for 0% -> 0% of each run, Pallas kernels for 35% -> 36%
where the time goes in v7:
time: 24.2 us; the launch traced here: 24 us
  Pallas kernels  11.3 us (47%)
  starting transfers between devices  7.77 us (32%)
  waiting for transfers between devices  4.82 us (20%)
    ppermute x4, starting transfers between devices, body(): lax.ppermute(total, 'ctx', [(i, i ^ m << low) for i in range(ranks)])  4.74 us
    pallas_call x2, Pallas kernels, body(): pl.pallas_call(functools.partial(near_kernel, size, cuts[b]), in_specs=[V...  4.3 us
    ppermute x4, waiting for transfers between devices, body(): lax.ppermute(total, 'ctx', [(i, i ^ m << low) for i in range(ranks)])  3.94 us
    ppermute x1, starting transfers between devices, body(): lax.ppermute(rims, 'ctx', [(i, (i + 1) % ranks) for i in range(ranks)])  3.03 us
    pallas_call x1, Pallas kernels, body(): pl.pallas_call(functools.partial(state_kernel, size), grid=(width // tile...  2.66 us
    pallas_call x1, Pallas kernels, body(): pl.pallas_call(functools.partial(mix_kernel, size, first, len(gots), len(...  1.51 us
    pallas_call x1, Pallas kernels, body(): pl.pallas_call(functools.partial(table_kernel, ranks), in_specs=[VMEM] *...  1.17 us
    pallas_call x1, Pallas kernels, body(): pl.pallas_call(rim_kernel, in_specs=[pl.BlockSpec(memory_space=pltpu.HBM)...  0.98 us
  transfers between devices with their start and end apart: 5, of which 4 were waited for; matrix products, arithmetic and copies ran while one was open for 0% of the time, Pallas kernels for 36%

profile of v7, /device:TPU:0, one launch (start us, length us, event | category | flops | bytes accessed | tf_op | source)
XLA Modules:
  0.0 24.0 jit_solution(6196714256273091074)
XLA Ops:
  0.0 0.0 copy-start
  0.0 0.0 copy-start.1
  0.0 1.0 %rim.1 = (bf16[8,1024]{1,0:T(8,128)(2,1)S(1)}, f32[16,64]{1,0:T(8,128)S(1)}, f32[16,64]{1,0:T(8,128)S(1)}, f32[1,1024]{1,0:T(1,128)S(1)}) custom-call(bf16[512,1024]{1,0:T(8,128)(2,1)} %q_ref.5, bf16[512,1024]{1,0:T(8,128)(2,1)} %k_ref.5, bf16[512,1024]{1,0:T(8,128)(2,1)} %v_ref.5, f32[16,64]{1,0:T(8,128)} %refs_0_.1, f32[16,64]{1,0:T(8,128)} %refs_1_.1, ...), custom_call_target="tpu_custom_call" | custom-call | tf_op jit(solution)/shard_map/rim/pallas_call | solution.py:306
  1.0 3.0 %collective-permute-start = (bf16[8,1024]{1,0:T(8,128)(2,1)S(1)}, bf16[8,1024]{1,0:T(8,128)(2,1)S(1)}, u32[]{:S(2)}, u32[]{:S(2)}) collective-permute-start(bf16[8,1024]{1,0:T(8,128)(2,1)S(1)} %get-tuple-element.25), channel_id=1, source_target_pairs={{0,4},{4,8},{8,12},{12,16},{16,20},{20,24},{24,28},{28,0},{1,5},{5... | collective-permute-start | bytes 49160 | tf_op jit(solution)/shard_map/ppermute | solution.py:315
  4.0 1.2 %tables.1 = (bf16[512,2048]{1,0:T(8,128)(2,1)S(1)}, bf16[1024,256]{1,0:T(8,128)(2,1)S(1)}, f32[2,1024]{1,0:T(2,128)S(1)}, f32[1,1024]{1,0:T(1,128)S(1)}, f32[16,...) custom-call(f32[16,64]{1,0:T(8,128)S(1)} %get-tuple-element.26.res_ref, ...), custom_call_target="tpu_custom_call" | custom-call | flops 10000000 | bytes 5242880 | tf_op jit(solution)/shard_map/tables/pallas_call | solution.py:321
  5.2 0.0 copy-done
  5.2 0.0 copy-done.1
  5.2 0.0 copy-done.2
  5.2 0.0 copy-done.3
  5.2 2.7 %state.1 = (f32[512,1024]{1,0:T(8,128)S(1)}, f32[16,1024]{1,0:T(8,128)S(1)}, f32[3,16,1024]{2,1,0:T(8,128)S(1)}) custom-call(bf16[512,1024]{1,0:T(8,128)(2,1)S(1)} %copy-done.1, bf16[512,1024]{1,0:T(8,128)(2,1)S(1)} %copy-done.2, f32[3,3,1024]{2,1,0:T(4,128)S(1)} %copy-done.3, bf16[1024,256]{1,0:T(8,128)(2,1)S(1)} %get-tuple-element.33.tail_ref, ...), custom_call_target="tpu_custom_call" | custom-call | flops 10000000 | bytes 5242880 | tf_op jit(solution)/shard_map/state/pallas_call | solution.py:344
  7.9 0.9 %collective-permute-done.halo_ref = bf16[8,1024]{1,0:T(8,128)(2,1)S(1)} collective-permute-done((bf16[8,1024]{1,0:T(8,128)(2,1)S(1)}, bf16[8,1024]{1,0:T(8,128)(2,1)S(1)}, u32[]{:S(2)}, u32[]{:S(2)}) %collective-permute-start) | collective-permute-done | bytes 16416 | tf_op jit(solution)/shard_map/ppermute | solution.py:315
  8.8 0.1 seam.1
  8.9 0.8 %collective-permute-start.1 = (f32[16,1024]{1,0:T(8,128)S(1)}, f32[16,1024]{1,0:T(8,128)S(1)}, u32[]{:S(2)}, u32[]{:S(2)}) collective-permute-start(f32[16,1024]{1,0:T(8,128)S(1)} %get-tuple-element.37.refs_0_), channel_id=1, source_target_pairs={{0,4},{4,0},{8,12},{12,8},{16,20},{20,16},{24,28},{28,24},{1,5},{5... | collective-permute-start | bytes 196616 | tf_op jit(solution)/shard_map/ppermute | solution.py:389
  9.6 1.6 %collective-permute-start.2 = (f32[16,1024]{1,0:T(8,128)S(1)}, f32[16,1024]{1,0:T(8,128)S(1)}, u32[]{:S(2)}, u32[]{:S(2)}) collective-permute-start(f32[16,1024]{1,0:T(8,128)S(1)} %get-tuple-element.37.refs_0_), channel_id=1, source_target_pairs={{0,8},{4,12},{8,0},{12,4},{16,24},{20,28},{24,16},{28,20},{1,9},{5... | collective-permute-start | bytes 196616 | tf_op jit(solution)/shard_map/ppermute | solution.py:389
  11.2 1.2 %collective-permute-start.3 = (f32[16,1024]{1,0:T(8,128)S(1)}, f32[16,1024]{1,0:T(8,128)S(1)}, u32[]{:S(2)}, u32[]{:S(2)}) collective-permute-start(f32[16,1024]{1,0:T(8,128)S(1)} %get-tuple-element.37.refs_0_), channel_id=1, source_target_pairs={{0,12},{4,8},{8,4},{12,0},{16,28},{20,24},{24,20},{28,16},{1,13},{... | collective-permute-start | bytes 196616 | tf_op jit(solution)/shard_map/ppermute | solution.py:389
  12.4 0.8 %collective-permute-done.1.refs_1_ = f32[16,1024]{1,0:T(8,128)S(1)} collective-permute-done((f32[16,1024]{1,0:T(8,128)S(1)}, f32[16,1024]{1,0:T(8,128)S(1)}, u32[]{:S(2)}, u32[]{:S(2)}) %collective-permute-start.1) | collective-permute-done | bytes 65568 | tf_op jit(solution)/shard_map/ppermute | solution.py:389
  13.2 0.9 %collective-permute-done.2.refs_2_ = f32[16,1024]{1,0:T(8,128)S(1)} collective-permute-done((f32[16,1024]{1,0:T(8,128)S(1)}, f32[16,1024]{1,0:T(8,128)S(1)}, u32[]{:S(2)}, u32[]{:S(2)}) %collective-permute-start.2) | collective-permute-done | bytes 65568 | tf_op jit(solution)/shard_map/ppermute | solution.py:389
  14.1 2.3 %collective-permute-done.3.refs_3_ = f32[16,1024]{1,0:T(8,128)S(1)} collective-permute-done((f32[16,1024]{1,0:T(8,128)S(1)}, f32[16,1024]{1,0:T(8,128)S(1)}, u32[]{:S(2)}, u32[]{:S(2)}) %collective-permute-start.3) | collective-permute-done | bytes 65568 | tf_op jit(solution)/shard_map/ppermute | solution.py:389
  16.4 1.2 %collective-permute-start.4 = (f32[16,1024]{1,0:T(8,128)S(1)}, f32[16,1024]{1,0:T(8,128)S(1)}, u32[]{:S(2)}, u32[]{:S(2)}) collective-permute-start(f32[16,1024]{1,0:T(8,128)S(1)} %get-tuple-element.39), channel_id=1, source_target_pairs={{0,16},{4,20},{8,24},{12,28},{16,0},{20,4},{24,8},{28,12},{1,17},{... | collective-permute-start | bytes 196616 | tf_op jit(solution)/shard_map/ppermute | solution.py:389
  17.6 0.6 %query.1.query_ref.refs_0_ = f32[512,1024]{1,0:T(8,128)S(1)} custom-call(bf16[8,1024]{1,0:T(8,128)(2,1)S(1)} %collective-permute-done.halo_ref, bf16[512,1024]{1,0:T(8,128)(2,1)S(1)} %copy-done, f32[3,3,1024]{2,1,0:T(4,128)S(1)} %copy-done.3), custom_call_target="tpu_custom_call" | custom-call | flops 10000000 | bytes 4194304 | tf_op jit(solution)/shard_map/query/pallas_call | solution.py:373
  18.2 2.1 %near.3.refs_5_ = f32[512,512]{1,0:T(8,128)S(1)} custom-call(f32[512,1024]{1,0:T(8,128)S(1)} %get-tuple-element.40.gated_ref, f32[512,1024]{1,0:T(8,128)S(1)} %query.1.query_ref.refs_0_, f32[3,16,1024]{2,1,0:T(8,128)S(1)} %get-tuple-element.41.into_ref, f32[2,1024]{1,0:T(2,128)S(1)} %get-tuple-element.42.row_ref, f32[1,1024]{1,0:T(1,128)S(1)} %get-tuple-element.43.plain_ref, ...), custom_call_target="tpu_custom_call" | custom-call | flops 10000000 | bytes 4194304 | tf_op jit(solution)/shard_map/near/pallas_call | solution.py:393
  20.4 2.2 %near.2.refs_4_ = f32[512,512]{1,0:T(8,128)S(1)} custom-call(f32[512,1024]{1,0:T(8,128)S(1)} %get-tuple-element.40.gated_ref, f32[512,1024]{1,0:T(8,128)S(1)} %query.1.query_ref.refs_0_, f32[3,16,1024]{2,1,0:T(8,128)S(1)} %get-tuple-element.41.into_ref, f32[2,1024]{1,0:T(2,128)S(1)} %get-tuple-element.42.row_ref, f32[1,1024]{1,0:T(1,128)S(1)} %get-tuple-element.43.plain_ref, ...), custom_call_target="tpu_custom_call" | custom-call | flops 10000000 | bytes 4194304 | tf_op jit(solution)/shard_map/near/pallas_call | solution.py:393
  22.5 0.0 collective-permute-done.4.refs_3_
  22.5 1.5 %mix.1 = bf16[512,1024]{1,0:T(8,128)(2,1)} custom-call(f32[512,1024]{1,0:T(8,128)S(1)} %query.1.query_ref.refs_0_, f32[4,16,1024]{2,1,0:T(8,128)S(1)} %get-tuple-element.29.refs_5_.refs_1_, bf16[512,2048]{1,0:T(8,128)(2,1)S(1)} %get-tuple-element.30.lead_ref.refs_2_, f32[16,1024]{1,0:T(8,128)S(1)} %collective-permute-done.4.refs_3_, ...), custom_call_target="tpu_custom_call" | custom-call | tf_op jit(solution)/shard_map/mix/pallas_call | solution.py:416
  (3 shorter events, 0.0 us)
Async XLA Ops:
  0.0 5.2 %copy-start = (bf16[512,1024]{1,0:T(8,128)(2,1)S(1)}, bf16[512,1024]{1,0:T(8,128)(2,1)}, u32[]{:S(2)}) copy-start(bf16[512,1024]{1,0:T(8,128)(2,1)} %q_ref.5) | copy-start | bytes 3145732
  0.0 5.2 %copy-start.1 = (bf16[512,1024]{1,0:T(8,128)(2,1)S(1)}, bf16[512,1024]{1,0:T(8,128)(2,1)}, u32[]{:S(2)}) copy-start(bf16[512,1024]{1,0:T(8,128)(2,1)} %k_ref.5) | copy-start | bytes 3145732
  0.0 5.2 %copy-start.2 = (bf16[512,1024]{1,0:T(8,128)(2,1)S(1)}, bf16[512,1024]{1,0:T(8,128)(2,1)}, u32[]{:S(2)}) copy-start(bf16[512,1024]{1,0:T(8,128)(2,1)} %v_ref.5) | copy-start | bytes 3145732
  0.0 5.2 %copy-start.3 = (f32[3,3,1024]{2,1,0:T(4,128)S(1)}, f32[3,3,1024]{2,1,0:T(4,128)}, u32[]{:S(2)}) copy-start(f32[3,3,1024]{2,1,0:T(4,128)} %sf_ref.5) | copy-start | bytes 110596
  1.0 7.8 %collective-permute-start = (bf16[8,1024]{1,0:T(8,128)(2,1)S(1)}, bf16[8,1024]{1,0:T(8,128)(2,1)S(1)}, u32[]{:S(2)}, u32[]{:S(2)}) collective-permute-start(bf16[8,1024]{1,0:T(8,128)(2,1)S(1)} %get-tuple-element.25), channel_id=1, source_target_pairs={{0,4},{4,8},{8,12},{12,16},{16,20},{20,24},{24,28},{28,0},{1,5},{5... | collective-permute-start | bytes 49160 | tf_op jit(solution)/shard_map/ppermute | solution.py:315
  8.9 4.3 %collective-permute-start.1 = (f32[16,1024]{1,0:T(8,128)S(1)}, f32[16,1024]{1,0:T(8,128)S(1)}, u32[]{:S(2)}, u32[]{:S(2)}) collective-permute-start(f32[16,1024]{1,0:T(8,128)S(1)} %get-tuple-element.37.refs_0_), channel_id=1, source_target_pairs={{0,4},{4,0},{8,12},{12,8},{16,20},{20,16},{24,28},{28,24},{1,5},{5... | collective-permute-start | bytes 196616 | tf_op jit(solution)/shard_map/ppermute | solution.py:389
  9.6 4.5 %collective-permute-start.2 = (f32[16,1024]{1,0:T(8,128)S(1)}, f32[16,1024]{1,0:T(8,128)S(1)}, u32[]{:S(2)}, u32[]{:S(2)}) collective-permute-start(f32[16,1024]{1,0:T(8,128)S(1)} %get-tuple-element.37.refs_0_), channel_id=1, source_target_pairs={{0,8},{4,12},{8,0},{12,4},{16,24},{20,28},{24,16},{28,20},{1,9},{5... | collective-permute-start | bytes 196616 | tf_op jit(solution)/shard_map/ppermute | solution.py:389
  11.2 5.2 %collective-permute-start.3 = (f32[16,1024]{1,0:T(8,128)S(1)}, f32[16,1024]{1,0:T(8,128)S(1)}, u32[]{:S(2)}, u32[]{:S(2)}) collective-permute-start(f32[16,1024]{1,0:T(8,128)S(1)} %get-tuple-element.37.refs_0_), channel_id=1, source_target_pairs={{0,12},{4,8},{8,4},{12,0},{16,28},{20,24},{24,20},{28,16},{1,13},{... | collective-permute-start | bytes 196616 | tf_op jit(solution)/shard_map/ppermute | solution.py:389
  16.4 6.1 %collective-permute-start.4 = (f32[16,1024]{1,0:T(8,128)S(1)}, f32[16,1024]{1,0:T(8,128)S(1)}, u32[]{:S(2)}, u32[]{:S(2)}) collective-permute-start(f32[16,1024]{1,0:T(8,128)S(1)} %get-tuple-element.39), channel_id=1, source_target_pairs={{0,16},{4,20},{8,24},{12,28},{16,0},{20,4},{24,8},{28,12},{1,17},{... | collective-permute-start | bytes 196616 | tf_op jit(solution)/shard_map/ppermute | solution.py:389

commit v8 on v7

--- a/solution.py
+++ b/solution.py
@@ -9,7 +9,6 @@
 
 
 LANES = 128
-WIDE = 256
 SUB = 8
 F32 = jnp.float32
 BF16 = jnp.bfloat16
@@ -98,26 +97,34 @@
     return table
 
 
-def table_kernel(ranks, res_ref, decay_ref, skip_ref, lead_ref, tail_ref, row_ref, plain_ref, hop_ref, seam_ref, span_ref, reach_ref):
-    length, width = lead_ref.shape[0], skip_ref.shape[1]
-    modes = decay_ref.shape[0]
-    gaps = gaps_of(ranks, length)
+def table_kernel(res_ref, decay_ref, skip_ref, tail_ref, row_ref, plain_ref, rate_ref, hop_ref, seam_ref):
+    modes, width = hop_ref.shape
     plain_ref[...] = skip_ref[...]
     lane = lax.broadcasted_iota(jnp.int32, (modes, LANES), 1)
     own = lane % modes == lax.broadcasted_iota(jnp.int32, (modes, LANES), 0)
-    down = lax.broadcasted_iota(jnp.int32, (LANES, LANES), 0).astype(F32)
     along = lax.broadcasted_iota(jnp.int32, (LANES, LANES), 1).astype(F32)
     for tile in range(width // LANES):
         at = slice(tile * LANES, (tile + 1) * LANES)
         rates = expand(decay_ref[...], tile * (LANES // modes), LANES, modes)
         gains = expand(res_ref[...], tile * (LANES // modes), LANES, modes) * norm_of(rates)
         rate = jnp.sum(jnp.where(own, rates, 0.0), axis=0, keepdims=True)
-        gain = jnp.sum(jnp.where(own, gains, 0.0), axis=0, keepdims=True)
         row_ref[0:1, at] = rate
-        row_ref[1:2, at] = gain
+        row_ref[1:2, at] = jnp.sum(jnp.where(own, gains, 0.0), axis=0, keepdims=True)
+        rate_ref[:, at] = rates
         hop_ref[:, at] = jnp.exp(-rates * float(LANES))
         for i in range(2):
             seam_ref[i, :, at] = jnp.exp(-rates * (LANES - 1.0 - i))
+        rate_rows = jnp.transpose(jnp.broadcast_to(rate, (LANES, LANES)))
+        tail_ref[at, 0:LANES], tail_ref[at, LANES:] = split2(jnp.exp(-rate_rows * (LANES - 1.0 - along)))
+
+
+def lead_kernel(ranks, row_ref, rate_ref, lead_ref, span_ref, reach_ref):
+    length, width = lead_ref.shape[0], rate_ref.shape[1]
+    gaps = gaps_of(ranks, length)
+    down = lax.broadcasted_iota(jnp.int32, (LANES, LANES), 0).astype(F32)
+    for tile in range(width // LANES):
+        at = slice(tile * LANES, (tile + 1) * LANES)
+        rates = rate_ref[:, at]
         e = f = 0
         for step, row in enumerate(gaps):
             for m, (before, gap, after) in enumerate(row):
@@ -127,34 +134,38 @@
                 if step + 1 < len(gaps):
                     span_ref[f, :, at] = jnp.exp(-rates * after)
                     f += 1
-        rate_rows = jnp.transpose(jnp.broadcast_to(rate, (LANES, LANES)))
-        tail_ref[at, 0:LANES], tail_ref[at, LANES:] = split2(jnp.exp(-rate_rows * (LANES - 1.0 - along)))
-        lead = gain * jnp.exp(-rate * (down + 1.0))
+        rate = row_ref[0:1, at]
+        lead = row_ref[1:2, at] * jnp.exp(-rate * (down + 1.0))
         hop = jnp.exp(-rate * float(LANES))
+        mid = 2 * tile * LANES + LANES
         for c in range(length // LANES):
             rows = slice(c * LANES, (c + 1) * LANES)
-            mid = 2 * tile * LANES + LANES
             lead_ref[rows, mid - LANES : mid], lead_ref[rows, mid : mid + LANES] = split2(lead)
             lead = lead * hop
 
 
-def state_kernel(size, k_ref, v_ref, sf_ref, tail_ref, hop_ref, q_ref, gated_ref, fresh_ref, enter_ref, kf, vf):
-    length, lanes = k_ref.shape
+def state_kernel(size, k_ref, v_ref, sf_ref, tail_ref, hop_ref, q_ref, gated_ref, fresh_ref, enter_ref, kfs, vfs):
+    length, width = k_ref.shape
     modes = fresh_ref.shape[0]
-    tile = pl.program_id(0)
     row = lax.broadcasted_iota(jnp.int32, (modes, LANES), 1) // size
     piece = 64
     inner = lax.broadcasted_iota(jnp.int32, (piece, LANES), 0) >= 2
-    kf[0:SUB] = jnp.zeros((SUB, LANES), F32)
-    vf[0:SUB] = jnp.zeros((SUB, LANES), F32)
-    for part in range(lanes // LANES):
-        at = slice(part * LANES, (part + 1) * LANES)
-        base = pl.multiple_of(tile * lanes + part * LANES, LANES)
-        own = pl.ds(base, LANES)
+    for slot in range(2):
+        kfs[slot, 0:SUB] = jnp.zeros((SUB, LANES), F32)
+        vfs[slot, 0:SUB] = jnp.zeros((SUB, LANES), F32)
+
+    def two(i, carry):
+        for slot in range(2):
+            one(pl.multiple_of((2 * i + slot) * LANES, LANES), slot)
+        return carry
+
+    def one(base, slot):
+        at = pl.ds(base, LANES)
+        kf, vf = kfs.at[slot], vfs.at[slot]
         kt = [sf_ref[1, i : i + 1, at] for i in range(3)]
         vt = [sf_ref[2, i : i + 1, at] for i in range(3)]
-        hop = hop_ref[:, own]
-        tail = tail_ref[own, :]
+        hop = hop_ref[:, at]
+        tail = tail_ref[at, :]
         total = jnp.zeros((modes, LANES), F32)
         for c in range(length // LANES):
             his, los = [], []
@@ -165,7 +176,7 @@
                 gated = short3(kf, start, piece, kt) * short3(vf, start, piece, vt)
                 if start == 0:
                     gated = jnp.where(inner, gated, 0.0)
-                gated_ref[rows, own] = gated
+                gated_ref[rows, at] = gated
                 hi, lo = split2(gated)
                 his.append(hi)
                 los.append(lo)
@@ -174,9 +185,11 @@
             for g in range(LANES // size):
                 fresh = jnp.where(row == g, out[g * modes : (g + 1) * modes], fresh)
             if c:
-                enter_ref[c - 1, :, own] = total
+                enter_ref[c - 1, :, at] = total
             total = total * hop + fresh
-        fresh_ref[:, own] = total
+        fresh_ref[:, at] = total
+
+    lax.fori_loop(0, width // (2 * LANES), two, 0)
 
 
 def seam_kernel(halo_ref, k_ref, v_ref, sf_ref, seam_ref, hop_ref, fresh_ref, enter_ref, gated_ref, out_ref, into_ref, whole_ref, kf, vf):
@@ -221,7 +234,7 @@
             out_ref[rows, at] = short3(qf, start, piece, taps)
 
 
-def near_kernel(size, first, gated_ref, query_ref, into_ref, row_ref, plain_ref, lead_ref, out_ref):
+def near_kernel(size, first, gated_ref, into_ref, row_ref, plain_ref, lead_ref, out_ref):
     length, lanes = out_ref.shape
     modes = into_ref.shape[1]
     chunks = length // LANES
@@ -255,7 +268,7 @@
             if c:
                 wide = jnp.where(block, jnp.concatenate([into_ref[c - 1, :, at]] * groups, 0), 0.0)
                 near = near + dot3(lead, pair(*split2(wide)))
-            out_ref[rows, to] = query_ref[rows, at] * near
+            out_ref[rows, to] = near
 
 
 def mix_kernel(size, first, count, parts, *refs):
@@ -285,7 +298,7 @@
         for start in range(0, length, LANES):
             rows = slice(start, start + LANES)
             term = dot3(lead_ref[rows, 2 * at.start : 2 * at.stop], right)
-            stage[rows, at] = (near[rows, c : c + LANES] + query_ref[rows, at] * term).astype(BF16)
+            stage[rows, at] = (query_ref[rows, at] * (near[rows, c : c + LANES] + term)).astype(BF16)
         copy = pltpu.make_async_copy(stage.at[:, at], out_ref.at[:, at], sem.at[tile])
         copy.start()
         copies.append(copy)
@@ -318,43 +331,40 @@
     tail_shape = jax.ShapeDtypeStruct((width, 2 * LANES), BF16)
     scan_shape = lambda count: jax.ShapeDtypeStruct((count, modes, width), F32)
     row_shape = jax.ShapeDtypeStruct((modes, width), F32)
-    lead, tail, row, plain, hop, seam, span, reach = pl.pallas_call(
-        functools.partial(table_kernel, ranks),
+    tail, row, plain, rate, hop, seam = pl.pallas_call(
+        table_kernel,
         in_specs=[VMEM] * 3,
-        out_specs=[VMEM] * 8,
+        out_specs=[VMEM] * 6,
         out_shape=[
-            lead_shape,
             tail_shape,
             jax.ShapeDtypeStruct((2, width), F32),
             jax.ShapeDtypeStruct((1, width), F32),
             row_shape,
+            row_shape,
             scan_shape(2),
-            scan_shape(max(1, spans)),
-            scan_shape(reaches),
         ],
         compiler_params=PARAMS,
         cost_estimate=pl.CostEstimate(flops=10**7, bytes_accessed=5 << 20, transcendentals=0),
         name="tables",
     )(residues, decay_rate, skip_gain)
-
-    tile = min(width, WIDE)
-    cols = lambda rows: pl.BlockSpec((rows, tile), lambda j: (0, j))
+    lead, span, reach = pl.pallas_call(
+        functools.partial(lead_kernel, ranks),
+        in_specs=[VMEM] * 2,
+        out_specs=[VMEM] * 3,
+        out_shape=[lead_shape, scan_shape(max(1, spans)), scan_shape(reaches)],
+        compiler_params=PARAMS,
+        cost_estimate=pl.CostEstimate(flops=10**7, bytes_accessed=2 << 20, transcendentals=0),
+        name="lead",
+    )(row, rate)
+
     gated_shape = jax.ShapeDtypeStruct((length, width), F32)
     enter_shape = scan_shape(length // LANES - 1)
     gated, fresh, enter = pl.pallas_call(
         functools.partial(state_kernel, size),
-        grid=(width // tile,),
-        in_specs=[
-            cols(length),
-            cols(length),
-            pl.BlockSpec((3, 3, tile), lambda j: (0, 0, j)),
-            VMEM,
-            VMEM,
-            VMEM,
-        ],
+        in_specs=[VMEM] * 6,
         out_specs=[VMEM] * 3,
         out_shape=[gated_shape, row_shape, enter_shape],
-        scratch_shapes=[pltpu.VMEM((SUB + length, LANES), F32)] * 2,
+        scratch_shapes=[pltpu.VMEM((2, SUB + length, LANES), F32)] * 2,
         compiler_params=PARAMS,
         cost_estimate=pl.CostEstimate(flops=10**7, bytes_accessed=5 << 20, transcendentals=0),
         name="state",
@@ -381,7 +391,9 @@
         name="query",
     )(halo, query_in, short_filter)
 
-    cuts = [width // LANES * b // len(steps) * LANES for b in range(len(steps) + 1)]
+    tiles = width // LANES
+    head = tiles * 4 // 8
+    cuts = [0] + [(head + (tiles - head) * b // max(1, len(steps) - 1)) * LANES for b in range(len(steps))]
     nears, total, prefix, first, at = [], fresh, [], 0, 0
     for b, (low, count) in enumerate(steps):
         gots = []
@@ -392,13 +404,13 @@
             nears.append(
                 pl.pallas_call(
                     functools.partial(near_kernel, size, cuts[b]),
-                    in_specs=[VMEM] * 6,
+                    in_specs=[VMEM] * 5,
                     out_specs=VMEM,
                     out_shape=jax.ShapeDtypeStruct((length, lanes), F32),
                     compiler_params=PARAMS,
                     cost_estimate=pl.CostEstimate(flops=10**7, bytes_accessed=4 << 20, transcendentals=0),
                     name="near",
-                )(gated, query, into, row, plain, lead)
+                )(gated, into, row, plain, lead)
             )
         if b + 1 < len(steps):
             total, ahead = pl.pallas_call(

time: 24.2 us -> 23.8 us (0.983)
  starting transfers between devices: 7.77 us -> 8.47 us
  waiting for transfers between devices: 4.82 us -> 4.17 us
  Pallas kernels: 11.3 us -> 10.9 us
    ppermute x4, waiting for transfers between devices: 3.94 us -> 2.35 us  [body(): lax.ppermute(total, 'ctx', [(i, i ^ m << low) for i in range(ranks)])]
    ppermute x1, waiting for transfers between devices: 0.88 us -> 1.82 us  [body(): lax.ppermute(rims, 'ctx', [(i, (i + 1) % ranks) for i in range(ranks)])]
    ppermute x4, starting transfers between devices: 4.74 us -> 5.44 us  [body(): lax.ppermute(total, 'ctx', [(i, i ^ m << low) for i in range(ranks)])]
    pallas_call x2 -> x3, Pallas kernels: 3.83 us -> 3.53 us  [the longest x1 2.43 us: body(): pl.pallas_call(functools.partial(state_kernel, size), in_specs=[VMEM] * 6...]
  transfers between devices with their start and end apart: 5 -> 5, of which waited for: 4 -> 3; matrix products, arithmetic and copies ran while one was open for 0% -> 0% of each run, Pallas kernels for 36% -> 35%
where the time goes in v8:
time: 23.8 us; the launch traced here: 23.7 us
  Pallas kernels  10.9 us (46%)
  starting transfers between devices  8.47 us (36%)
  waiting for transfers between devices  4.17 us (18%)
    ppermute x4, starting transfers between devices, body(): lax.ppermute(total, 'ctx', [(i, i ^ m << low) for i in range(ranks)])  5.44 us
    pallas_call x2, Pallas kernels, body(): pl.pallas_call(functools.partial(near_kernel, size, cuts[b]), in_specs=[V...  4.23 us
    ppermute x1, starting transfers between devices, body(): lax.ppermute(rims, 'ctx', [(i, (i + 1) % ranks) for i in range(ranks)])  3.03 us
    pallas_call x1, Pallas kernels, body(): pl.pallas_call(functools.partial(state_kernel, size), in_specs=[VMEM] * 6...  2.43 us
    ppermute x4, waiting for transfers between devices, body(): lax.ppermute(total, 'ctx', [(i, i ^ m << low) for i in range(ranks)])  2.35 us
    ppermute x1, waiting for transfers between devices, body(): lax.ppermute(rims, 'ctx', [(i, (i + 1) % ranks) for i in range(ranks)])  1.82 us
    pallas_call x1, Pallas kernels, body(): pl.pallas_call(functools.partial(mix_kernel, size, first, len(gots), len(...  1.48 us
    pallas_call x1, Pallas kernels, body(): pl.pallas_call(rim_kernel, in_specs=[pl.BlockSpec(memory_space=pltpu.HBM)...  0.98 us
  transfers between devices with their start and end apart: 5, of which 3 were waited for; matrix products, arithmetic and copies ran while one was open for 0% of the time, Pallas kernels for 35%

profile of v8, /device:TPU:0, one launch (start us, length us, event | category | flops | bytes accessed | tf_op | source)
XLA Modules:
  0.0 23.7 jit_solution(1537686061723371591)
XLA Ops:
  0.0 0.0 copy-start
  0.0 1.0 %rim.1 = (bf16[8,1024]{1,0:T(8,128)(2,1)S(1)}, f32[16,64]{1,0:T(8,128)S(1)}, f32[16,64]{1,0:T(8,128)S(1)}, f32[1,1024]{1,0:T(1,128)S(1)}) custom-call(bf16[512,1024]{1,0:T(8,128)(2,1)} %q_ref.5, bf16[512,1024]{1,0:T(8,128)(2,1)} %k_ref.5, bf16[512,1024]{1,0:T(8,128)(2,1)} %v_ref.5, f32[16,64]{1,0:T(8,128)} %refs_0_.1, f32[16,64]{1,0:T(8,128)} %refs_1_.1, ...), custom_call_target="tpu_custom_call" | custom-call | tf_op jit(solution)/shard_map/rim/pallas_call | solution.py:319
  1.0 3.0 %collective-permute-start = (bf16[8,1024]{1,0:T(8,128)(2,1)S(1)}, bf16[8,1024]{1,0:T(8,128)(2,1)S(1)}, u32[]{:S(2)}, u32[]{:S(2)}) collective-permute-start(bf16[8,1024]{1,0:T(8,128)(2,1)S(1)} %get-tuple-element.26), channel_id=1, source_target_pairs={{0,4},{4,8},{8,12},{12,16},{16,20},{20,24},{24,28},{28,0},{1,5},{5... | collective-permute-start | bytes 49160 | tf_op jit(solution)/shard_map/ppermute | solution.py:328
  4.0 0.5 %tables.1 = (bf16[1024,256]{1,0:T(8,128)(2,1)S(1)}, f32[2,1024]{1,0:T(2,128)S(1)}, f32[1,1024]{1,0:T(1,128)S(1)}, f32[16,1024]{1,0:T(8,128)S(1)}, f32[16,1024]{1,0:T(8,128)S(1)}, /*index=5*/f32[2,16,1024]{2,1,0:T(8,128)S(1)}) custom-call(f32[16,64]{1,0:T(8,128)S(1)} %get-tuple-element.27.res_ref, f32[16,64]{1,0:T(8,128)S(1)} %get-tuple-element.28.decay_ref, ...), custom_call_target="tpu_custom_call" | custom-call | flops 10000000 | bytes 5242880 | tf_op jit(solution)/shard_map/tables/pallas_call | solution.py:334
  4.5 0.0 copy-done
  4.5 0.0 copy-done.1
  4.5 0.0 copy-done.2
  4.5 0.0 copy-done.3
  4.5 2.4 %state.1 = (f32[512,1024]{1,0:T(8,128)S(1)}, f32[16,1024]{1,0:T(8,128)S(1)}, f32[3,16,1024]{2,1,0:T(8,128)S(1)}) custom-call(bf16[512,1024]{1,0:T(8,128)(2,1)S(1)} %copy-done.1, bf16[512,1024]{1,0:T(8,128)(2,1)S(1)} %copy-done.2, f32[3,3,1024]{2,1,0:T(4,128)S(1)} %copy-done.3, bf16[1024,256]{1,0:T(8,128)(2,1)S(1)} %get-tuple-element.36.tail_ref, ...), custom_call_target="tpu_custom_call" | custom-call | flops 10000000 | bytes 5242880 | tf_op jit(solution)/shard_map/state/pallas_call | solution.py:362
  7.0 1.8 %collective-permute-done.halo_ref = bf16[8,1024]{1,0:T(8,128)(2,1)S(1)} collective-permute-done((bf16[8,1024]{1,0:T(8,128)(2,1)S(1)}, bf16[8,1024]{1,0:T(8,128)(2,1)S(1)}, u32[]{:S(2)}, u32[]{:S(2)}) %collective-permute-start) | collective-permute-done | bytes 16416 | tf_op jit(solution)/shard_map/ppermute | solution.py:328
  8.8 0.1 seam.1
  8.9 0.1 collective-permute-start.1
  8.9 1.3 %collective-permute-start.2 = (f32[16,1024]{1,0:T(8,128)S(1)}, f32[16,1024]{1,0:T(8,128)S(1)}, u32[]{:S(2)}, u32[]{:S(2)}) collective-permute-start(f32[16,1024]{1,0:T(8,128)S(1)} %get-tuple-element.40.refs_0_), channel_id=1, source_target_pairs={{0,8},{4,12},{8,0},{12,4},{16,24},{20,28},{24,16},{28,20},{1,9},{5... | collective-permute-start | bytes 196616 | tf_op jit(solution)/shard_map/ppermute | solution.py:401
  10.3 2.2 %collective-permute-start.3 = (f32[16,1024]{1,0:T(8,128)S(1)}, f32[16,1024]{1,0:T(8,128)S(1)}, u32[]{:S(2)}, u32[]{:S(2)}) collective-permute-start(f32[16,1024]{1,0:T(8,128)S(1)} %get-tuple-element.40.refs_0_), channel_id=1, source_target_pairs={{0,12},{4,8},{8,4},{12,0},{16,28},{20,24},{24,20},{28,16},{1,13},{... | collective-permute-start | bytes 196616 | tf_op jit(solution)/shard_map/ppermute | solution.py:401
  12.4 0.6 %lead.1 = (bf16[512,2048]{1,0:T(8,128)(2,1)S(1)}, f32[4,16,1024]{2,1,0:T(8,128)S(1)}, f32[4,16,1024]{2,1,0:T(8,128)S(1)}) custom-call(f32[2,1024]{1,0:T(2,128)S(1)} %get-tuple-element.30.row_ref, f32[16,1024]{1,0:T(8,128)S(1)} %get-tuple-element.31.rate_ref), custom_call_target="tpu_custom_call" | custom-call | flops 10000000 | bytes 2097152 | tf_op jit(solution)/shard_map/lead/pallas_call | solution.py:350
  13.1 0.8 %collective-permute-done.1.refs_1_ = f32[16,1024]{1,0:T(8,128)S(1)} collective-permute-done((f32[16,1024]{1,0:T(8,128)S(1)}, f32[16,1024]{1,0:T(8,128)S(1)}, u32[]{:S(2)}, u32[]{:S(2)}) %collective-permute-start.1) | collective-permute-done | bytes 65568 | tf_op jit(solution)/shard_map/ppermute | solution.py:401
  13.9 0.0 collective-permute-done.2.refs_2_
  13.9 1.5 %collective-permute-done.3.refs_3_ = f32[16,1024]{1,0:T(8,128)S(1)} collective-permute-done((f32[16,1024]{1,0:T(8,128)S(1)}, f32[16,1024]{1,0:T(8,128)S(1)}, u32[]{:S(2)}, u32[]{:S(2)}) %collective-permute-start.3) | collective-permute-done | bytes 65568 | tf_op jit(solution)/shard_map/ppermute | solution.py:401
  15.5 1.9 %collective-permute-start.4 = (f32[16,1024]{1,0:T(8,128)S(1)}, f32[16,1024]{1,0:T(8,128)S(1)}, u32[]{:S(2)}, u32[]{:S(2)}) collective-permute-start(f32[16,1024]{1,0:T(8,128)S(1)} %get-tuple-element.42), channel_id=1, source_target_pairs={{0,16},{4,20},{8,24},{12,28},{16,0},{20,4},{24,8},{28,12},{1,17},{... | collective-permute-start | bytes 196616 | tf_op jit(solution)/shard_map/ppermute | solution.py:401
  17.4 2.1 %near.3.refs_5_ = f32[512,512]{1,0:T(8,128)S(1)} custom-call(f32[512,1024]{1,0:T(8,128)S(1)} %get-tuple-element.43.gated_ref, f32[3,16,1024]{2,1,0:T(8,128)S(1)} %get-tuple-element.44.into_ref, f32[2,1024]{1,0:T(2,128)S(1)} %get-tuple-element.30.row_ref, f32[1,1024]{1,0:T(1,128)S(1)} %get-tuple-element.45.plain_ref, ...), custom_call_target="tpu_custom_call" | custom-call | flops 10000000 | bytes 4194304 | tf_op jit(solution)/shard_map/near/pallas_call | solution.py:405
  19.5 2.1 %near.2.refs_4_ = f32[512,512]{1,0:T(8,128)S(1)} custom-call(f32[512,1024]{1,0:T(8,128)S(1)} %get-tuple-element.43.gated_ref, f32[3,16,1024]{2,1,0:T(8,128)S(1)} %get-tuple-element.44.into_ref, f32[2,1024]{1,0:T(2,128)S(1)} %get-tuple-element.30.row_ref, f32[1,1024]{1,0:T(1,128)S(1)} %get-tuple-element.45.plain_ref, ...), custom_call_target="tpu_custom_call" | custom-call | flops 10000000 | bytes 4194304 | tf_op jit(solution)/shard_map/near/pallas_call | solution.py:405
  21.6 0.6 %query.1.refs_0_ = f32[512,1024]{1,0:T(8,128)S(1)} custom-call(bf16[8,1024]{1,0:T(8,128)(2,1)S(1)} %collective-permute-done.halo_ref, bf16[512,1024]{1,0:T(8,128)(2,1)S(1)} %copy-done, f32[3,3,1024]{2,1,0:T(4,128)S(1)} %copy-done.3), custom_call_target="tpu_custom_call" | custom-call | flops 10000000 | bytes 4194304 | tf_op jit(solution)/shard_map/query/pallas_call | solution.py:383
  22.2 0.0 collective-permute-done.4.refs_3_
  22.2 1.5 %mix.1 = bf16[512,1024]{1,0:T(8,128)(2,1)} custom-call(f32[512,1024]{1,0:T(8,128)S(1)} %query.1.refs_0_, f32[4,16,1024]{2,1,0:T(8,128)S(1)} %get-tuple-element.32.refs_5_.refs_1_, bf16[512,2048]{1,0:T(8,128)(2,1)S(1)} %get-tuple-element.33.lead_ref.refs_2_, f32[16,1024]{1,0:T(8,128)S(1)} %collective-permute-done.4.refs_3_, f32[512,512]{1,0:T(8,128)S(1)} %near.2.refs_4_, ...), custom_call_target="tpu_custom_call" | custom-call | tf_op jit(solution)/shard_map/mix/pallas_call | solution.py:428
  (4 shorter events, 0.0 us)
Async XLA Ops:
  0.0 4.5 %copy-start = (bf16[512,1024]{1,0:T(8,128)(2,1)S(1)}, bf16[512,1024]{1,0:T(8,128)(2,1)}, u32[]{:S(2)}) copy-start(bf16[512,1024]{1,0:T(8,128)(2,1)} %q_ref.5) | copy-start | bytes 3145732
  0.0 4.5 %copy-start.1 = (bf16[512,1024]{1,0:T(8,128)(2,1)S(1)}, bf16[512,1024]{1,0:T(8,128)(2,1)}, u32[]{:S(2)}) copy-start(bf16[512,1024]{1,0:T(8,128)(2,1)} %k_ref.5) | copy-start | bytes 3145732
  0.0 4.5 %copy-start.2 = (bf16[512,1024]{1,0:T(8,128)(2,1)S(1)}, bf16[512,1024]{1,0:T(8,128)(2,1)}, u32[]{:S(2)}) copy-start(bf16[512,1024]{1,0:T(8,128)(2,1)} %v_ref.5) | copy-start | bytes 3145732
  0.0 4.5 %copy-start.3 = (f32[3,3,1024]{2,1,0:T(4,128)S(1)}, f32[3,3,1024]{2,1,0:T(4,128)}, u32[]{:S(2)}) copy-start(f32[3,3,1024]{2,1,0:T(4,128)} %sf_ref.5) | copy-start | bytes 110596
  1.0 7.8 %collective-permute-start = (bf16[8,1024]{1,0:T(8,128)(2,1)S(1)}, bf16[8,1024]{1,0:T(8,128)(2,1)S(1)}, u32[]{:S(2)}, u32[]{:S(2)}) collective-permute-start(bf16[8,1024]{1,0:T(8,128)(2,1)S(1)} %get-tuple-element.26), channel_id=1, source_target_pairs={{0,4},{4,8},{8,12},{12,16},{16,20},{20,24},{24,28},{28,0},{1,5},{5... | collective-permute-start | bytes 49160 | tf_op jit(solution)/shard_map/ppermute | solution.py:328
  8.9 5.0 %collective-permute-start.1 = (f32[16,1024]{1,0:T(8,128)S(1)}, f32[16,1024]{1,0:T(8,128)S(1)}, u32[]{:S(2)}, u32[]{:S(2)}) collective-permute-start(f32[16,1024]{1,0:T(8,128)S(1)} %get-tuple-element.40.refs_0_), channel_id=1, source_target_pairs={{0,4},{4,0},{8,12},{12,8},{16,20},{20,16},{24,28},{28,24},{1,5},{5... | collective-permute-start | bytes 196616 | tf_op jit(solution)/shard_map/ppermute | solution.py:401
  8.9 5.0 %collective-permute-start.2 = (f32[16,1024]{1,0:T(8,128)S(1)}, f32[16,1024]{1,0:T(8,128)S(1)}, u32[]{:S(2)}, u32[]{:S(2)}) collective-permute-start(f32[16,1024]{1,0:T(8,128)S(1)} %get-tuple-element.40.refs_0_), channel_id=1, source_target_pairs={{0,8},{4,12},{8,0},{12,4},{16,24},{20,28},{24,16},{28,20},{1,9},{5... | collective-permute-start | bytes 196616 | tf_op jit(solution)/shard_map/ppermute | solution.py:401
  10.3 5.2 %collective-permute-start.3 = (f32[16,1024]{1,0:T(8,128)S(1)}, f32[16,1024]{1,0:T(8,128)S(1)}, u32[]{:S(2)}, u32[]{:S(2)}) collective-permute-start(f32[16,1024]{1,0:T(8,128)S(1)} %get-tuple-element.40.refs_0_), channel_id=1, source_target_pairs={{0,12},{4,8},{8,4},{12,0},{16,28},{20,24},{24,20},{28,16},{1,13},{... | collective-permute-start | bytes 196616 | tf_op jit(solution)/shard_map/ppermute | solution.py:401
  15.5 6.8 %collective-permute-start.4 = (f32[16,1024]{1,0:T(8,128)S(1)}, f32[16,1024]{1,0:T(8,128)S(1)}, u32[]{:S(2)}, u32[]{:S(2)}) collective-permute-start(f32[16,1024]{1,0:T(8,128)S(1)} %get-tuple-element.42), channel_id=1, source_target_pairs={{0,16},{4,20},{8,24},{12,28},{16,0},{20,4},{24,8},{28,12},{1,17},{... | collective-permute-start | bytes 196616 | tf_op jit(solution)/shard_map/ppermute | solution.py:401

commit v9 on v7

--- a/solution.py
+++ b/solution.py
@@ -9,12 +9,12 @@
 
 
 LANES = 128
-WIDE = 256
 SUB = 8
 F32 = jnp.float32
 BF16 = jnp.bfloat16
 VMEM = pl.BlockSpec(memory_space=pltpu.VMEM)
 PARAMS = pltpu.CompilerParams(vmem_limit_bytes=8 << 20)
+PACKED = pltpu.CompilerParams(vmem_limit_bytes=8 << 20)
 
 
 def split2(x):
@@ -138,23 +138,28 @@
             lead = lead * hop
 
 
-def state_kernel(size, k_ref, v_ref, sf_ref, tail_ref, hop_ref, q_ref, gated_ref, fresh_ref, enter_ref, kf, vf):
-    length, lanes = k_ref.shape
+def state_kernel(size, k_ref, v_ref, sf_ref, tail_ref, hop_ref, q_ref, gated_ref, fresh_ref, enter_ref, kfs, vfs):
+    length, width = k_ref.shape
     modes = fresh_ref.shape[0]
-    tile = pl.program_id(0)
     row = lax.broadcasted_iota(jnp.int32, (modes, LANES), 1) // size
     piece = 64
     inner = lax.broadcasted_iota(jnp.int32, (piece, LANES), 0) >= 2
-    kf[0:SUB] = jnp.zeros((SUB, LANES), F32)
-    vf[0:SUB] = jnp.zeros((SUB, LANES), F32)
-    for part in range(lanes // LANES):
-        at = slice(part * LANES, (part + 1) * LANES)
-        base = pl.multiple_of(tile * lanes + part * LANES, LANES)
-        own = pl.ds(base, LANES)
+    for slot in range(2):
+        kfs[slot, 0:SUB] = jnp.zeros((SUB, LANES), F32)
+        vfs[slot, 0:SUB] = jnp.zeros((SUB, LANES), F32)
+
+    def two(i, carry):
+        for slot in range(2):
+            one(pl.multiple_of((2 * i + slot) * LANES, LANES), slot)
+        return carry
+
+    def one(base, slot):
+        at = pl.ds(base, LANES)
+        kf, vf = kfs.at[slot], vfs.at[slot]
         kt = [sf_ref[1, i : i + 1, at] for i in range(3)]
         vt = [sf_ref[2, i : i + 1, at] for i in range(3)]
-        hop = hop_ref[:, own]
-        tail = tail_ref[own, :]
+        hop = hop_ref[:, at]
+        tail = tail_ref[at, :]
         total = jnp.zeros((modes, LANES), F32)
         for c in range(length // LANES):
             his, los = [], []
@@ -165,7 +170,7 @@
                 gated = short3(kf, start, piece, kt) * short3(vf, start, piece, vt)
                 if start == 0:
                     gated = jnp.where(inner, gated, 0.0)
-                gated_ref[rows, own] = gated
+                gated_ref[rows, at] = gated
                 hi, lo = split2(gated)
                 his.append(hi)
                 los.append(lo)
@@ -174,9 +179,11 @@
             for g in range(LANES // size):
                 fresh = jnp.where(row == g, out[g * modes : (g + 1) * modes], fresh)
             if c:
-                enter_ref[c - 1, :, own] = total
+                enter_ref[c - 1, :, at] = total
             total = total * hop + fresh
-        fresh_ref[:, own] = total
+        fresh_ref[:, at] = total
+
+    lax.fori_loop(0, width // (2 * LANES), two, 0)
 
 
 def seam_kernel(halo_ref, k_ref, v_ref, sf_ref, seam_ref, hop_ref, fresh_ref, enter_ref, gated_ref, out_ref, into_ref, whole_ref, kf, vf):
@@ -337,25 +344,15 @@
         name="tables",
     )(residues, decay_rate, skip_gain)
 
-    tile = min(width, WIDE)
-    cols = lambda rows: pl.BlockSpec((rows, tile), lambda j: (0, j))
     gated_shape = jax.ShapeDtypeStruct((length, width), F32)
     enter_shape = scan_shape(length // LANES - 1)
     gated, fresh, enter = pl.pallas_call(
         functools.partial(state_kernel, size),
-        grid=(width // tile,),
-        in_specs=[
-            cols(length),
-            cols(length),
-            pl.BlockSpec((3, 3, tile), lambda j: (0, 0, j)),
-            VMEM,
-            VMEM,
-            VMEM,
-        ],
+        in_specs=[VMEM] * 6,
         out_specs=[VMEM] * 3,
         out_shape=[gated_shape, row_shape, enter_shape],
-        scratch_shapes=[pltpu.VMEM((SUB + length, LANES), F32)] * 2,
-        compiler_params=PARAMS,
+        scratch_shapes=[pltpu.VMEM((2, SUB + length, LANES), F32)] * 2,
+        compiler_params=PACKED,
         cost_estimate=pl.CostEstimate(flops=10**7, bytes_accessed=5 << 20, transcendentals=0),
         name="state",
     )(key_in, value_in, short_filter, tail, hop, query_in)

time: 24.2 us -> 23.9 us (0.988)
  no operation moved by 1% of the time
where the time goes in v9:
time: 23.9 us; the launch traced here: 23.8 us
  Pallas kernels  11.1 us (46%)
  starting transfers between devices  7.77 us (33%)
  waiting for transfers between devices  4.82 us (20%)
    ppermute x4, starting transfers between devices, body(): lax.ppermute(total, 'ctx', [(i, i ^ m << low) for i in range(ranks)])  4.74 us
    pallas_call x2, Pallas kernels, body(): pl.pallas_call(functools.partial(near_kernel, size, cuts[b]), in_specs=[V...  4.3 us
    ppermute x4, waiting for transfers between devices, body(): lax.ppermute(total, 'ctx', [(i, i ^ m << low) for i in range(ranks)])  3.71 us
    ppermute x1, starting transfers between devices, body(): lax.ppermute(rims, 'ctx', [(i, (i + 1) % ranks) for i in range(ranks)])  3.03 us
    pallas_call x1, Pallas kernels, body(): pl.pallas_call(functools.partial(state_kernel, size), in_specs=[VMEM] * 6...  2.43 us
    pallas_call x1, Pallas kernels, body(): pl.pallas_call(functools.partial(mix_kernel, size, first, len(gots), len(...  1.51 us
    pallas_call x1, Pallas kernels, body(): pl.pallas_call(functools.partial(table_kernel, ranks), in_specs=[VMEM] *...  1.17 us
    ppermute x1, waiting for transfers between devices, body(): lax.ppermute(rims, 'ctx', [(i, (i + 1) % ranks) for i in range(ranks)])  1.11 us
  transfers between devices with their start and end apart: 5, of which 4 were waited for; matrix products, arithmetic and copies ran while one was open for 0% of the time, Pallas kernels for 36%

profile of v9, /device:TPU:0, one launch (start us, length us, event | category | flops | bytes accessed | tf_op | source)
XLA Modules:
  0.0 23.8 jit_solution(8298550682037798104)
XLA Ops:
  0.0 0.0 copy-start
  0.0 0.0 copy-start.1
  0.0 1.0 %rim.1 = (bf16[8,1024]{1,0:T(8,128)(2,1)S(1)}, f32[16,64]{1,0:T(8,128)S(1)}, f32[16,64]{1,0:T(8,128)S(1)}, f32[1,1024]{1,0:T(1,128)S(1)}) custom-call(bf16[512,1024]{1,0:T(8,128)(2,1)} %q_ref.5, bf16[512,1024]{1,0:T(8,128)(2,1)} %k_ref.5, bf16[512,1024]{1,0:T(8,128)(2,1)} %v_ref.5, f32[16,64]{1,0:T(8,128)} %refs_0_.1, f32[16,64]{1,0:T(8,128)} %refs_1_.1, ...), custom_call_target="tpu_custom_call" | custom-call | tf_op jit(solution)/shard_map/rim/pallas_call | solution.py:313
  1.0 3.0 %collective-permute-start = (bf16[8,1024]{1,0:T(8,128)(2,1)S(1)}, bf16[8,1024]{1,0:T(8,128)(2,1)S(1)}, u32[]{:S(2)}, u32[]{:S(2)}) collective-permute-start(bf16[8,1024]{1,0:T(8,128)(2,1)S(1)} %get-tuple-element.25), channel_id=1, source_target_pairs={{0,4},{4,8},{8,12},{12,16},{16,20},{20,24},{24,28},{28,0},{1,5},{5... | collective-permute-start | bytes 49160 | tf_op jit(solution)/shard_map/ppermute | solution.py:322
  4.0 1.2 %tables.1 = (bf16[512,2048]{1,0:T(8,128)(2,1)S(1)}, bf16[1024,256]{1,0:T(8,128)(2,1)S(1)}, f32[2,1024]{1,0:T(2,128)S(1)}, f32[1,1024]{1,0:T(1,128)S(1)}, f32[16,...) custom-call(f32[16,64]{1,0:T(8,128)S(1)} %get-tuple-element.26.res_ref, ...), custom_call_target="tpu_custom_call" | custom-call | flops 10000000 | bytes 5242880 | tf_op jit(solution)/shard_map/tables/pallas_call | solution.py:328
  5.2 0.0 copy-done
  5.2 0.0 copy-done.1
  5.2 0.0 copy-done.2
  5.2 0.0 copy-done.3
  5.2 2.4 %state.1 = (f32[512,1024]{1,0:T(8,128)S(1)}, f32[16,1024]{1,0:T(8,128)S(1)}, f32[3,16,1024]{2,1,0:T(8,128)S(1)}) custom-call(bf16[512,1024]{1,0:T(8,128)(2,1)S(1)} %copy-done.1, bf16[512,1024]{1,0:T(8,128)(2,1)S(1)} %copy-done.2, f32[3,3,1024]{2,1,0:T(4,128)S(1)} %copy-done.3, bf16[1024,256]{1,0:T(8,128)(2,1)S(1)} %get-tuple-element.33.tail_ref, ...), custom_call_target="tpu_custom_call" | custom-call | flops 10000000 | bytes 5242880 | tf_op jit(solution)/shard_map/state/pallas_call | solution.py:349
  7.7 1.1 %collective-permute-done.halo_ref = bf16[8,1024]{1,0:T(8,128)(2,1)S(1)} collective-permute-done((bf16[8,1024]{1,0:T(8,128)(2,1)S(1)}, bf16[8,1024]{1,0:T(8,128)(2,1)S(1)}, u32[]{:S(2)}, u32[]{:S(2)}) %collective-permute-start) | collective-permute-done | bytes 16416 | tf_op jit(solution)/shard_map/ppermute | solution.py:322
  8.8 0.1 seam.1
  8.9 0.5 %collective-permute-start.1 = (f32[16,1024]{1,0:T(8,128)S(1)}, f32[16,1024]{1,0:T(8,128)S(1)}, u32[]{:S(2)}, u32[]{:S(2)}) collective-permute-start(f32[16,1024]{1,0:T(8,128)S(1)} %get-tuple-element.37.refs_0_), channel_id=1, source_target_pairs={{0,4},{4,0},{8,12},{12,8},{16,20},{20,16},{24,28},{28,24},{1,5},{5... | collective-permute-start | bytes 196616 | tf_op jit(solution)/shard_map/ppermute | solution.py:386
  9.4 1.6 %collective-permute-start.2 = (f32[16,1024]{1,0:T(8,128)S(1)}, f32[16,1024]{1,0:T(8,128)S(1)}, u32[]{:S(2)}, u32[]{:S(2)}) collective-permute-start(f32[16,1024]{1,0:T(8,128)S(1)} %get-tuple-element.37.refs_0_), channel_id=1, source_target_pairs={{0,8},{4,12},{8,0},{12,4},{16,24},{20,28},{24,16},{28,20},{1,9},{5... | collective-permute-start | bytes 196616 | tf_op jit(solution)/shard_map/ppermute | solution.py:386
  11.0 1.5 %collective-permute-start.3 = (f32[16,1024]{1,0:T(8,128)S(1)}, f32[16,1024]{1,0:T(8,128)S(1)}, u32[]{:S(2)}, u32[]{:S(2)}) collective-permute-start(f32[16,1024]{1,0:T(8,128)S(1)} %get-tuple-element.37.refs_0_), channel_id=1, source_target_pairs={{0,12},{4,8},{8,4},{12,0},{16,28},{20,24},{24,20},{28,16},{1,13},{... | collective-permute-start | bytes 196616 | tf_op jit(solution)/shard_map/ppermute | solution.py:386
  12.4 0.8 %collective-permute-done.1.refs_1_ = f32[16,1024]{1,0:T(8,128)S(1)} collective-permute-done((f32[16,1024]{1,0:T(8,128)S(1)}, f32[16,1024]{1,0:T(8,128)S(1)}, u32[]{:S(2)}, u32[]{:S(2)}) %collective-permute-start.1) | collective-permute-done | bytes 65568 | tf_op jit(solution)/shard_map/ppermute | solution.py:386
  13.2 0.7 %collective-permute-done.2.refs_2_ = f32[16,1024]{1,0:T(8,128)S(1)} collective-permute-done((f32[16,1024]{1,0:T(8,128)S(1)}, f32[16,1024]{1,0:T(8,128)S(1)}, u32[]{:S(2)}, u32[]{:S(2)}) %collective-permute-start.2) | collective-permute-done | bytes 65568 | tf_op jit(solution)/shard_map/ppermute | solution.py:386
  13.9 2.3 %collective-permute-done.3.refs_3_ = f32[16,1024]{1,0:T(8,128)S(1)} collective-permute-done((f32[16,1024]{1,0:T(8,128)S(1)}, f32[16,1024]{1,0:T(8,128)S(1)}, u32[]{:S(2)}, u32[]{:S(2)}) %collective-permute-start.3) | collective-permute-done | bytes 65568 | tf_op jit(solution)/shard_map/ppermute | solution.py:386
  16.2 1.2 %collective-permute-start.4 = (f32[16,1024]{1,0:T(8,128)S(1)}, f32[16,1024]{1,0:T(8,128)S(1)}, u32[]{:S(2)}, u32[]{:S(2)}) collective-permute-start(f32[16,1024]{1,0:T(8,128)S(1)} %get-tuple-element.39), channel_id=1, source_target_pairs={{0,16},{4,20},{8,24},{12,28},{16,0},{20,4},{24,8},{28,12},{1,17},{... | collective-permute-start | bytes 196616 | tf_op jit(solution)/shard_map/ppermute | solution.py:386
  17.4 0.6 %query.1.query_ref.refs_0_ = f32[512,1024]{1,0:T(8,128)S(1)} custom-call(bf16[8,1024]{1,0:T(8,128)(2,1)S(1)} %collective-permute-done.halo_ref, bf16[512,1024]{1,0:T(8,128)(2,1)S(1)} %copy-done, f32[3,3,1024]{2,1,0:T(4,128)S(1)} %copy-done.3), custom_call_target="tpu_custom_call" | custom-call | flops 10000000 | bytes 4194304 | tf_op jit(solution)/shard_map/query/pallas_call | solution.py:370
  18.0 2.1 %near.3.refs_5_ = f32[512,512]{1,0:T(8,128)S(1)} custom-call(f32[512,1024]{1,0:T(8,128)S(1)} %get-tuple-element.40.gated_ref, f32[512,1024]{1,0:T(8,128)S(1)} %query.1.query_ref.refs_0_, f32[3,16,1024]{2,1,0:T(8,128)S(1)} %get-tuple-element.41.into_ref, f32[2,1024]{1,0:T(2,128)S(1)} %get-tuple-element.42.row_ref, f32[1,1024]{1,0:T(1,128)S(1)} %get-tuple-element.43.plain_ref, ...), custom_call_target="tpu_custom_call" | custom-call | flops 10000000 | bytes 4194304 | tf_op jit(solution)/shard_map/near/pallas_call | solution.py:390
  20.1 2.2 %near.2.refs_4_ = f32[512,512]{1,0:T(8,128)S(1)} custom-call(f32[512,1024]{1,0:T(8,128)S(1)} %get-tuple-element.40.gated_ref, f32[512,1024]{1,0:T(8,128)S(1)} %query.1.query_ref.refs_0_, f32[3,16,1024]{2,1,0:T(8,128)S(1)} %get-tuple-element.41.into_ref, f32[2,1024]{1,0:T(2,128)S(1)} %get-tuple-element.42.row_ref, f32[1,1024]{1,0:T(1,128)S(1)} %get-tuple-element.43.plain_ref, ...), custom_call_target="tpu_custom_call" | custom-call | flops 10000000 | bytes 4194304 | tf_op jit(solution)/shard_map/near/pallas_call | solution.py:390
  22.3 0.0 collective-permute-done.4.refs_3_
  22.3 1.5 %mix.1 = bf16[512,1024]{1,0:T(8,128)(2,1)} custom-call(f32[512,1024]{1,0:T(8,128)S(1)} %query.1.query_ref.refs_0_, f32[4,16,1024]{2,1,0:T(8,128)S(1)} %get-tuple-element.29.refs_5_.refs_1_, bf16[512,2048]{1,0:T(8,128)(2,1)S(1)} %get-tuple-element.30.lead_ref.refs_2_, f32[16,1024]{1,0:T(8,128)S(1)} %collective-permute-done.4.refs_3_, ...), custom_call_target="tpu_custom_call" | custom-call | tf_op jit(solution)/shard_map/mix/pallas_call | solution.py:413
  (3 shorter events, 0.0 us)
Async XLA Ops:
  0.0 5.2 %copy-start = (bf16[512,1024]{1,0:T(8,128)(2,1)S(1)}, bf16[512,1024]{1,0:T(8,128)(2,1)}, u32[]{:S(2)}) copy-start(bf16[512,1024]{1,0:T(8,128)(2,1)} %q_ref.5) | copy-start | bytes 3145732
  0.0 5.2 %copy-start.1 = (bf16[512,1024]{1,0:T(8,128)(2,1)S(1)}, bf16[512,1024]{1,0:T(8,128)(2,1)}, u32[]{:S(2)}) copy-start(bf16[512,1024]{1,0:T(8,128)(2,1)} %k_ref.5) | copy-start | bytes 3145732
  0.0 5.2 %copy-start.2 = (bf16[512,1024]{1,0:T(8,128)(2,1)S(1)}, bf16[512,1024]{1,0:T(8,128)(2,1)}, u32[]{:S(2)}) copy-start(bf16[512,1024]{1,0:T(8,128)(2,1)} %v_ref.5) | copy-start | bytes 3145732
  0.0 5.2 %copy-start.3 = (f32[3,3,1024]{2,1,0:T(4,128)S(1)}, f32[3,3,1024]{2,1,0:T(4,128)}, u32[]{:S(2)}) copy-start(f32[3,3,1024]{2,1,0:T(4,128)} %sf_ref.5) | copy-start | bytes 110596
  1.0 7.8 %collective-permute-start = (bf16[8,1024]{1,0:T(8,128)(2,1)S(1)}, bf16[8,1024]{1,0:T(8,128)(2,1)S(1)}, u32[]{:S(2)}, u32[]{:S(2)}) collective-permute-start(bf16[8,1024]{1,0:T(8,128)(2,1)S(1)} %get-tuple-element.25), channel_id=1, source_target_pairs={{0,4},{4,8},{8,12},{12,16},{16,20},{20,24},{24,28},{28,0},{1,5},{5... | collective-permute-start | bytes 49160 | tf_op jit(solution)/shard_map/ppermute | solution.py:322
  8.9 4.3 %collective-permute-start.1 = (f32[16,1024]{1,0:T(8,128)S(1)}, f32[16,1024]{1,0:T(8,128)S(1)}, u32[]{:S(2)}, u32[]{:S(2)}) collective-permute-start(f32[16,1024]{1,0:T(8,128)S(1)} %get-tuple-element.37.refs_0_), channel_id=1, source_target_pairs={{0,4},{4,0},{8,12},{12,8},{16,20},{20,16},{24,28},{28,24},{1,5},{5... | collective-permute-start | bytes 196616 | tf_op jit(solution)/shard_map/ppermute | solution.py:386
  9.4 4.5 %collective-permute-start.2 = (f32[16,1024]{1,0:T(8,128)S(1)}, f32[16,1024]{1,0:T(8,128)S(1)}, u32[]{:S(2)}, u32[]{:S(2)}) collective-permute-start(f32[16,1024]{1,0:T(8,128)S(1)} %get-tuple-element.37.refs_0_), channel_id=1, source_target_pairs={{0,8},{4,12},{8,0},{12,4},{16,24},{20,28},{24,16},{28,20},{1,9},{5... | collective-permute-start | bytes 196616 | tf_op jit(solution)/shard_map/ppermute | solution.py:386
  11.0 5.2 %collective-permute-start.3 = (f32[16,1024]{1,0:T(8,128)S(1)}, f32[16,1024]{1,0:T(8,128)S(1)}, u32[]{:S(2)}, u32[]{:S(2)}) collective-permute-start(f32[16,1024]{1,0:T(8,128)S(1)} %get-tuple-element.37.refs_0_), channel_id=1, source_target_pairs={{0,12},{4,8},{8,4},{12,0},{16,28},{20,24},{24,20},{28,16},{1,13},{... | collective-permute-start | bytes 196616 | tf_op jit(solution)/shard_map/ppermute | solution.py:386
  16.2 6.1 %collective-permute-start.4 = (f32[16,1024]{1,0:T(8,128)S(1)}, f32[16,1024]{1,0:T(8,128)S(1)}, u32[]{:S(2)}, u32[]{:S(2)}) collective-permute-start(f32[16,1024]{1,0:T(8,128)S(1)} %get-tuple-element.39), channel_id=1, source_target_pairs={{0,16},{4,20},{8,24},{12,28},{16,0},{20,4},{24,8},{28,12},{1,17},{... | collective-permute-start | bytes 196616 | tf_op jit(solution)/shard_map/ppermute | solution.py:386
